TPU v7x, 512 devices: a whole 4x4x16 slice. The times are simulated.
512 devices in a mesh: fsdp: 16 (over z_hi, x, core), seq: 32 (over z_lo, y).
Axes of the slice: x: 4, y: 4, z: 16 (z_hi: 2, z_lo: 8; z = z_hi * 8 + z_lo), core: 2. Of those that a mesh axis runs over, the one named last changes fastest.
Arguments:
- qkv: bfloat16 [16, 4096, 6144], P('fsdp', 'seq'), may hold values from -128 to 128
- resid: bfloat16 [16, 4096, 2048], P('fsdp', 'seq'), may hold values from -0.625 to 0.625
- earlier: float32 [16, 4096, 2048], P('fsdp', 'seq'), may hold values from -12 to 12
- lengths: int32 [16, 12], P('fsdp'), may hold values from 1 to 512, 4096 in all within a row
- teacher_out: bfloat16 [2048, 2048], P('seq', 'fsdp'), may hold values from -6 to 6
- student_out: bfloat16 [2048, 2048], P('seq', 'fsdp'), may hold values from -6 to 6
Outputs:
- targets: float32 [16, 4096, 2048], P('fsdp', 'seq')
- teacher_new: bfloat16 [2048, 2048], P('seq', 'fsdp')
Inputs may be any that keep to these rules, and one draw needn't show every extreme that they name: Each pack's 12 utterance lengths add up to its 4096 frames, and one of them is exactly 512.
All inputs are finite; a program needn't handle non-finite values.
Results may differ from a plain program's by a relative error of at most 0.0019.
Values may be sent and summed in bfloat16 or wider, within the bound.
No kernel may reach another device: no remote copies, remote signals or barrier semaphores. Data moves between devices by JAX's collectives and lax.ppermute only.
A program may use at most 64 MiB of HBM per device.

v0:
```python
import functools
import math

import jax
import jax.numpy as jnp
from jax import lax
from jax.experimental import pallas as pl
from jax.experimental.pallas import tpu as pltpu
from jax.sharding import Mesh, PartitionSpec as P

D = 2048
HEAD_DIM = 64
TOP_K = 8
UTTS = 12
LANES = 128
TOKENS = 128
ROW = 512
WIDTH = 512
CHUNK = 256
PAIRS = WIDTH // LANES
PACKED = 32

ema_decay = 0.9
norm_epsilon = 1e-05
masked_score = -1e30


def pack_kernel(place_ref, qkv_ref, *outs):
    y = place_ref[1]
    low = lax.broadcasted_iota(jnp.int32, (PACKED, LANES), 1) < HEAD_DIM
    for turn in range(4):
        target = lax.rem(y + 4 - turn, 4)
        odd = lax.rem(target, 2) == 1
        half = lax.div(target, 2) * LANES
        for part in range(3):
            for pair in range(PAIRS):
                base = part * D + pair * 512
                first = qkv_ref[:, pl.ds(pl.multiple_of(base + half, LANES), LANES)].astype(jnp.float32)
                second = qkv_ref[:, pl.ds(pl.multiple_of(base + 256 + half, LANES), LANES)].astype(jnp.float32)
                left = jnp.where(odd, pltpu.roll(first, HEAD_DIM, 1), first)
                right = jnp.where(odd, second, pltpu.roll(second, HEAD_DIM, 1))
                both = jnp.where(low, left, right)
                if part == 0:
                    both = both * (1.0 / math.sqrt(HEAD_DIM))
                    outs[4 + turn][:, pair * LANES : (pair + 1) * LANES] = both.astype(jnp.bfloat16)
                else:
                    start = (part - 1) * WIDTH + pair * LANES
                    outs[turn][:, start : start + LANES] = both.astype(jnp.bfloat16)


class Attention:
    def __init__(self, lengths_ref, place_ref, sources, kv, scores, tops, totals, sums, sems):
        self.kv, self.scores, self.tops, self.totals, self.sums = kv, scores, tops, totals, sums
        self.row_start = place_ref[0] * ROW
        self.y = place_ref[1]
        self.base = self.row_start - ROW
        self.ends = []
        total = jnp.int32(0)
        for j in range(UTTS):
            total = total + lengths_ref[0, j]
            self.ends.append(total)
        self.low = lax.broadcasted_iota(jnp.int32, (TOKENS, LANES), 1) < HEAD_DIM
        self.copies = []
        for turn in range(4):
            slot = lax.rem(self.y + turn, 4)
            views = [sources[turn]]
            for side in range(2):
                own, rest = sources[4 + 2 * side], sources[5 + 2 * side]
                views.append(own if turn == 0 else rest.at[pl.ds((turn - 1) * TOKENS, TOKENS)])
            for view, row in zip(views, (1, 0, 2)):
                where = slot + 4 * row
                target = kv.at[pl.ds(pl.multiple_of(where * TOKENS, TOKENS), TOKENS)]
                self.copies.append(
                    (where, pltpu.make_async_copy(view, target, sems.at[len(self.copies)]))
                )

    def keys_of(self, which):
        first = self.row_start + which * TOKENS
        last = first + TOKENS - 1
        begin = jnp.int32(0)
        finish = jnp.int32(0)
        for end in reversed(self.ends):
            finish = jnp.where(end > last, end, finish)
        for end in self.ends:
            begin = jnp.where(end <= first, end, begin)
        start = lax.div(begin - self.base, TOKENS)
        stop = lax.div(finish - self.base + TOKENS - 1, TOKENS)
        return start, stop

    def load(self, blocks):
        ranges = [self.keys_of(which) for which in blocks]
        start = functools.reduce(jnp.minimum, [r[0] for r in ranges])
        stop = functools.reduce(jnp.maximum, [r[1] for r in ranges])
        for where, copy in self.copies:
            @pl.when((where >= start) & (where < stop))
            def _():
                copy.start()
        self.kv[pl.ds(pl.multiple_of(stop * TOKENS, TOKENS), TOKENS), :] = jnp.zeros(
            (TOKENS, 2 * WIDTH), jnp.bfloat16
        )
        for where, copy in self.copies:
            @pl.when((where >= start) & (where < stop))
            def _():
                copy.wait()

    def segments(self, frames):
        found = jnp.zeros(frames.shape, jnp.int32)
        for end in self.ends:
            found = found + (frames >= end).astype(jnp.int32)
        return jnp.where(frames < 0, -1, found)

    def attend(self, which, q_ref, store):
        kv, scores, tops, totals, sums, low = (
            self.kv, self.scores, self.tops, self.totals, self.sums, self.low,
        )
        key_block, stop = self.keys_of(which)
        steps = lax.div(stop - key_block + 1, CHUNK // TOKENS)
        row_segment = self.segments(
            self.row_start + which * TOKENS + lax.broadcasted_iota(jnp.int32, (TOKENS, LANES), 0)
        )
        row_segment = jnp.concatenate([row_segment, row_segment], axis=1)
        queries = []
        for pair in range(PAIRS):
            one = q_ref[:, pair * LANES : (pair + 1) * LANES]
            zero = jnp.zeros_like(one)
            queries.append(
                jnp.concatenate([jnp.where(low, one, zero), jnp.where(low, zero, one)], axis=0)
            )
        tops[...] = jnp.full(tops.shape, masked_score, jnp.float32)
        totals[...] = jnp.zeros(totals.shape, jnp.float32)
        sums[...] = jnp.zeros(sums.shape, jnp.float32)

        def score(step, carry):
            start = pl.multiple_of(key_block * TOKENS + step * CHUNK, TOKENS)
            key_segment = self.segments(
                self.base + start + lax.broadcasted_iota(jnp.int32, (8, CHUNK), 1)
            )[:1]
            allowed = row_segment == key_segment
            allowed = jnp.concatenate([allowed, allowed], axis=0)
            for pair in range(PAIRS):
                keys = kv[pl.ds(start, CHUNK), pair * LANES : (pair + 1) * LANES]
                found = lax.dot_general(
                    queries[pair], keys, (((1,), (1,)), ((), ())),
                    preferred_element_type=jnp.float32,
                )
                found = jnp.where(allowed, found, masked_score)
                scores[step, pair] = found
                tops[pair] = jnp.maximum(
                    tops[pair], jnp.maximum(found[:, :LANES], found[:, LANES:])
                )
            return carry

        lax.fori_loop(0, steps, score, 0)
        for pair in range(PAIRS):
            top = jnp.max(tops[pair], axis=1, keepdims=True)
            tops[pair] = jnp.broadcast_to(top, (2 * TOKENS, LANES))

        def mix(step, carry):
            start = pl.multiple_of(key_block * TOKENS + step * CHUNK, TOKENS)
            for pair in range(PAIRS):
                found = scores[step, pair]
                left = jnp.exp(found[:, :LANES] - tops[pair])
                right = jnp.exp(found[:, LANES:] - tops[pair])
                totals[pair] = totals[pair] + (left + right)
                weights = jnp.concatenate([left, right], axis=1).astype(jnp.bfloat16)
                values = kv[
                    pl.ds(start, CHUNK), WIDTH + pair * LANES : WIDTH + (pair + 1) * LANES
                ]
                sums[pair] = sums[pair] + jnp.dot(
                    weights, values, preferred_element_type=jnp.float32
                )
            return carry

        lax.fori_loop(0, steps, mix, 0)
        for pair in range(PAIRS):
            row_total = jnp.sum(totals[pair], axis=1, keepdims=True)
            mixed = sums[pair] / row_total
            store(
                pair * LANES,
                jnp.where(low, mixed[:TOKENS], mixed[TOKENS:]).astype(jnp.bfloat16),
            )


def project(mixed, weights_ref, store):
    for tile in range(0, 16, 2):
        high, place = divmod(tile, 8)
        both = jnp.concatenate(
            [weights_ref[2 * place + high], weights_ref[2 * (place + 1) + high]], axis=1
        )
        store(tile * LANES, jnp.dot(mixed, both, preferred_element_type=jnp.float32))


HALF = D // 2
PAIR = 2 * LANES


def far_kernel(lengths_ref, place_ref, weights_hbm, q_ref, *rest):
    sources, (one_ref, two_ref), scratch = rest[:8], rest[8:10], rest[10:]
    weights, mixed, weight_sem = scratch[6:]
    fetch = pltpu.make_async_copy(weights_hbm, weights, weight_sem)
    fetch.start()
    attention = Attention(lengths_ref, place_ref, sources, *scratch[:6])
    which = lax.rem(attention.y + 2, 4)
    attention.load([which])

    def keep(start, value):
        mixed[:, start : start + LANES] = value

    attention.attend(which, q_ref, keep)
    fetch.wait()

    def store(start, value):
        out_ref = one_ref if start < HALF else two_ref
        start = start % HALF
        out_ref[:, start : start + PAIR] = value.astype(jnp.bfloat16)

    project(mixed[...], weights, store)


def near_kernel(lengths_ref, place_ref, q_ref, q3_ref, *rest):
    sources, out_ref, scratch = rest[:8], rest[8], rest[9:]
    attention = Attention(lengths_ref, place_ref, sources, *scratch)
    blocks = [lax.rem(attention.y + 1, 4), lax.rem(attention.y + 3, 4)]
    attention.load(blocks)
    for i, ref in enumerate((q_ref, q3_ref)):
        def keep(start, value):
            out_ref[i * TOKENS : (i + 1) * TOKENS, start : start + LANES] = value

        attention.attend(blocks[i], ref, keep)


def pass_kernel(mixed_ref, weights_ref, one_ref, two_ref, up_ref, down_ref):
    def store(start, value):
        up, down = value[:TOKENS], value[TOKENS:]
        span = slice(start, start + PAIR)
        if start < HALF:
            up = up + one_ref[:, span].astype(jnp.float32)
        else:
            down = down + two_ref[:, start - HALF : start - HALF + PAIR].astype(jnp.float32)
        up_ref[:, span] = up.astype(jnp.bfloat16)
        down_ref[:, span] = down.astype(jnp.bfloat16)

    project(mixed_ref[...], weights_ref, store)


def own_kernel(lengths_ref, place_ref, weights_hbm, q_ref, *rest):
    sources, out_ref, scratch = rest[:8], rest[8], rest[9:]
    weights, mixed, weight_sem = scratch[6:]
    fetch = pltpu.make_async_copy(weights_hbm, weights, weight_sem)
    fetch.start()
    attention = Attention(lengths_ref, place_ref, sources, *scratch[:6])
    attention.load([attention.y])

    def keep(start, value):
        mixed[:, start : start + LANES] = value

    attention.attend(attention.y, q_ref, keep)
    fetch.wait()

    def store(start, value):
        out_ref[:, start : start + PAIR] = value

    project(mixed[...], weights, store)


def finish_kernel(own_ref, up_ref, down_ref, resid_ref, earlier_ref, out_ref):
    branch = own_ref[...] + up_ref[...].astype(jnp.float32)
    branch = branch + down_ref[...].astype(jnp.float32)
    summed = resid_ref[...].astype(jnp.float32) + branch * (1.0 / math.sqrt(D))
    centered = summed - jnp.mean(summed, axis=1, keepdims=True)
    spread = jnp.mean(centered * centered, axis=1, keepdims=True)
    normed = centered * lax.rsqrt(spread + norm_epsilon)
    out_ref[...] = (earlier_ref[...] + normed) * (1.0 / TOP_K)


vmem = pl.BlockSpec(memory_space=pltpu.VMEM)
smem = pl.BlockSpec(memory_space=pltpu.SMEM)
anywhere = pl.BlockSpec(memory_space=pl.ANY)
attend_scratch = [
    pltpu.VMEM((13 * TOKENS, 2 * WIDTH), jnp.bfloat16),
    pltpu.VMEM((6, PAIRS, 2 * TOKENS, CHUNK), jnp.float32),
    pltpu.VMEM((PAIRS, 2 * TOKENS, LANES), jnp.float32),
    pltpu.VMEM((PAIRS, 2 * TOKENS, LANES), jnp.float32),
    pltpu.VMEM((PAIRS, 2 * TOKENS, LANES), jnp.float32),
    pltpu.SemaphoreType.DMA((12,)),
]
project_scratch = [
    pltpu.VMEM((16, ROW, LANES), jnp.bfloat16),
    pltpu.VMEM((TOKENS, WIDTH), jnp.bfloat16),
    pltpu.SemaphoreType.DMA,
]


def cost(flops, moved, exps=0):
    return pl.CostEstimate(flops=flops, bytes_accessed=moved, transcendentals=exps)


def array(*shape, dtype=jnp.bfloat16):
    return jax.ShapeDtypeStruct(shape, dtype)


def shift(value, amount, axis="y", size=4):
    return lax.ppermute(value, axis, [(i, (i + amount) % size) for i in range(size)])


def block(qkv, resid, earlier, lengths, teacher_out, student_out):
    teacher_new = (
        ema_decay * teacher_out.astype(jnp.float32)
        + (1.0 - ema_decay) * student_out.astype(jnp.float32)
    ).astype(jnp.bfloat16)
    place = jnp.stack([lax.axis_index("z"), lax.axis_index("y")]).astype(jnp.int32)

    packed = pl.pallas_call(
        pack_kernel,
        grid=(TOKENS // PACKED,),
        out_shape=(array(TOKENS, 2 * WIDTH),) * 4 + (array(TOKENS, WIDTH),) * 4,
        in_specs=[smem, pl.BlockSpec((PACKED, 3 * D), lambda i: (i, 0))],
        out_specs=(pl.BlockSpec((PACKED, 2 * WIDTH), lambda i: (i, 0)),) * 4
        + (pl.BlockSpec((PACKED, WIDTH), lambda i: (i, 0)),) * 4,
        cost_estimate=cost(0, 3 << 20),
        name="pack",
    )(place, qkv[0])
    kv, q = packed[:4], packed[4:]

    ring = 2 * lax.axis_size("z")
    kv_far = shift(kv[2], -2)
    kv_next = shift(kv[1], -1)
    kv_last = shift(kv[3], -3)
    own_after = shift(kv[0], -1, ("h", "z"), ring)
    own_before = shift(kv[0], 1, ("h", "z"), ring)
    others = jnp.concatenate([kv_next, kv_far, kv_last], axis=0)
    after = shift(others, -1, ("h", "z"), ring)
    before = shift(others, 1, ("h", "z"), ring)
    q_far = shift(q[2], -2)
    q_next = shift(q[1], -1)
    q_last = shift(q[3], -3)

    ring_weights = lax.all_to_all(
        jnp.broadcast_to(teacher_new[None], (16,) + teacher_new.shape), ("h", "z"), 0, 0, tiled=True
    )
    weights = lax.all_to_all(
        jnp.broadcast_to(ring_weights[None], (8,) + ring_weights.shape), ("x", "c"), 0, 0, tiled=True
    )
    weights = weights.reshape(16, ROW, LANES)

    sources = (kv[0], kv_next, kv_far, kv_last, own_before, before, own_after, after)
    places = [anywhere] * 8
    one, two = pl.pallas_call(
        far_kernel,
        out_shape=(array(TOKENS, HALF),) * 2,
        in_specs=[smem, smem, anywhere, vmem] + places,
        out_specs=(vmem,) * 2,
        scratch_shapes=attend_scratch + project_scratch,
        cost_estimate=cost(1 << 29, 4 << 20, 1 << 20),
        name="far",
    )(lengths, place, weights, q_far, *sources)
    one = shift(one, 1)
    two = shift(two, -1)
    mixed = pl.pallas_call(
        near_kernel,
        out_shape=array(2 * TOKENS, WIDTH),
        in_specs=[smem, smem, vmem, vmem] + places,
        out_specs=vmem,
        scratch_shapes=attend_scratch,
        cost_estimate=cost(1 << 30, 4 << 20, 2 << 20),
        name="near",
    )(lengths, place, q_next, q_last, *sources)
    up, down = pl.pallas_call(
        pass_kernel,
        out_shape=(array(TOKENS, D),) * 2,
        in_specs=[vmem] * 4,
        out_specs=(vmem,) * 2,
        cost_estimate=cost(4 * TOKENS * WIDTH * D, 4 << 20),
        name="pass",
    )(mixed, weights, one, two)
    up = shift(up, 1)
    down = shift(down, -1)
    own = pl.pallas_call(
        own_kernel,
        out_shape=array(TOKENS, D, dtype=jnp.float32),
        in_specs=[smem, smem, anywhere, vmem] + places,
        out_specs=vmem,
        scratch_shapes=attend_scratch + project_scratch,
        cost_estimate=cost(1 << 29, 4 << 20, 1 << 20),
        name="own",
    )(lengths, place, weights, q[0], *sources)
    rows = pl.BlockSpec((32, D), lambda i: (i, 0))
    targets = pl.pallas_call(
        finish_kernel,
        grid=(4,),
        out_shape=array(TOKENS, D, dtype=jnp.float32),
        in_specs=[rows] * 5,
        out_specs=rows,
        cost_estimate=cost(1 << 22, 5 << 20),
        name="finish",
    )(own, up, down, resid[0], earlier[0])
    return (targets[None], teacher_new)


def solution(mesh):
    fine = Mesh(
        mesh.devices.reshape(2, 4, 2, 8, 4), ("h", "x", "c", "z", "y")
    )
    packs, frames = ("h", "x", "c"), ("z", "y")
    placed = (
        P(packs, frames, None),
        P(packs, frames, None),
        P(packs, frames, None),
        P(packs, None),
        P(frames, packs),
        P(frames, packs),
    )
    return jax.shard_map(
        block,
        mesh=fine,
        in_specs=placed,
        out_specs=(P(packs, frames, None), P(frames, packs)),
        check_vma=False,
    )
```

profile of v0, /device:TPU:56, one launch (start us, length us, event | category | flops | bytes accessed | tf_op | source)
XLA Modules:
  0.0 160.9 jit_solution(6685786298524627920)
XLA Ops:
  1.4 32.9 %all_to_all.10 = bf16[16,64,128]{2,1,0:T(8,128)(2,1)S(1)} all-to-all(bf16[16,64,128]{2,1,0:T(8,128)(2,1)S(1)} %broadcast_in_dim.6), channel_id=1, replica_groups=mesh['h'=2,'x'=4,'c'=2,'z'=8,'y'=4] {'h','z'}, dimensions={0} | all-to-all | bytes 524288 | tf_op jit(solution)/shard_map/all_to_all | solution.py:338
  34.4 1.9 %broadcast_in_dim.7 = bf16[8,16,64,128]{3,2,1,0:T(8,128)(2,1)} broadcast(bf16[16,64,128]{2,1,0:T(8,128)(2,1)S(1)} %all_to_all.10), dimensions={1,2,3} | broadcast | bytes 2359296 | tf_op jit(solution)/shard_map/broadcast_in_dim | solution.py:342
  36.3 4.3 %all-to-all-start.1 = ((bf16[8,16,64,128]{3,2,1,0:T(8,128)(2,1)}), bf16[8,16,64,128]{3,2,1,0:T(8,128)(2,1)S(1)}, u32[]{:S(2)}, u32[]{:S(2)}) async-start(bf16[8,16,64,128]{3,2,1,0:T(8,128)(2,1)} %broadcast_in_dim.7), calls=%async_computation.1 | async-start | bytes 4194304 | tf_op jit(solution)/shard_map/all_to_all | solution.py:341
  41.2 4.1 %pack.1 = (bf16[128,1024]{1,0:T(8,128)(2,1)}, bf16[128,1024]{1,0:T(8,128)(2,1)}, bf16[128,1024]{1,0:T(8,128)(2,1)}, bf16[128,1024]{1,0:T(8,128)(2,1)}, bf16[128,...) custom-call(s32[2]{0:T(128)} %pad_add_fusion.place_ref, ...), custom_call_target="tpu_custom_call" | custom-call | bytes 3145728 | tf_op jit(solution)/shard_map/pack/pallas_call | solution.py:313
  45.3 2.7 %collective-permute-start = (bf16[128,1024]{1,0:T(8,128)(2,1)}, bf16[128,1024]{1,0:T(8,128)(2,1)S(1)}, u32[]{:S(2)}, u32[]{:S(2)}) collective-permute-start(bf16[128,1024]{1,0:T(8,128)(2,1)} %get-tuple-element.16), channel_id=1, source_target_pairs={{0,3},{1,0},{2,1},{3,2},{4,7},{5,4},{6,5},{7,6},{8,11},{9,8},{10,9... | collective-permute-start | bytes 786440 | tf_op jit(solution)/shard_map/ppermute | solution.py:303
  48.0 2.8 %collective-permute-start.1 = (bf16[128,1024]{1,0:T(8,128)(2,1)}, bf16[128,1024]{1,0:T(8,128)(2,1)S(1)}, u32[]{:S(2)}, u32[]{:S(2)}) collective-permute-start(bf16[128,1024]{1,0:T(8,128)(2,1)} %get-tuple-element.17), channel_id=1, source_target_pairs={{0,2},{1,3},{2,0},{3,1},{4,6},{5,7},{6,4},{7,5},{8,10},{9,11},{10,... | collective-permute-start | bytes 786440 | tf_op jit(solution)/shard_map/ppermute | solution.py:303
  50.8 4.1 %collective-permute-start.2 = (bf16[128,1024]{1,0:T(8,128)(2,1)}, bf16[128,1024]{1,0:T(8,128)(2,1)S(1)}, u32[]{:S(2)}, u32[]{:S(2)}) collective-permute-start(bf16[128,1024]{1,0:T(8,128)(2,1)} %get-tuple-element.18), channel_id=1, source_target_pairs={{0,1},{1,2},{2,3},{3,0},{4,5},{5,6},{6,7},{7,4},{8,9},{9,10},{10,1... | collective-permute-start | bytes 786440 | tf_op jit(solution)/shard_map/ppermute | solution.py:303
  54.9 8.0 %collective-permute-done.rest_1_ = bf16[128,1024]{1,0:T(8,128)(2,1)S(1)} collective-permute-done((bf16[128,1024]{1,0:T(8,128)(2,1)}, bf16[128,1024]{1,0:T(8,128)(2,1)S(1)}, u32[]{:S(2)}, u32[]{:S(2)}) %collective-permute-start) | collective-permute-done | bytes 262176 | tf_op jit(solution)/shard_map/ppermute | solution.py:303
  63.0 2.5 %collective-permute-done.2.rest_3_ = bf16[128,1024]{1,0:T(8,128)(2,1)S(1)} collective-permute-done((bf16[128,1024]{1,0:T(8,128)(2,1)}, bf16[128,1024]{1,0:T(8,128)(2,1)S(1)}, u32[]{:S(2)}, u32[]{:S(2)}) %collective-permute-start.2) | collective-permute-done | bytes 262176 | tf_op jit(solution)/shard_map/ppermute | solution.py:303
  66.2 3.5 %collective-permute-start.4 = (bf16[384,1024]{1,0:T(8,128)(2,1)S(1)}, bf16[384,1024]{1,0:T(8,128)(2,1)S(1)}, u32[]{:S(2)}, u32[]{:S(2)}) collective-permute-start(bf16[384,1024]{1,0:T(8,128)(2,1)S(1)} %constant_dynamic-update-slice_fusion), channel_id=1, source_target_pairs={{0,4},{4,8},{8,12},{12,16},{16,20},{20,24},{24,28},{28,256},{256,2... | collective-permute-start | bytes 2359304 | tf_op jit(solution)/shard_map/ppermute | solution.py:303
  69.7 2.3 %collective-permute-start.6 = (bf16[384,1024]{1,0:T(8,128)(2,1)S(1)}, bf16[384,1024]{1,0:T(8,128)(2,1)}, u32[]{:S(2)}, u32[]{:S(2)}) collective-permute-start(bf16[384,1024]{1,0:T(8,128)(2,1)S(1)} %constant_dynamic-update-slice_fusion), channel_id=1, source_target_pairs={{0,284},{4,0},{8,4},{12,8},{16,12},{20,16},{24,20},{28,24},{256,28... | collective-permute-start | bytes 2359304 | tf_op jit(solution)/shard_map/ppermute | solution.py:303
  72.1 3.5 %collective-permute-start.3 = (bf16[128,1024]{1,0:T(8,128)(2,1)}, bf16[128,1024]{1,0:T(8,128)(2,1)S(1)}, u32[]{:S(2)}, u32[]{:S(2)}) collective-permute-start(bf16[128,1024]{1,0:T(8,128)(2,1)} %get-tuple-element.15.rest_0_), channel_id=1, source_target_pairs={{0,4},{4,8},{8,12},{12,16},{16,20},{20,24},{24,28},{28,256},{256,2... | collective-permute-start | bytes 786440 | tf_op jit(solution)/shard_map/ppermute | solution.py:303
  75.6 2.4 %collective-permute-start.5 = (bf16[128,1024]{1,0:T(8,128)(2,1)}, bf16[128,1024]{1,0:T(8,128)(2,1)S(1)}, u32[]{:S(2)}, u32[]{:S(2)}) collective-permute-start(bf16[128,1024]{1,0:T(8,128)(2,1)} %get-tuple-element.15.rest_0_), channel_id=1, source_target_pairs={{0,284},{4,0},{8,4},{12,8},{16,12},{20,16},{24,20},{28,24},{256,28... | collective-permute-start | bytes 786440 | tf_op jit(solution)/shard_map/ppermute | solution.py:303
  78.1 3.1 %collective-permute-start.9 = (bf16[128,512]{1,0:T(8,128)(2,1)}, bf16[128,512]{1,0:T(8,128)(2,1)S(1)}, u32[]{:S(2)}, u32[]{:S(2)}) collective-permute-start(bf16[128,512]{1,0:T(8,128)(2,1)} %get-tuple-element.21), channel_id=1, source_target_pairs={{0,2},{1,3},{2,0},{3,1},{4,6},{5,7},{6,4},{7,5},{8,10},{9,11},{10,... | collective-permute-start | bytes 393224 | tf_op jit(solution)/shard_map/ppermute | solution.py:303
  81.2 5.4 %collective-permute-done.9.q_ref = bf16[128,512]{1,0:T(8,128)(2,1)S(1)} collective-permute-done((bf16[128,512]{1,0:T(8,128)(2,1)}, bf16[128,512]{1,0:T(8,128)(2,1)S(1)}, u32[]{:S(2)}, u32[]{:S(2)}) %collective-permute-start.9) | collective-permute-done | bytes 131104 | tf_op jit(solution)/shard_map/ppermute | solution.py:303
  86.6 5.9 %collective-permute-done.3.rest_4_ = bf16[128,1024]{1,0:T(8,128)(2,1)S(1)} collective-permute-done((bf16[128,1024]{1,0:T(8,128)(2,1)}, bf16[128,1024]{1,0:T(8,128)(2,1)S(1)}, u32[]{:S(2)}, u32[]{:S(2)}) %collective-permute-start.3) | collective-permute-done | bytes 262176 | tf_op jit(solution)/shard_map/ppermute | solution.py:303
  92.6 3.2 %collective-permute-done.5.rest_6_ = bf16[128,1024]{1,0:T(8,128)(2,1)S(1)} collective-permute-done((bf16[128,1024]{1,0:T(8,128)(2,1)}, bf16[128,1024]{1,0:T(8,128)(2,1)S(1)}, u32[]{:S(2)}, u32[]{:S(2)}) %collective-permute-start.5) | collective-permute-done | bytes 262176 | tf_op jit(solution)/shard_map/ppermute | solution.py:303
  96.6 0.8 copy-done.1
  98.1 5.3 %far.1 = (bf16[128,1024]{1,0:T(8,128)(2,1)}, bf16[128,1024]{1,0:T(8,128)(2,1)}) custom-call(s32[1,12]{1,0:T(1,128)} %lengths_ref.5, s32[2]{0:T(128)} %pad_add_fusion.place_ref, bf16[16,512,128]{2,1,0:T(8,128)(2,1)} %bitcast.7, bf16[128,512]{1,0:T(8,128)(2,1)} %copy-done.11, bf16[128,1024]{1,0:T(8,128)(2,1)} %get-tuple-element.15.rest_0_, ...), custom_call_target="tpu_custom_call" | custom-call | flops 536870912 | bytes 4194304 | tf_op jit(solution)/shard_map/far/pallas_call | solution.py:348
  103.4 6.7 %collective-permute-start.10 = (bf16[128,1024]{1,0:T(8,128)(2,1)}, bf16[128,1024]{1,0:T(8,128)(2,1)S(1)}, u32[]{:S(2)}, u32[]{:S(2)}) collective-permute-start(bf16[128,1024]{1,0:T(8,128)(2,1)} %get-tuple-element.22), channel_id=1, source_target_pairs={{0,1},{1,2},{2,3},{3,0},{4,5},{5,6},{6,7},{7,4},{8,9},{9,10},{10,1... | collective-permute-start | bytes 786440 | tf_op jit(solution)/shard_map/ppermute | solution.py:303
  110.2 1.9 %collective-permute-start.11 = (bf16[128,1024]{1,0:T(8,128)(2,1)}, bf16[128,1024]{1,0:T(8,128)(2,1)S(1)}, u32[]{:S(2)}, u32[]{:S(2)}) collective-permute-start(bf16[128,1024]{1,0:T(8,128)(2,1)} %get-tuple-element.23), channel_id=1, source_target_pairs={{0,3},{1,0},{2,1},{3,2},{4,7},{5,4},{6,5},{7,6},{8,11},{9,8},{10,9... | collective-permute-start | bytes 786440 | tf_op jit(solution)/shard_map/ppermute | solution.py:303
  112.1 1.9 %collective-permute-start.7 = (bf16[128,512]{1,0:T(8,128)(2,1)}, bf16[128,512]{1,0:T(8,128)(2,1)S(1)}, u32[]{:S(2)}, u32[]{:S(2)}) collective-permute-start(bf16[128,512]{1,0:T(8,128)(2,1)} %get-tuple-element.19), channel_id=1, source_target_pairs={{0,3},{1,0},{2,1},{3,2},{4,7},{5,4},{6,5},{7,6},{8,11},{9,8},{10,9... | collective-permute-start | bytes 393224 | tf_op jit(solution)/shard_map/ppermute | solution.py:303
  114.1 5.1 %collective-permute-start.8 = (bf16[128,512]{1,0:T(8,128)(2,1)}, bf16[128,512]{1,0:T(8,128)(2,1)S(1)}, u32[]{:S(2)}, u32[]{:S(2)}) collective-permute-start(bf16[128,512]{1,0:T(8,128)(2,1)} %get-tuple-element.20), channel_id=1, source_target_pairs={{0,1},{1,2},{2,3},{3,0},{4,5},{5,6},{6,7},{7,4},{8,9},{9,10},{10,1... | collective-permute-start | bytes 393224 | tf_op jit(solution)/shard_map/ppermute | solution.py:303
  119.2 3.1 %collective-permute-done.7.q_ref = bf16[128,512]{1,0:T(8,128)(2,1)S(1)} collective-permute-done((bf16[128,512]{1,0:T(8,128)(2,1)}, bf16[128,512]{1,0:T(8,128)(2,1)S(1)}, u32[]{:S(2)}, u32[]{:S(2)}) %collective-permute-start.7) | collective-permute-done | bytes 131104 | tf_op jit(solution)/shard_map/ppermute | solution.py:303
  123.6 8.3 %near.1.mixed_ref = bf16[256,512]{1,0:T(8,128)(2,1)} custom-call(s32[1,12]{1,0:T(1,128)} %lengths_ref.5, s32[2]{0:T(128)} %pad_add_fusion.place_ref, bf16[128,512]{1,0:T(8,128)(2,1)} %copy-done.13, bf16[128,512]{1,0:T(8,128)(2,1)} %copy-done.14, bf16[128,1024]{1,0:T(8,128)(2,1)} %get-tuple-element.15.rest_0_, bf16[128,1024]{1,0:T(8,128)(2,1)} %copy-done.2, ...), custom_call_target="tpu_custom_call" | custom-call | flops 1073741824 | bytes 4194304 | tf_op jit(solution)/shard_map/near/pallas_call | solution.py:359
  133.3 3.4 %pass.1 = (bf16[128,2048]{1,0:T(8,128)(2,1)}, bf16[128,2048]{1,0:T(8,128)(2,1)}) custom-call(bf16[256,512]{1,0:T(8,128)(2,1)} %near.1.mixed_ref, bf16[16,512,128]{2,1,0:T(8,128)(2,1)} %bitcast.8, bf16[128,1024]{1,0:T(8,128)(2,1)} %copy-done.9, bf16[128,1024]{1,0:T(8,128)(2,1)} %copy-done.10), custom_call_target="tpu_custom_call" | custom-call | flops 536870912 | bytes 4194304 | tf_op jit(solution)/shard_map/pass/pallas_call | solution.py:368
  136.7 3.9 %collective-permute-start.12 = (bf16[128,2048]{1,0:T(8,128)(2,1)}, bf16[128,2048]{1,0:T(8,128)(2,1)S(1)}, u32[]{:S(2)}, u32[]{:S(2)}) collective-permute-start(bf16[128,2048]{1,0:T(8,128)(2,1)} %get-tuple-element.24), channel_id=1, source_target_pairs={{0,1},{1,2},{2,3},{3,0},{4,5},{5,6},{6,7},{7,4},{8,9},{9,10},{10,1... | collective-permute-start | bytes 1572872 | tf_op jit(solution)/shard_map/ppermute | solution.py:303
  140.6 2.0 %collective-permute-start.13 = (bf16[128,2048]{1,0:T(8,128)(2,1)}, bf16[128,2048]{1,0:T(8,128)(2,1)S(1)}, u32[]{:S(2)}, u32[]{:S(2)}) collective-permute-start(bf16[128,2048]{1,0:T(8,128)(2,1)} %get-tuple-element.25), channel_id=1, source_target_pairs={{0,3},{1,0},{2,1},{3,2},{4,7},{5,4},{6,5},{7,6},{8,11},{9,8},{10,9... | collective-permute-start | bytes 1572872 | tf_op jit(solution)/shard_map/ppermute | solution.py:303
  142.5 6.3 %own.1.own_ref = f32[128,2048]{1,0:T(8,128)} custom-call(s32[1,12]{1,0:T(1,128)} %lengths_ref.5, s32[2]{0:T(128)} %pad_add_fusion.place_ref, bf16[16,512,128]{2,1,0:T(8,128)(2,1)} %bitcast.9, bf16[128,512]{1,0:T(8,128)(2,1)} %get-tuple-element.14.q_ref, bf16[128,1024]{1,0:T(8,128)(2,1)} %get-tuple-element.15.rest_0_, bf16[128,1024]{1,0:T(8,128)(2,1)} %copy-done.2, ...), custom_call_target="tpu_custom_call" | custom-call | flops 536870912 | bytes 4194304 | tf_op jit(solution)/shard_map/own/pallas_call | solution.py:378
  148.8 1.7 %collective-permute-done.12.up_ref = bf16[128,2048]{1,0:T(8,128)(2,1)S(1)} collective-permute-done((bf16[128,2048]{1,0:T(8,128)(2,1)}, bf16[128,2048]{1,0:T(8,128)(2,1)S(1)}, u32[]{:S(2)}, u32[]{:S(2)}) %collective-permute-start.12) | collective-permute-done | bytes 524320 | tf_op jit(solution)/shard_map/ppermute | solution.py:303
  150.5 5.2 %collective-permute-done.13.down_ref = bf16[128,2048]{1,0:T(8,128)(2,1)S(1)} collective-permute-done((bf16[128,2048]{1,0:T(8,128)(2,1)}, bf16[128,2048]{1,0:T(8,128)(2,1)S(1)}, u32[]{:S(2)}, u32[]{:S(2)}) %collective-permute-start.13) | collective-permute-done | bytes 524320 | tf_op jit(solution)/shard_map/ppermute | solution.py:303
  156.5 4.4 %finish.1 = f32[128,2048]{1,0:T(8,128)} custom-call(f32[128,2048]{1,0:T(8,128)} %own.1.own_ref, bf16[128,2048]{1,0:T(8,128)(2,1)} %copy-done.7, bf16[128,2048]{1,0:T(8,128)(2,1)} %copy-done.8, bf16[128,2048]{1,0:T(8,128)(2,1)} %bitcast.13, f32[128,2048]{1,0:T(8,128)} %bitcast.11), custom_call_target="tpu_custom_call" | custom-call | flops 4194304 | bytes 5242880 | tf_op jit(solution)/shard_map/finish/pallas_call | solution.py:388
  (42 shorter events, 7.2 us)
Async XLA Ops:
  1.4 34.9 %copy-start.12 = (bf16[64,128]{1,0:T(8,128)(2,1)}, bf16[64,128]{1,0:T(8,128)(2,1)S(1)}, u32[]{:S(2)}) copy-start(bf16[64,128]{1,0:T(8,128)(2,1)S(1)} %add_convert_fusion) | copy-start | bytes 49156
  36.3 60.3 %all-to-all-start.1 = ((bf16[8,16,64,128]{3,2,1,0:T(8,128)(2,1)}), bf16[8,16,64,128]{3,2,1,0:T(8,128)(2,1)S(1)}, u32[]{:S(2)}, u32[]{:S(2)}) async-start(bf16[8,16,64,128]{3,2,1,0:T(8,128)(2,1)} %broadcast_in_dim.7), calls=%async_computation.1 | async-start | bytes 4194304 | tf_op jit(solution)/shard_map/all_to_all | solution.py:341
  45.3 17.6 %collective-permute-start = (bf16[128,1024]{1,0:T(8,128)(2,1)}, bf16[128,1024]{1,0:T(8,128)(2,1)S(1)}, u32[]{:S(2)}, u32[]{:S(2)}) collective-permute-start(bf16[128,1024]{1,0:T(8,128)(2,1)} %get-tuple-element.16), channel_id=1, source_target_pairs={{0,3},{1,0},{2,1},{3,2},{4,7},{5,4},{6,5},{7,6},{8,11},{9,8},{10,9... | collective-permute-start | bytes 786440 | tf_op jit(solution)/shard_map/ppermute | solution.py:303
  48.0 15.0 %collective-permute-start.1 = (bf16[128,1024]{1,0:T(8,128)(2,1)}, bf16[128,1024]{1,0:T(8,128)(2,1)S(1)}, u32[]{:S(2)}, u32[]{:S(2)}) collective-permute-start(bf16[128,1024]{1,0:T(8,128)(2,1)} %get-tuple-element.17), channel_id=1, source_target_pairs={{0,2},{1,3},{2,0},{3,1},{4,6},{5,7},{6,4},{7,5},{8,10},{9,11},{10,... | collective-permute-start | bytes 786440 | tf_op jit(solution)/shard_map/ppermute | solution.py:303
  50.8 14.7 %collective-permute-start.2 = (bf16[128,1024]{1,0:T(8,128)(2,1)}, bf16[128,1024]{1,0:T(8,128)(2,1)S(1)}, u32[]{:S(2)}, u32[]{:S(2)}) collective-permute-start(bf16[128,1024]{1,0:T(8,128)(2,1)} %get-tuple-element.18), channel_id=1, source_target_pairs={{0,1},{1,2},{2,3},{3,0},{4,5},{5,6},{6,7},{7,4},{8,9},{9,10},{10,1... | collective-permute-start | bytes 786440 | tf_op jit(solution)/shard_map/ppermute | solution.py:303
  63.0 33.6 %copy-start.2 = (bf16[128,1024]{1,0:T(8,128)(2,1)}, bf16[128,1024]{1,0:T(8,128)(2,1)S(1)}, u32[]{:S(2)}) copy-start(bf16[128,1024]{1,0:T(8,128)(2,1)S(1)} %collective-permute-done.rest_1_) | copy-start | bytes 786436
  63.0 33.6 %copy-start.3 = (bf16[128,1024]{1,0:T(8,128)(2,1)}, bf16[128,1024]{1,0:T(8,128)(2,1)S(1)}, u32[]{:S(2)}) copy-start(bf16[128,1024]{1,0:T(8,128)(2,1)S(1)} %collective-permute-done.1.rest_2_) | copy-start | bytes 786436
  65.5 0.7 copy-start.4
  66.2 29.6 %collective-permute-start.4 = (bf16[384,1024]{1,0:T(8,128)(2,1)S(1)}, bf16[384,1024]{1,0:T(8,128)(2,1)S(1)}, u32[]{:S(2)}, u32[]{:S(2)}) collective-permute-start(bf16[384,1024]{1,0:T(8,128)(2,1)S(1)} %constant_dynamic-update-slice_fusion), channel_id=1, source_target_pairs={{0,4},{4,8},{8,12},{12,16},{16,20},{20,24},{24,28},{28,256},{256,2... | collective-permute-start | bytes 2359304 | tf_op jit(solution)/shard_map/ppermute | solution.py:303
  69.7 26.8 %collective-permute-start.6 = (bf16[384,1024]{1,0:T(8,128)(2,1)S(1)}, bf16[384,1024]{1,0:T(8,128)(2,1)}, u32[]{:S(2)}, u32[]{:S(2)}) collective-permute-start(bf16[384,1024]{1,0:T(8,128)(2,1)S(1)} %constant_dynamic-update-slice_fusion), channel_id=1, source_target_pairs={{0,284},{4,0},{8,4},{12,8},{16,12},{20,16},{24,20},{28,24},{256,28... | collective-permute-start | bytes 2359304 | tf_op jit(solution)/shard_map/ppermute | solution.py:303
  72.1 20.5 %collective-permute-start.3 = (bf16[128,1024]{1,0:T(8,128)(2,1)}, bf16[128,1024]{1,0:T(8,128)(2,1)S(1)}, u32[]{:S(2)}, u32[]{:S(2)}) collective-permute-start(bf16[128,1024]{1,0:T(8,128)(2,1)} %get-tuple-element.15.rest_0_), channel_id=1, source_target_pairs={{0,4},{4,8},{8,12},{12,16},{16,20},{20,24},{24,28},{28,256},{256,2... | collective-permute-start | bytes 786440 | tf_op jit(solution)/shard_map/ppermute | solution.py:303
  75.6 20.2 %collective-permute-start.5 = (bf16[128,1024]{1,0:T(8,128)(2,1)}, bf16[128,1024]{1,0:T(8,128)(2,1)S(1)}, u32[]{:S(2)}, u32[]{:S(2)}) collective-permute-start(bf16[128,1024]{1,0:T(8,128)(2,1)} %get-tuple-element.15.rest_0_), channel_id=1, source_target_pairs={{0,284},{4,0},{8,4},{12,8},{16,12},{20,16},{24,20},{28,24},{256,28... | collective-permute-start | bytes 786440 | tf_op jit(solution)/shard_map/ppermute | solution.py:303
  78.1 8.6 %collective-permute-start.9 = (bf16[128,512]{1,0:T(8,128)(2,1)}, bf16[128,512]{1,0:T(8,128)(2,1)S(1)}, u32[]{:S(2)}, u32[]{:S(2)}) collective-permute-start(bf16[128,512]{1,0:T(8,128)(2,1)} %get-tuple-element.21), channel_id=1, source_target_pairs={{0,2},{1,3},{2,0},{3,1},{4,6},{5,7},{6,4},{7,5},{8,10},{9,11},{10,... | collective-permute-start | bytes 393224 | tf_op jit(solution)/shard_map/ppermute | solution.py:303
  86.6 9.9 %copy-start.11 = (bf16[128,512]{1,0:T(8,128)(2,1)}, bf16[128,512]{1,0:T(8,128)(2,1)S(1)}, u32[]{:S(2)}) copy-start(bf16[128,512]{1,0:T(8,128)(2,1)S(1)} %collective-permute-done.9.q_ref) | copy-start | bytes 393220
  92.6 3.3 %copy-start.5 = (bf16[128,1024]{1,0:T(8,128)(2,1)}, bf16[128,1024]{1,0:T(8,128)(2,1)S(1)}, u32[]{:S(2)}) copy-start(bf16[128,1024]{1,0:T(8,128)(2,1)S(1)} %collective-permute-done.3.rest_4_) | copy-start | bytes 786436
  95.8 0.7 copy-start.6
  96.5 0.9 copy-start.1
  96.5 1.6 copy-start
  103.4 28.4 %collective-permute-start.10 = (bf16[128,1024]{1,0:T(8,128)(2,1)}, bf16[128,1024]{1,0:T(8,128)(2,1)S(1)}, u32[]{:S(2)}, u32[]{:S(2)}) collective-permute-start(bf16[128,1024]{1,0:T(8,128)(2,1)} %get-tuple-element.22), channel_id=1, source_target_pairs={{0,1},{1,2},{2,3},{3,0},{4,5},{5,6},{6,7},{7,4},{8,9},{9,10},{10,1... | collective-permute-start | bytes 786440 | tf_op jit(solution)/shard_map/ppermute | solution.py:303
  110.2 21.7 %collective-permute-start.11 = (bf16[128,1024]{1,0:T(8,128)(2,1)}, bf16[128,1024]{1,0:T(8,128)(2,1)S(1)}, u32[]{:S(2)}, u32[]{:S(2)}) collective-permute-start(bf16[128,1024]{1,0:T(8,128)(2,1)} %get-tuple-element.23), channel_id=1, source_target_pairs={{0,3},{1,0},{2,1},{3,2},{4,7},{5,4},{6,5},{7,6},{8,11},{9,8},{10,9... | collective-permute-start | bytes 786440 | tf_op jit(solution)/shard_map/ppermute | solution.py:303
  112.1 10.1 %collective-permute-start.7 = (bf16[128,512]{1,0:T(8,128)(2,1)}, bf16[128,512]{1,0:T(8,128)(2,1)S(1)}, u32[]{:S(2)}, u32[]{:S(2)}) collective-permute-start(bf16[128,512]{1,0:T(8,128)(2,1)} %get-tuple-element.19), channel_id=1, source_target_pairs={{0,3},{1,0},{2,1},{3,2},{4,7},{5,4},{6,5},{7,6},{8,11},{9,8},{10,9... | collective-permute-start | bytes 393224 | tf_op jit(solution)/shard_map/ppermute | solution.py:303
  114.1 8.2 %collective-permute-start.8 = (bf16[128,512]{1,0:T(8,128)(2,1)}, bf16[128,512]{1,0:T(8,128)(2,1)S(1)}, u32[]{:S(2)}, u32[]{:S(2)}) collective-permute-start(bf16[128,512]{1,0:T(8,128)(2,1)} %get-tuple-element.20), channel_id=1, source_target_pairs={{0,1},{1,2},{2,3},{3,0},{4,5},{5,6},{6,7},{7,4},{8,9},{9,10},{10,1... | collective-permute-start | bytes 393224 | tf_op jit(solution)/shard_map/ppermute | solution.py:303
  122.3 0.7 copy-start.13
  122.9 0.6 copy-start.14
  131.9 0.7 copy-start.9
  132.6 0.7 copy-start.10
  136.7 13.8 %collective-permute-start.12 = (bf16[128,2048]{1,0:T(8,128)(2,1)}, bf16[128,2048]{1,0:T(8,128)(2,1)S(1)}, u32[]{:S(2)}, u32[]{:S(2)}) collective-permute-start(bf16[128,2048]{1,0:T(8,128)(2,1)} %get-tuple-element.24), channel_id=1, source_target_pairs={{0,1},{1,2},{2,3},{3,0},{4,5},{5,6},{6,7},{7,4},{8,9},{9,10},{10,1... | collective-permute-start | bytes 1572872 | tf_op jit(solution)/shard_map/ppermute | solution.py:303
  140.6 15.2 %collective-permute-start.13 = (bf16[128,2048]{1,0:T(8,128)(2,1)}, bf16[128,2048]{1,0:T(8,128)(2,1)S(1)}, u32[]{:S(2)}, u32[]{:S(2)}) collective-permute-start(bf16[128,2048]{1,0:T(8,128)(2,1)} %get-tuple-element.25), channel_id=1, source_target_pairs={{0,3},{1,0},{2,1},{3,2},{4,7},{5,4},{6,5},{7,6},{8,11},{9,8},{10,9... | collective-permute-start | bytes 1572872 | tf_op jit(solution)/shard_map/ppermute | solution.py:303
  150.5 5.2 %copy-start.7 = (bf16[128,2048]{1,0:T(8,128)(2,1)}, bf16[128,2048]{1,0:T(8,128)(2,1)S(1)}, u32[]{:S(2)}) copy-start(bf16[128,2048]{1,0:T(8,128)(2,1)S(1)} %collective-permute-done.12.up_ref) | copy-start | bytes 1572868
  155.7 0.8 copy-start.8
where the time goes:
time: 162 us; the launch traced here: 161 us
  starting transfers between devices  50.4 us (31%)
  waiting for transfers between devices  35.1 us (22%)
  blocking collectives  32.9 us (20%)
  Pallas kernels  31.8 us (20%)
  local copies, waits for them, and re-layouts  8.5 us (5%)
    ppermute x14, starting transfers between devices, shift(): lax.ppermute(value, axis, [(i, (i + amount) % size) for i in range(size)])  46.1 us
    ppermute x14, waiting for transfers between devices, shift(): lax.ppermute(value, axis, [(i, (i + amount) % size) for i in range(size)])  35.1 us
    all_to_all x1, blocking collectives, block(): lax.all_to_all(jnp.broadcast_to(teacher_new[None], (16,) + teacher_new.sh...  32.9 us
    pallas_call x1, Pallas kernels, block(): pl.pallas_call(near_kernel, out_shape=array(2 * TOKENS, WIDTH), in_specs=...  8.27 us
    unnamed x32, local copies, waits for them, and re-layouts  6.55 us
    pallas_call x1, Pallas kernels, block(): pl.pallas_call(own_kernel, out_shape=array(TOKENS, D, dtype=jnp.float32),...  6.29 us
    pallas_call x1, Pallas kernels, block(): pl.pallas_call(far_kernel, out_shape=(array(TOKENS, HALF),) * 2, in_specs...  5.3 us
    pallas_call x1, Pallas kernels, block(): pl.pallas_call(finish_kernel, grid=(4,), out_shape=array(TOKENS, D, dtype...  4.37 us
  transfers between devices with their start and end apart: 15, of which 8 were waited for; matrix products, arithmetic and copies ran while one was open for 0% of the time, Pallas kernels for 12%

commit v1 on v0

--- a/solution.py
+++ b/solution.py
@@ -42,10 +42,8 @@
                 both = jnp.where(low, left, right)
                 if part == 0:
                     both = both * (1.0 / math.sqrt(HEAD_DIM))
-                    outs[4 + turn][:, pair * LANES : (pair + 1) * LANES] = both.astype(jnp.bfloat16)
-                else:
-                    start = (part - 1) * WIDTH + pair * LANES
-                    outs[turn][:, start : start + LANES] = both.astype(jnp.bfloat16)
+                start = part * WIDTH + pair * LANES
+                outs[turn][:, start : start + LANES] = both.astype(jnp.bfloat16)
 
 
 class Attention:
@@ -60,19 +58,17 @@
             total = total + lengths_ref[0, j]
             self.ends.append(total)
         self.low = lax.broadcasted_iota(jnp.int32, (TOKENS, LANES), 1) < HEAD_DIM
+        pieces, before, after = sources
         self.copies = []
         for turn in range(4):
             slot = lax.rem(self.y + turn, 4)
-            views = [sources[turn]]
-            for side in range(2):
-                own, rest = sources[4 + 2 * side], sources[5 + 2 * side]
-                views.append(own if turn == 0 else rest.at[pl.ds((turn - 1) * TOKENS, TOKENS)])
-            for view, row in zip(views, (1, 0, 2)):
+            span = pl.ds(turn * TOKENS, TOKENS)
+            views = (before.at[span], pieces[turn].at[:, pl.ds(WIDTH, 2 * WIDTH)], after.at[span])
+            for row, view in enumerate(views):
                 where = slot + 4 * row
                 target = kv.at[pl.ds(pl.multiple_of(where * TOKENS, TOKENS), TOKENS)]
-                self.copies.append(
-                    (where, pltpu.make_async_copy(view, target, sems.at[len(self.copies)]))
-                )
+                copy = pltpu.make_async_copy(view, target, sems.at[3 * turn + row])
+                self.copies.append((where, copy))
 
     def keys_of(self, which):
         first = self.row_start + which * TOKENS
@@ -182,90 +178,53 @@
 
 
 def project(mixed, weights_ref, store):
-    for tile in range(0, 16, 2):
-        high, place = divmod(tile, 8)
-        both = jnp.concatenate(
-            [weights_ref[2 * place + high], weights_ref[2 * (place + 1) + high]], axis=1
-        )
-        store(tile * LANES, jnp.dot(mixed, both, preferred_element_type=jnp.float32))
-
-
-HALF = D // 2
+    for tile in range(8):
+        high, place = divmod(tile, 4)
+        both = jnp.concatenate([weights_ref[0, place, high], weights_ref[1, place, high]], axis=1)
+        store(tile * PAIR, jnp.dot(mixed, both, preferred_element_type=jnp.float32))
+
+
 PAIR = 2 * LANES
 
 
-def far_kernel(lengths_ref, place_ref, weights_hbm, q_ref, *rest):
-    sources, (one_ref, two_ref), scratch = rest[:8], rest[8:10], rest[10:]
-    weights, mixed, weight_sem = scratch[6:]
-    fetch = pltpu.make_async_copy(weights_hbm, weights, weight_sem)
-    fetch.start()
-    attention = Attention(lengths_ref, place_ref, sources, *scratch[:6])
-    which = lax.rem(attention.y + 2, 4)
+def rows_kernel(
+    offset, lengths_ref, place_ref, own_weights, other_weights, own, next_piece, far, last, before, after,
+    out_ref, kv, scores, tops, totals, sums, weights, queries, mixed, sems,
+):
+    core = place_ref[2]
+    fetches = [
+        pltpu.make_async_copy(own_weights, weights.at[core], sems.at[12]),
+        pltpu.make_async_copy(other_weights, weights.at[1 - core], sems.at[13]),
+    ]
+    pieces = (own, next_piece, far, last)
+    attention = Attention(
+        lengths_ref, place_ref, (pieces, before, after), kv, scores, tops, totals, sums, sems
+    )
+    which = lax.rem(attention.y + offset, 4)
+    ask = pltpu.make_async_copy(pieces[offset].at[:, pl.ds(0, WIDTH)], queries, sems.at[14])
+    ask.start()
+    for fetch in fetches:
+        fetch.start()
     attention.load([which])
+    ask.wait()
 
     def keep(start, value):
         mixed[:, start : start + LANES] = value
 
-    attention.attend(which, q_ref, keep)
-    fetch.wait()
+    attention.attend(which, queries, keep)
+    for fetch in fetches:
+        fetch.wait()
 
     def store(start, value):
-        out_ref = one_ref if start < HALF else two_ref
-        start = start % HALF
-        out_ref[:, start : start + PAIR] = value.astype(jnp.bfloat16)
+        out_ref[:, start : start + PAIR] = value.astype(out_ref.dtype)
 
     project(mixed[...], weights, store)
 
 
-def near_kernel(lengths_ref, place_ref, q_ref, q3_ref, *rest):
-    sources, out_ref, scratch = rest[:8], rest[8], rest[9:]
-    attention = Attention(lengths_ref, place_ref, sources, *scratch)
-    blocks = [lax.rem(attention.y + 1, 4), lax.rem(attention.y + 3, 4)]
-    attention.load(blocks)
-    for i, ref in enumerate((q_ref, q3_ref)):
-        def keep(start, value):
-            out_ref[i * TOKENS : (i + 1) * TOKENS, start : start + LANES] = value
-
-        attention.attend(blocks[i], ref, keep)
-
-
-def pass_kernel(mixed_ref, weights_ref, one_ref, two_ref, up_ref, down_ref):
-    def store(start, value):
-        up, down = value[:TOKENS], value[TOKENS:]
-        span = slice(start, start + PAIR)
-        if start < HALF:
-            up = up + one_ref[:, span].astype(jnp.float32)
-        else:
-            down = down + two_ref[:, start - HALF : start - HALF + PAIR].astype(jnp.float32)
-        up_ref[:, span] = up.astype(jnp.bfloat16)
-        down_ref[:, span] = down.astype(jnp.bfloat16)
-
-    project(mixed_ref[...], weights_ref, store)
-
-
-def own_kernel(lengths_ref, place_ref, weights_hbm, q_ref, *rest):
-    sources, out_ref, scratch = rest[:8], rest[8], rest[9:]
-    weights, mixed, weight_sem = scratch[6:]
-    fetch = pltpu.make_async_copy(weights_hbm, weights, weight_sem)
-    fetch.start()
-    attention = Attention(lengths_ref, place_ref, sources, *scratch[:6])
-    attention.load([attention.y])
-
-    def keep(start, value):
-        mixed[:, start : start + LANES] = value
-
-    attention.attend(attention.y, q_ref, keep)
-    fetch.wait()
-
-    def store(start, value):
-        out_ref[:, start : start + PAIR] = value
-
-    project(mixed[...], weights, store)
-
-
-def finish_kernel(own_ref, up_ref, down_ref, resid_ref, earlier_ref, out_ref):
-    branch = own_ref[...] + up_ref[...].astype(jnp.float32)
-    branch = branch + down_ref[...].astype(jnp.float32)
+def finish_kernel(own_ref, one_ref, two_ref, three_ref, resid_ref, earlier_ref, out_ref):
+    branch = own_ref[...] + one_ref[...].astype(jnp.float32)
+    branch = branch + two_ref[...].astype(jnp.float32)
+    branch = branch + three_ref[...].astype(jnp.float32)
     summed = resid_ref[...].astype(jnp.float32) + branch * (1.0 / math.sqrt(D))
     centered = summed - jnp.mean(summed, axis=1, keepdims=True)
     spread = jnp.mean(centered * centered, axis=1, keepdims=True)
@@ -276,23 +235,25 @@
 vmem = pl.BlockSpec(memory_space=pltpu.VMEM)
 smem = pl.BlockSpec(memory_space=pltpu.SMEM)
 anywhere = pl.BlockSpec(memory_space=pl.ANY)
-attend_scratch = [
+scratch = [
     pltpu.VMEM((13 * TOKENS, 2 * WIDTH), jnp.bfloat16),
     pltpu.VMEM((6, PAIRS, 2 * TOKENS, CHUNK), jnp.float32),
     pltpu.VMEM((PAIRS, 2 * TOKENS, LANES), jnp.float32),
     pltpu.VMEM((PAIRS, 2 * TOKENS, LANES), jnp.float32),
     pltpu.VMEM((PAIRS, 2 * TOKENS, LANES), jnp.float32),
-    pltpu.SemaphoreType.DMA((12,)),
-]
-project_scratch = [
-    pltpu.VMEM((16, ROW, LANES), jnp.bfloat16),
+    pltpu.VMEM((2, 4, 2, ROW, LANES), jnp.bfloat16),
     pltpu.VMEM((TOKENS, WIDTH), jnp.bfloat16),
-    pltpu.SemaphoreType.DMA,
+    pltpu.VMEM((TOKENS, WIDTH), jnp.bfloat16),
+    pltpu.SemaphoreType.DMA((15,)),
 ]
 
 
 def cost(flops, moved, exps=0):
     return pl.CostEstimate(flops=flops, bytes_accessed=moved, transcendentals=exps)
+
+
+def limit(mebibytes):
+    return pltpu.CompilerParams(vmem_limit_bytes=mebibytes << 20)
 
 
 def array(*shape, dtype=jnp.bfloat16):
@@ -308,92 +269,64 @@
         ema_decay * teacher_out.astype(jnp.float32)
         + (1.0 - ema_decay) * student_out.astype(jnp.float32)
     ).astype(jnp.bfloat16)
-    place = jnp.stack([lax.axis_index("z"), lax.axis_index("y")]).astype(jnp.int32)
+    place = jnp.stack([lax.axis_index(name) for name in ("z", "y", "c")]).astype(jnp.int32)
 
     packed = pl.pallas_call(
         pack_kernel,
         grid=(TOKENS // PACKED,),
-        out_shape=(array(TOKENS, 2 * WIDTH),) * 4 + (array(TOKENS, WIDTH),) * 4,
+        out_shape=(array(TOKENS, 3 * WIDTH),) * 4,
         in_specs=[smem, pl.BlockSpec((PACKED, 3 * D), lambda i: (i, 0))],
-        out_specs=(pl.BlockSpec((PACKED, 2 * WIDTH), lambda i: (i, 0)),) * 4
-        + (pl.BlockSpec((PACKED, WIDTH), lambda i: (i, 0)),) * 4,
+        out_specs=(pl.BlockSpec((PACKED, 3 * WIDTH), lambda i: (i, 0)),) * 4,
+        compiler_params=limit(12),
         cost_estimate=cost(0, 3 << 20),
         name="pack",
     )(place, qkv[0])
-    kv, q = packed[:4], packed[4:]
-
+
+    pieces = [packed[0]]
+    for turn in (1, 2, 3):
+        pieces.append(shift(packed[turn], -turn))
     ring = 2 * lax.axis_size("z")
-    kv_far = shift(kv[2], -2)
-    kv_next = shift(kv[1], -1)
-    kv_last = shift(kv[3], -3)
-    own_after = shift(kv[0], -1, ("h", "z"), ring)
-    own_before = shift(kv[0], 1, ("h", "z"), ring)
-    others = jnp.concatenate([kv_next, kv_far, kv_last], axis=0)
-    after = shift(others, -1, ("h", "z"), ring)
-    before = shift(others, 1, ("h", "z"), ring)
-    q_far = shift(q[2], -2)
-    q_next = shift(q[1], -1)
-    q_last = shift(q[3], -3)
+    keys = jnp.concatenate([piece[:, WIDTH:] for piece in pieces], axis=0)
+    after = shift(keys, -1, ("h", "z"), ring)
+    before = shift(keys, 1, ("h", "z"), ring)
 
     ring_weights = lax.all_to_all(
         jnp.broadcast_to(teacher_new[None], (16,) + teacher_new.shape), ("h", "z"), 0, 0, tiled=True
     )
-    weights = lax.all_to_all(
-        jnp.broadcast_to(ring_weights[None], (8,) + ring_weights.shape), ("x", "c"), 0, 0, tiled=True
-    )
-    weights = weights.reshape(16, ROW, LANES)
-
-    sources = (kv[0], kv_next, kv_far, kv_last, own_before, before, own_after, after)
-    places = [anywhere] * 8
-    one, two = pl.pallas_call(
-        far_kernel,
-        out_shape=(array(TOKENS, HALF),) * 2,
-        in_specs=[smem, smem, anywhere, vmem] + places,
-        out_specs=(vmem,) * 2,
-        scratch_shapes=attend_scratch + project_scratch,
-        cost_estimate=cost(1 << 29, 4 << 20, 1 << 20),
-        name="far",
-    )(lengths, place, weights, q_far, *sources)
-    one = shift(one, 1)
-    two = shift(two, -1)
-    mixed = pl.pallas_call(
-        near_kernel,
-        out_shape=array(2 * TOKENS, WIDTH),
-        in_specs=[smem, smem, vmem, vmem] + places,
-        out_specs=vmem,
-        scratch_shapes=attend_scratch,
-        cost_estimate=cost(1 << 30, 4 << 20, 2 << 20),
-        name="near",
-    )(lengths, place, q_next, q_last, *sources)
-    up, down = pl.pallas_call(
-        pass_kernel,
-        out_shape=(array(TOKENS, D),) * 2,
-        in_specs=[vmem] * 4,
-        out_specs=(vmem,) * 2,
-        cost_estimate=cost(4 * TOKENS * WIDTH * D, 4 << 20),
-        name="pass",
-    )(mixed, weights, one, two)
-    up = shift(up, 1)
-    down = shift(down, -1)
-    own = pl.pallas_call(
-        own_kernel,
-        out_shape=array(TOKENS, D, dtype=jnp.float32),
-        in_specs=[smem, smem, anywhere, vmem] + places,
-        out_specs=vmem,
-        scratch_shapes=attend_scratch + project_scratch,
-        cost_estimate=cost(1 << 29, 4 << 20, 1 << 20),
-        name="own",
-    )(lengths, place, weights, q[0], *sources)
+    ring_weights = ring_weights.reshape(2, ROW, LANES)
+    own_weights = lax.all_to_all(
+        jnp.broadcast_to(ring_weights[None], (4,) + ring_weights.shape), "x", 0, 0, tiled=True
+    )
+    other_weights = shift(own_weights, 1, "c", 2)
+
+    def rows_of(offset, dtype):
+        return pl.pallas_call(
+            functools.partial(rows_kernel, offset),
+            out_shape=array(TOKENS, D, dtype=dtype),
+            in_specs=[smem, smem] + [anywhere] * 8,
+            out_specs=vmem,
+            scratch_shapes=scratch,
+            compiler_params=limit(24),
+            cost_estimate=cost(1 << 29, 4 << 20, 1 << 20),
+            name="rows",
+        )(lengths, place, own_weights, other_weights, *pieces, before, after)
+
+    arrived = []
+    for offset in (2, 1, 3):
+        part = rows_of(offset, jnp.bfloat16)
+        arrived.append(shift(part, offset))
+    own = rows_of(0, jnp.float32)
     rows = pl.BlockSpec((32, D), lambda i: (i, 0))
     targets = pl.pallas_call(
         finish_kernel,
         grid=(4,),
         out_shape=array(TOKENS, D, dtype=jnp.float32),
-        in_specs=[rows] * 5,
+        in_specs=[rows] * 6,
         out_specs=rows,
+        compiler_params=limit(12),
         cost_estimate=cost(1 << 22, 5 << 20),
         name="finish",
-    )(own, up, down, resid[0], earlier[0])
+    )(own, *arrived, resid[0], earlier[0])
     return (targets[None], teacher_new)
 
 

time: 162 us -> 139 us (0.86)
  the two profiles are of different devices: /device:TPU:56 before, /device:TPU:40 now
where the time goes in v1:
time: 139 us
  waiting for transfers between devices  43.3 us (31%)
  starting transfers between devices  33.9 us (24%)
  blocking collectives  32.9 us (24%)
  Pallas kernels  20.1 us (14%)
  local copies, waits for them, and re-layouts  5.54 us (4%)
  other arithmetic  1.89 us (1%)
    ppermute x9, waiting for transfers between devices, shift(): lax.ppermute(value, axis, [(i, (i + amount) % size) for i in range(size)])  43.3 us
    all_to_all x1, blocking collectives, block(): lax.all_to_all(jnp.broadcast_to(teacher_new[None], (16,) + teacher_new.sh...  32.9 us
    ppermute x9, starting transfers between devices, shift(): lax.ppermute(value, axis, [(i, (i + amount) % size) for i in range(size)])  29.7 us
    pallas_call x4, Pallas kernels, rows_of(): pl.pallas_call(functools.partial(rows_kernel, offset), out_shape=array(TO...  15.6 us
    unnamed x22, local copies, waits for them, and re-layouts  4.32 us
    all_to_all x1, starting transfers between devices, block(): lax.all_to_all(jnp.broadcast_to(ring_weights[None], (4,) + ring_weights.s...  4.29 us
  transfers between devices with their start and end apart: 10, of which 7 were waited for; matrix products, arithmetic and copies ran while one was open for 1% of the time, Pallas kernels for 10%

profile of v1, /device:TPU:40, one launch (start us, length us, event | category | flops | bytes accessed | tf_op | source)
XLA Modules:
  0.0 138.5 jit_solution(8487312223627508393)
XLA Ops:
  0.6 0.7 add_convert_fusion
  1.4 0.6 copy-done.10
  2.0 32.9 %all_to_all.10 = bf16[16,64,128]{2,1,0:T(8,128)(2,1)S(1)} all-to-all(bf16[16,64,128]{2,1,0:T(8,128)(2,1)S(1)} %broadcast_in_dim.16), channel_id=1, replica_groups=mesh['h'=2,'x'=4,'c'=2,'z'=8,'y'=4] {'h','z'}, dimensions={0} | all-to-all | bytes 524288 | tf_op jit(solution)/shard_map/all_to_all | solution.py:293
  35.0 1.1 broadcast_in_dim.18
  36.1 4.3 %all-to-all-start.1 = ((bf16[4,2,512,128]{3,2,1,0:T(8,128)(2,1)}), bf16[4,2,512,128]{3,2,1,0:T(8,128)(2,1)S(1)}, u32[]{:S(2)}, u32[]{:S(2)}) async-start(bf16[4,2,512,128]{3,2,1,0:T(8,128)(2,1)} %broadcast_in_dim.18), calls=%async_computation.1 | async-start | bytes 2097152 | tf_op jit(solution)/shard_map/all_to_all | solution.py:297
  40.4 2.2 %pack.1 = (bf16[128,1536]{1,0:T(8,128)(2,1)S(1)}, bf16[128,1536]{1,0:T(8,128)(2,1)S(1)}, bf16[128,1536]{1,0:T(8,128)(2,1)S(1)}, bf16[128,1536]{1,0:T(8,128)(2,1)S(1)}) custom-call(s32[3]{0:T(128)S(1)} %pad_add_fusion.place_ref, bf16[128,6144]{1,0:T(8,128)(2,1)S(1)} %bitcast.8), custom_call_target="tpu_custom_call" | custom-call | bytes 3145728 | tf_op jit(solution)/shard_map/pack/pallas_call | solution.py:274
  42.6 2.4 %collective-permute-start.1 = (bf16[128,1536]{1,0:T(8,128)(2,1)S(1)}, bf16[128,1536]{1,0:T(8,128)(2,1)S(1)}, u32[]{:S(2)}, u32[]{:S(2)}) collective-permute-start(bf16[128,1536]{1,0:T(8,128)(2,1)S(1)} %get-tuple-element.7), channel_id=1, source_target_pairs={{0,3},{1,0},{2,1},{3,2},{4,7},{5,4},{6,5},{7,6},{8,11},{9,8},{10,9... | collective-permute-start | bytes 1179656 | tf_op jit(solution)/shard_map/ppermute | solution.py:264
  45.0 4.5 %collective-permute-start.2 = (bf16[128,1536]{1,0:T(8,128)(2,1)S(1)}, bf16[128,1536]{1,0:T(8,128)(2,1)S(1)}, u32[]{:S(2)}, u32[]{:S(2)}) collective-permute-start(bf16[128,1536]{1,0:T(8,128)(2,1)S(1)} %get-tuple-element.8), channel_id=1, source_target_pairs={{0,2},{1,3},{2,0},{3,1},{4,6},{5,7},{6,4},{7,5},{8,10},{9,11},{10,... | collective-permute-start | bytes 1179656 | tf_op jit(solution)/shard_map/ppermute | solution.py:264
  49.5 3.8 %collective-permute-start.3 = (bf16[128,1536]{1,0:T(8,128)(2,1)S(1)}, bf16[128,1536]{1,0:T(8,128)(2,1)S(1)}, u32[]{:S(2)}, u32[]{:S(2)}) collective-permute-start(bf16[128,1536]{1,0:T(8,128)(2,1)S(1)} %get-tuple-element.9), channel_id=1, source_target_pairs={{0,1},{1,2},{2,3},{3,0},{4,5},{5,6},{6,7},{7,4},{8,9},{9,10},{10,1... | collective-permute-start | bytes 1179656 | tf_op jit(solution)/shard_map/ppermute | solution.py:264
  53.4 2.2 %collective-permute-done.1.next_piece = bf16[128,1536]{1,0:T(8,128)(2,1)S(1)} collective-permute-done((bf16[128,1536]{1,0:T(8,128)(2,1)S(1)}, bf16[128,1536]{1,0:T(8,128)(2,1)S(1)}, u32[]{:S(2)}, u32[]{:S(2)}) %collective-permute-start.1) | collective-permute-done | bytes 393248 | tf_op jit(solution)/shard_map/ppermute | solution.py:264
  55.6 8.2 %collective-permute-done.2.far = bf16[128,1536]{1,0:T(8,128)(2,1)S(1)} collective-permute-done((bf16[128,1536]{1,0:T(8,128)(2,1)S(1)}, bf16[128,1536]{1,0:T(8,128)(2,1)S(1)}, u32[]{:S(2)}, u32[]{:S(2)}) %collective-permute-start.2) | collective-permute-done | bytes 393248 | tf_op jit(solution)/shard_map/ppermute | solution.py:264
  63.8 2.7 %collective-permute-done.3.last = bf16[128,1536]{1,0:T(8,128)(2,1)S(1)} collective-permute-done((bf16[128,1536]{1,0:T(8,128)(2,1)S(1)}, bf16[128,1536]{1,0:T(8,128)(2,1)S(1)}, u32[]{:S(2)}, u32[]{:S(2)}) %collective-permute-start.3) | collective-permute-done | bytes 393248 | tf_op jit(solution)/shard_map/ppermute | solution.py:264
  66.5 0.7 copy-done.4
  67.2 1.1 pad_maximum_fusion
  68.3 1.9 %collective-permute-start.5 = (bf16[512,1024]{1,0:T(8,128)(2,1)}, bf16[512,1024]{1,0:T(8,128)(2,1)S(1)}, u32[]{:S(2)}, u32[]{:S(2)}) collective-permute-start(bf16[512,1024]{1,0:T(8,128)(2,1)} %pad_maximum_fusion), channel_id=1, source_target_pairs={{0,284},{4,0},{8,4},{12,8},{16,12},{20,16},{24,20},{28,24},{256,28... | collective-permute-start | bytes 3145736 | tf_op jit(solution)/shard_map/ppermute | solution.py:264
  70.2 3.9 %collective-permute-start.4 = (bf16[512,1024]{1,0:T(8,128)(2,1)}, bf16[512,1024]{1,0:T(8,128)(2,1)S(1)}, u32[]{:S(2)}, u32[]{:S(2)}) collective-permute-start(bf16[512,1024]{1,0:T(8,128)(2,1)} %pad_maximum_fusion), channel_id=1, source_target_pairs={{0,4},{4,8},{8,12},{12,16},{16,20},{20,24},{24,28},{28,256},{256,2... | collective-permute-start | bytes 3145736 | tf_op jit(solution)/shard_map/ppermute | solution.py:264
  74.2 1.9 %collective-permute-start = (bf16[4,2,512,128]{3,2,1,0:T(8,128)(2,1)S(1)}, bf16[4,2,512,128]{3,2,1,0:T(8,128)(2,1)S(1)}, u32[]{:S(2)}, u32[]{:S(2)}) collective-permute-start(bf16[4,2,512,128]{3,2,1,0:T(8,128)(2,1)S(1)} %all-to-all-done.1.own_weights), channel_id=1, source_target_pairs={{0,32},{32,0},{1,33},{33,1},{2,34},{34,2},{3,35},{35,3},{4,36},{36... | collective-permute-start | bytes 3145736 | tf_op jit(solution)/shard_map/ppermute | solution.py:264
  76.1 18.3 %collective-permute-done.5.after = bf16[512,1024]{1,0:T(8,128)(2,1)S(1)} collective-permute-done((bf16[512,1024]{1,0:T(8,128)(2,1)}, bf16[512,1024]{1,0:T(8,128)(2,1)S(1)}, u32[]{:S(2)}, u32[]{:S(2)}) %collective-permute-start.5) | collective-permute-done | bytes 1048608 | tf_op jit(solution)/shard_map/ppermute | solution.py:264
  94.4 1.9 %collective-permute-done.4.before = bf16[512,1024]{1,0:T(8,128)(2,1)S(1)} collective-permute-done((bf16[512,1024]{1,0:T(8,128)(2,1)}, bf16[512,1024]{1,0:T(8,128)(2,1)S(1)}, u32[]{:S(2)}, u32[]{:S(2)}) %collective-permute-start.4) | collective-permute-done | bytes 1048608 | tf_op jit(solution)/shard_map/ppermute | solution.py:264
  96.4 1.0 copy-done.1
  97.4 1.0 copy-done.3
  98.3 1.0 copy-done.5
  99.3 4.0 %rows.5 = bf16[128,2048]{1,0:T(8,128)(2,1)S(1)} custom-call(s32[1,12]{1,0:T(1,128)S(1)} %copy-done.9, s32[3]{0:T(128)S(1)} %pad_add_fusion.place_ref, bf16[4,2,512,128]{3,2,1,0:T(8,128)(2,1)S(1)} %all-to-all-done.1.own_weights, bf16[4,2,512,128]{3,2,1,0:T(8,128)(2,1)S(1)} %collective-permute-done.other_weights, bf16[128,1536]{1,0:T(8,128)(2,1)S(1)} %get-tuple-element.6.own, ...), custom_call_target="tpu_custom_call" | custom-call | flops 536870912 | bytes 4194304 | tf_op jit(solution)/shard_map/rows/pallas_call | solution.py:303
  103.4 3.6 %collective-permute-start.6 = (bf16[128,2048]{1,0:T(8,128)(2,1)S(1)}, bf16[128,2048]{1,0:T(8,128)(2,1)S(1)}, u32[]{:S(2)}, u32[]{:S(2)}) collective-permute-start(bf16[128,2048]{1,0:T(8,128)(2,1)S(1)} %rows.5), channel_id=1, source_target_pairs={{0,2},{1,3},{2,0},{3,1},{4,6},{5,7},{6,4},{7,5},{8,10},{9,11},{10,... | collective-permute-start | bytes 1572872 | tf_op jit(solution)/shard_map/ppermute | solution.py:264
  107.0 4.7 %rows.6 = bf16[128,2048]{1,0:T(8,128)(2,1)S(1)} custom-call(s32[1,12]{1,0:T(1,128)S(1)} %copy-done.9, s32[3]{0:T(128)S(1)} %pad_add_fusion.place_ref, bf16[4,2,512,128]{3,2,1,0:T(8,128)(2,1)S(1)} %all-to-all-done.1.own_weights, bf16[4,2,512,128]{3,2,1,0:T(8,128)(2,1)S(1)} %collective-permute-done.other_weights, bf16[128,1536]{1,0:T(8,128)(2,1)S(1)} %get-tuple-element.6.own, ...), custom_call_target="tpu_custom_call" | custom-call | flops 536870912 | bytes 4194304 | tf_op jit(solution)/shard_map/rows/pallas_call | solution.py:303
  111.7 5.6 %collective-permute-start.7 = (bf16[128,2048]{1,0:T(8,128)(2,1)S(1)}, bf16[128,2048]{1,0:T(8,128)(2,1)S(1)}, u32[]{:S(2)}, u32[]{:S(2)}) collective-permute-start(bf16[128,2048]{1,0:T(8,128)(2,1)S(1)} %rows.6), channel_id=1, source_target_pairs={{0,1},{1,2},{2,3},{3,0},{4,5},{5,6},{6,7},{7,4},{8,9},{9,10},{10,1... | collective-permute-start | bytes 1572872 | tf_op jit(solution)/shard_map/ppermute | solution.py:264
  117.4 3.4 %rows.7 = bf16[128,2048]{1,0:T(8,128)(2,1)S(1)} custom-call(s32[1,12]{1,0:T(1,128)S(1)} %copy-done.9, s32[3]{0:T(128)S(1)} %pad_add_fusion.place_ref, bf16[4,2,512,128]{3,2,1,0:T(8,128)(2,1)S(1)} %all-to-all-done.1.own_weights, bf16[4,2,512,128]{3,2,1,0:T(8,128)(2,1)S(1)} %collective-permute-done.other_weights, bf16[128,1536]{1,0:T(8,128)(2,1)S(1)} %get-tuple-element.6.own, ...), custom_call_target="tpu_custom_call" | custom-call | flops 536870912 | bytes 4194304 | tf_op jit(solution)/shard_map/rows/pallas_call | solution.py:303
  120.8 2.1 %collective-permute-start.8 = (bf16[128,2048]{1,0:T(8,128)(2,1)S(1)}, bf16[128,2048]{1,0:T(8,128)(2,1)S(1)}, u32[]{:S(2)}, u32[]{:S(2)}) collective-permute-start(bf16[128,2048]{1,0:T(8,128)(2,1)S(1)} %rows.7), channel_id=1, source_target_pairs={{0,3},{1,0},{2,1},{3,2},{4,7},{5,4},{6,5},{7,6},{8,11},{9,8},{10,9... | collective-permute-start | bytes 1572872 | tf_op jit(solution)/shard_map/ppermute | solution.py:264
  122.9 3.4 %rows.4.own_ref = f32[128,2048]{1,0:T(8,128)S(1)} custom-call(s32[1,12]{1,0:T(1,128)S(1)} %copy-done.9, s32[3]{0:T(128)S(1)} %pad_add_fusion.place_ref, bf16[4,2,512,128]{3,2,1,0:T(8,128)(2,1)S(1)} %all-to-all-done.1.own_weights, bf16[4,2,512,128]{3,2,1,0:T(8,128)(2,1)S(1)} %collective-permute-done.other_weights, ...), custom_call_target="tpu_custom_call" | custom-call | flops 536870912 | bytes 4194304 | tf_op jit(solution)/shard_map/rows/pallas_call | solution.py:303
  126.3 5.5 %collective-permute-done.7.two_ref = bf16[128,2048]{1,0:T(8,128)(2,1)S(1)} collective-permute-done((bf16[128,2048]{1,0:T(8,128)(2,1)S(1)}, bf16[128,2048]{1,0:T(8,128)(2,1)S(1)}, u32[]{:S(2)}, u32[]{:S(2)}) %collective-permute-start.7) | collective-permute-done | bytes 524320 | tf_op jit(solution)/shard_map/ppermute | solution.py:264
  131.8 4.5 %collective-permute-done.8.three_ref = bf16[128,2048]{1,0:T(8,128)(2,1)S(1)} collective-permute-done((bf16[128,2048]{1,0:T(8,128)(2,1)S(1)}, bf16[128,2048]{1,0:T(8,128)(2,1)S(1)}, u32[]{:S(2)}, u32[]{:S(2)}) %collective-permute-start.8) | collective-permute-done | bytes 524320 | tf_op jit(solution)/shard_map/ppermute | solution.py:264
  136.2 2.3 %finish.1 = f32[128,2048]{1,0:T(8,128)} custom-call(f32[128,2048]{1,0:T(8,128)S(1)} %rows.4.own_ref, bf16[128,2048]{1,0:T(8,128)(2,1)S(1)} %collective-permute-done.6.one_ref, bf16[128,2048]{1,0:T(8,128)(2,1)S(1)} %collective-permute-done.7.two_ref, bf16[128,2048]{1,0:T(8,128)(2,1)S(1)} %collective-permute-done.8.three_ref, bf16[128,2048]{1,0:T(8,128)(2,1)S(1)} %bitcast.10, ...), custom_call_target="tpu_custom_call" | custom-call | flops 4194304 | bytes 5242880 | tf_op jit(solution)/shard_map/finish/pallas_call | solution.py:320
  (26 shorter events, 0.2 us)
Async XLA Ops:
  1.4 0.6 copy-start.10
  35.0 5.5 %copy-start.6 = (bf16[1,128,6144]{2,1,0:T(8,128)(2,1)S(1)}, bf16[1,128,6144]{2,1,0:T(8,128)(2,1)}, u32[]{:S(2)}) copy-start(bf16[1,128,6144]{2,1,0:T(8,128)(2,1)} %param.6) | copy-start | bytes 4718596
  36.1 38.1 %all-to-all-start.1 = ((bf16[4,2,512,128]{3,2,1,0:T(8,128)(2,1)}), bf16[4,2,512,128]{3,2,1,0:T(8,128)(2,1)S(1)}, u32[]{:S(2)}, u32[]{:S(2)}) async-start(bf16[4,2,512,128]{3,2,1,0:T(8,128)(2,1)} %broadcast_in_dim.18), calls=%async_computation.1 | async-start | bytes 2097152 | tf_op jit(solution)/shard_map/all_to_all | solution.py:297
  42.6 12.9 %collective-permute-start.1 = (bf16[128,1536]{1,0:T(8,128)(2,1)S(1)}, bf16[128,1536]{1,0:T(8,128)(2,1)S(1)}, u32[]{:S(2)}, u32[]{:S(2)}) collective-permute-start(bf16[128,1536]{1,0:T(8,128)(2,1)S(1)} %get-tuple-element.7), channel_id=1, source_target_pairs={{0,3},{1,0},{2,1},{3,2},{4,7},{5,4},{6,5},{7,6},{8,11},{9,8},{10,9... | collective-permute-start | bytes 1179656 | tf_op jit(solution)/shard_map/ppermute | solution.py:264
  45.0 18.7 %collective-permute-start.2 = (bf16[128,1536]{1,0:T(8,128)(2,1)S(1)}, bf16[128,1536]{1,0:T(8,128)(2,1)S(1)}, u32[]{:S(2)}, u32[]{:S(2)}) collective-permute-start(bf16[128,1536]{1,0:T(8,128)(2,1)S(1)} %get-tuple-element.8), channel_id=1, source_target_pairs={{0,2},{1,3},{2,0},{3,1},{4,6},{5,7},{6,4},{7,5},{8,10},{9,11},{10,... | collective-permute-start | bytes 1179656 | tf_op jit(solution)/shard_map/ppermute | solution.py:264
  49.5 17.0 %collective-permute-start.3 = (bf16[128,1536]{1,0:T(8,128)(2,1)S(1)}, bf16[128,1536]{1,0:T(8,128)(2,1)S(1)}, u32[]{:S(2)}, u32[]{:S(2)}) collective-permute-start(bf16[128,1536]{1,0:T(8,128)(2,1)S(1)} %get-tuple-element.9), channel_id=1, source_target_pairs={{0,1},{1,2},{2,3},{3,0},{4,5},{5,6},{6,7},{7,4},{8,9},{9,10},{10,1... | collective-permute-start | bytes 1179656 | tf_op jit(solution)/shard_map/ppermute | solution.py:264
  55.5 11.0 %copy-start = (bf16[128,1536]{1,0:T(8,128)(2,1)}, bf16[128,1536]{1,0:T(8,128)(2,1)S(1)}, u32[]{:S(2)}) copy-start(bf16[128,1536]{1,0:T(8,128)(2,1)S(1)} %collective-permute-done.1.next_piece) | copy-start | bytes 1179652
  55.5 40.8 %copy-start.9 = (s32[1,12]{1,0:T(1,128)S(1)}, s32[1,12]{1,0:T(1,128)}, u32[]{:S(2)}) copy-start(s32[1,12]{1,0:T(1,128)} %lengths_ref.7) | copy-start | bytes 148
  63.8 2.8 %copy-start.2 = (bf16[128,1536]{1,0:T(8,128)(2,1)}, bf16[128,1536]{1,0:T(8,128)(2,1)S(1)}, u32[]{:S(2)}) copy-start(bf16[128,1536]{1,0:T(8,128)(2,1)S(1)} %collective-permute-done.2.far) | copy-start | bytes 1179652
  66.5 0.8 copy-start.4
  68.3 26.1 %collective-permute-start.5 = (bf16[512,1024]{1,0:T(8,128)(2,1)}, bf16[512,1024]{1,0:T(8,128)(2,1)S(1)}, u32[]{:S(2)}, u32[]{:S(2)}) collective-permute-start(bf16[512,1024]{1,0:T(8,128)(2,1)} %pad_maximum_fusion), channel_id=1, source_target_pairs={{0,284},{4,0},{8,4},{12,8},{16,12},{20,16},{24,20},{28,24},{256,28... | collective-permute-start | bytes 3145736 | tf_op jit(solution)/shard_map/ppermute | solution.py:264
  70.2 26.1 %collective-permute-start.4 = (bf16[512,1024]{1,0:T(8,128)(2,1)}, bf16[512,1024]{1,0:T(8,128)(2,1)S(1)}, u32[]{:S(2)}, u32[]{:S(2)}) collective-permute-start(bf16[512,1024]{1,0:T(8,128)(2,1)} %pad_maximum_fusion), channel_id=1, source_target_pairs={{0,4},{4,8},{8,12},{12,16},{16,20},{20,24},{24,28},{28,256},{256,2... | collective-permute-start | bytes 3145736 | tf_op jit(solution)/shard_map/ppermute | solution.py:264
  74.2 22.2 %collective-permute-start = (bf16[4,2,512,128]{3,2,1,0:T(8,128)(2,1)S(1)}, bf16[4,2,512,128]{3,2,1,0:T(8,128)(2,1)S(1)}, u32[]{:S(2)}, u32[]{:S(2)}) collective-permute-start(bf16[4,2,512,128]{3,2,1,0:T(8,128)(2,1)S(1)} %all-to-all-done.1.own_weights), channel_id=1, source_target_pairs={{0,32},{32,0},{1,33},{33,1},{2,34},{34,2},{3,35},{35,3},{4,36},{36... | collective-permute-start | bytes 3145736 | tf_op jit(solution)/shard_map/ppermute | solution.py:264
  96.4 1.0 copy-start.1
  97.3 1.0 copy-start.3
  98.3 1.0 copy-start.5
  103.4 22.9 %collective-permute-start.6 = (bf16[128,2048]{1,0:T(8,128)(2,1)S(1)}, bf16[128,2048]{1,0:T(8,128)(2,1)S(1)}, u32[]{:S(2)}, u32[]{:S(2)}) collective-permute-start(bf16[128,2048]{1,0:T(8,128)(2,1)S(1)} %rows.5), channel_id=1, source_target_pairs={{0,2},{1,3},{2,0},{3,1},{4,6},{5,7},{6,4},{7,5},{8,10},{9,11},{10,... | collective-permute-start | bytes 1572872 | tf_op jit(solution)/shard_map/ppermute | solution.py:264
  111.7 20.0 %collective-permute-start.7 = (bf16[128,2048]{1,0:T(8,128)(2,1)S(1)}, bf16[128,2048]{1,0:T(8,128)(2,1)S(1)}, u32[]{:S(2)}, u32[]{:S(2)}) collective-permute-start(bf16[128,2048]{1,0:T(8,128)(2,1)S(1)} %rows.6), channel_id=1, source_target_pairs={{0,1},{1,2},{2,3},{3,0},{4,5},{5,6},{6,7},{7,4},{8,9},{9,10},{10,1... | collective-permute-start | bytes 1572872 | tf_op jit(solution)/shard_map/ppermute | solution.py:264
  120.8 15.5 %copy-start.7 = (f32[1,128,2048]{2,1,0:T(8,128)S(1)}, f32[1,128,2048]{2,1,0:T(8,128)}, u32[]{:S(2)}) copy-start(f32[1,128,2048]{2,1,0:T(8,128)} %param.8) | copy-start | bytes 3145732
  120.8 15.5 %copy-start.8 = (bf16[1,128,2048]{2,1,0:T(8,128)(2,1)S(1)}, bf16[1,128,2048]{2,1,0:T(8,128)(2,1)}, u32[]{:S(2)}) copy-start(bf16[1,128,2048]{2,1,0:T(8,128)(2,1)} %param.7) | copy-start | bytes 1572868
  120.8 15.4 %collective-permute-start.8 = (bf16[128,2048]{1,0:T(8,128)(2,1)S(1)}, bf16[128,2048]{1,0:T(8,128)(2,1)S(1)}, u32[]{:S(2)}, u32[]{:S(2)}) collective-permute-start(bf16[128,2048]{1,0:T(8,128)(2,1)S(1)} %rows.7), channel_id=1, source_target_pairs={{0,3},{1,0},{2,1},{3,2},{4,7},{5,4},{6,5},{7,6},{8,11},{9,8},{10,9... | collective-permute-start | bytes 1572872 | tf_op jit(solution)/shard_map/ppermute | solution.py:264

commit v2 on v1

--- a/solution.py
+++ b/solution.py
@@ -47,8 +47,7 @@
 
 
 class Attention:
-    def __init__(self, lengths_ref, place_ref, sources, kv, scores, tops, totals, sums, sems):
-        self.kv, self.scores, self.tops, self.totals, self.sums = kv, scores, tops, totals, sums
+    def __init__(self, lengths_ref, place_ref):
         self.row_start = place_ref[0] * ROW
         self.y = place_ref[1]
         self.base = self.row_start - ROW
@@ -58,19 +57,8 @@
             total = total + lengths_ref[0, j]
             self.ends.append(total)
         self.low = lax.broadcasted_iota(jnp.int32, (TOKENS, LANES), 1) < HEAD_DIM
-        pieces, before, after = sources
-        self.copies = []
-        for turn in range(4):
-            slot = lax.rem(self.y + turn, 4)
-            span = pl.ds(turn * TOKENS, TOKENS)
-            views = (before.at[span], pieces[turn].at[:, pl.ds(WIDTH, 2 * WIDTH)], after.at[span])
-            for row, view in enumerate(views):
-                where = slot + 4 * row
-                target = kv.at[pl.ds(pl.multiple_of(where * TOKENS, TOKENS), TOKENS)]
-                copy = pltpu.make_async_copy(view, target, sems.at[3 * turn + row])
-                self.copies.append((where, copy))
-
-    def keys_of(self, which):
+
+    def steps_of(self, which):
         first = self.row_start + which * TOKENS
         last = first + TOKENS - 1
         begin = jnp.int32(0)
@@ -79,25 +67,7 @@
             finish = jnp.where(end > last, end, finish)
         for end in self.ends:
             begin = jnp.where(end <= first, end, begin)
-        start = lax.div(begin - self.base, TOKENS)
-        stop = lax.div(finish - self.base + TOKENS - 1, TOKENS)
-        return start, stop
-
-    def load(self, blocks):
-        ranges = [self.keys_of(which) for which in blocks]
-        start = functools.reduce(jnp.minimum, [r[0] for r in ranges])
-        stop = functools.reduce(jnp.maximum, [r[1] for r in ranges])
-        for where, copy in self.copies:
-            @pl.when((where >= start) & (where < stop))
-            def _():
-                copy.start()
-        self.kv[pl.ds(pl.multiple_of(stop * TOKENS, TOKENS), TOKENS), :] = jnp.zeros(
-            (TOKENS, 2 * WIDTH), jnp.bfloat16
-        )
-        for where, copy in self.copies:
-            @pl.when((where >= start) & (where < stop))
-            def _():
-                copy.wait()
+        return lax.div(begin - self.base, CHUNK), lax.div(finish - self.base + CHUNK - 1, CHUNK)
 
     def segments(self, frames):
         found = jnp.zeros(frames.shape, jnp.int32)
@@ -105,56 +75,65 @@
             found = found + (frames >= end).astype(jnp.int32)
         return jnp.where(frames < 0, -1, found)
 
-    def attend(self, which, q_ref, store):
-        kv, scores, tops, totals, sums, low = (
-            self.kv, self.scores, self.tops, self.totals, self.sums, self.low,
-        )
-        key_block, stop = self.keys_of(which)
-        steps = lax.div(stop - key_block + 1, CHUNK // TOKENS)
+    def attend(self, which, queries, kv, step_of, count, scores, state, prior=None, ready=None):
+        low = self.low
+        tops, totals, sums = (state.at[i] for i in range(3))
         row_segment = self.segments(
             self.row_start + which * TOKENS + lax.broadcasted_iota(jnp.int32, (TOKENS, LANES), 0)
         )
         row_segment = jnp.concatenate([row_segment, row_segment], axis=1)
-        queries = []
+        stacked = []
         for pair in range(PAIRS):
-            one = q_ref[:, pair * LANES : (pair + 1) * LANES]
+            one = queries[:, pair * LANES : (pair + 1) * LANES]
             zero = jnp.zeros_like(one)
-            queries.append(
+            stacked.append(
                 jnp.concatenate([jnp.where(low, one, zero), jnp.where(low, zero, one)], axis=0)
             )
         tops[...] = jnp.full(tops.shape, masked_score, jnp.float32)
-        totals[...] = jnp.zeros(totals.shape, jnp.float32)
-        sums[...] = jnp.zeros(sums.shape, jnp.float32)
-
-        def score(step, carry):
-            start = pl.multiple_of(key_block * TOKENS + step * CHUNK, TOKENS)
+
+        def score(turn, carry):
+            step, place = step_of(turn)
+            start = pl.multiple_of(place * CHUNK, CHUNK)
             key_segment = self.segments(
-                self.base + start + lax.broadcasted_iota(jnp.int32, (8, CHUNK), 1)
+                self.base + step * CHUNK + lax.broadcasted_iota(jnp.int32, (8, CHUNK), 1)
             )[:1]
             allowed = row_segment == key_segment
             allowed = jnp.concatenate([allowed, allowed], axis=0)
             for pair in range(PAIRS):
                 keys = kv[pl.ds(start, CHUNK), pair * LANES : (pair + 1) * LANES]
                 found = lax.dot_general(
-                    queries[pair], keys, (((1,), (1,)), ((), ())),
+                    stacked[pair], keys, (((1,), (1,)), ((), ())),
                     preferred_element_type=jnp.float32,
                 )
                 found = jnp.where(allowed, found, masked_score)
-                scores[step, pair] = found
+                scores[turn, pair] = found
                 tops[pair] = jnp.maximum(
                     tops[pair], jnp.maximum(found[:, :LANES], found[:, LANES:])
                 )
             return carry
 
-        lax.fori_loop(0, steps, score, 0)
+        lax.fori_loop(0, count, score, 0)
+        if ready is not None:
+            ready()
         for pair in range(PAIRS):
             top = jnp.max(tops[pair], axis=1, keepdims=True)
-            tops[pair] = jnp.broadcast_to(top, (2 * TOKENS, LANES))
-
-        def mix(step, carry):
-            start = pl.multiple_of(key_block * TOKENS + step * CHUNK, TOKENS)
+            top = jnp.broadcast_to(top, (2 * TOKENS, LANES))
+            if prior is None:
+                tops[pair] = top
+                totals[pair] = jnp.zeros((2 * TOKENS, LANES), jnp.float32)
+                sums[pair] = jnp.zeros((2 * TOKENS, LANES), jnp.float32)
+            else:
+                top = jnp.maximum(top, prior[0, pair])
+                tops[pair] = top
+                factor = jnp.exp(prior[0, pair] - top)
+                totals[pair] = prior[1, pair] * factor
+                sums[pair] = prior[2, pair] * factor
+
+        def mix(turn, carry):
+            _, place = step_of(turn)
+            start = pl.multiple_of(place * CHUNK, CHUNK)
             for pair in range(PAIRS):
-                found = scores[step, pair]
+                found = scores[turn, pair]
                 left = jnp.exp(found[:, :LANES] - tops[pair])
                 right = jnp.exp(found[:, LANES:] - tops[pair])
                 totals[pair] = totals[pair] + (left + right)
@@ -167,14 +146,48 @@
                 )
             return carry
 
-        lax.fori_loop(0, steps, mix, 0)
-        for pair in range(PAIRS):
-            row_total = jnp.sum(totals[pair], axis=1, keepdims=True)
-            mixed = sums[pair] / row_total
-            store(
-                pair * LANES,
-                jnp.where(low, mixed[:TOKENS], mixed[TOKENS:]).astype(jnp.bfloat16),
+        lax.fori_loop(0, count, mix, 0)
+
+
+def local_kernel(lengths_ref, place_ref, own, next_piece, far, last, *rest):
+    outs, (kv, queries, scores, states, sems) = rest[:4], rest[4:]
+    attention = Attention(lengths_ref, place_ref)
+    pieces = (own, next_piece, far, last)
+    asks, copies = [], []
+    for turn in range(4):
+        slot = lax.rem(attention.y + turn, 4)
+        asks.append(
+            pltpu.make_async_copy(
+                pieces[turn].at[:, pl.ds(0, WIDTH)], queries.at[turn], sems.at[4 + turn]
             )
+        )
+        copies.append(
+            pltpu.make_async_copy(
+                pieces[turn].at[:, pl.ds(WIDTH, 2 * WIDTH)],
+                kv.at[pl.ds(pl.multiple_of(slot * TOKENS, TOKENS), TOKENS)],
+                sems.at[turn],
+            )
+        )
+    for copy in asks + copies:
+        copy.start()
+    for copy in asks + copies:
+        copy.wait()
+    stores = []
+    for i, offset in enumerate((2, 1, 3, 0)):
+        if i >= 2:
+            stores[i - 2].wait()
+        which = lax.rem(attention.y + offset, 4)
+        start, stop = attention.steps_of(which)
+        start, stop = jnp.maximum(start, 2), jnp.minimum(stop, 4)
+        attention.attend(
+            which, queries[offset], kv,
+            lambda turn: (start + turn, start + turn - 2), stop - start,
+            scores, states.at[i % 2],
+        )
+        stores.append(pltpu.make_async_copy(states.at[i % 2], outs[offset], sems.at[8 + i]))
+        stores[i].start()
+    stores[2].wait()
+    stores[3].wait()
 
 
 def project(mixed, weights_ref, store):
@@ -188,30 +201,61 @@
 
 
 def rows_kernel(
-    offset, lengths_ref, place_ref, own_weights, other_weights, own, next_piece, far, last, before, after,
-    out_ref, kv, scores, tops, totals, sums, weights, queries, mixed, sems,
+    offset, lengths_ref, place_ref, own_weights, other_weights, queries,
+    own_before, rest_before, own_after, rest_after, prior_hbm, out_ref,
+    kv, asked, prior, scores, state, weights, mixed, sems,
 ):
     core = place_ref[2]
     fetches = [
-        pltpu.make_async_copy(own_weights, weights.at[core], sems.at[12]),
-        pltpu.make_async_copy(other_weights, weights.at[1 - core], sems.at[13]),
+        pltpu.make_async_copy(own_weights, weights.at[core], sems.at[8]),
+        pltpu.make_async_copy(other_weights, weights.at[1 - core], sems.at[9]),
     ]
-    pieces = (own, next_piece, far, last)
-    attention = Attention(
-        lengths_ref, place_ref, (pieces, before, after), kv, scores, tops, totals, sums, sems
-    )
+    attention = Attention(lengths_ref, place_ref)
     which = lax.rem(attention.y + offset, 4)
-    ask = pltpu.make_async_copy(pieces[offset].at[:, pl.ds(0, WIDTH)], queries, sems.at[14])
+    start, stop = attention.steps_of(which)
+    ahead = jnp.maximum(2 - start, 0)
+    behind = jnp.maximum(stop - 4, 0)
+    copies = []
+    for side, (first, others) in enumerate(((own_before, rest_before), (own_after, rest_after))):
+        for turn in range(4):
+            slot = lax.rem(attention.y + turn, 4)
+            half = lax.div(slot, 2)
+            copy = pltpu.make_async_copy(
+                others.at[pl.ds((turn - 1) * TOKENS, TOKENS)] if turn else first,
+                kv.at[pl.ds(pl.multiple_of((4 * side + slot) * TOKENS, TOKENS), TOKENS)],
+                sems.at[4 * side + turn],
+            )
+            copies.append((half < behind if side else half >= 2 - ahead, copy))
+    ask = pltpu.make_async_copy(queries.at[:, pl.ds(0, WIDTH)], asked, sems.at[10])
+    recall = pltpu.make_async_copy(prior_hbm, prior, sems.at[11])
     ask.start()
+    for wanted, copy in copies:
+        @pl.when(wanted)
+        def _():
+            copy.start()
+    recall.start()
     for fetch in fetches:
         fetch.start()
-    attention.load([which])
     ask.wait()
-
-    def keep(start, value):
-        mixed[:, start : start + LANES] = value
-
-    attention.attend(which, queries, keep)
+    for wanted, copy in copies:
+        @pl.when(wanted)
+        def _():
+            copy.wait()
+
+    def step_of(turn):
+        early = turn < ahead
+        step = jnp.where(early, 2 - ahead + turn, 4 + turn - ahead)
+        return step, jnp.where(early, step, step - 2)
+
+    attention.attend(
+        which, asked[...], kv, step_of, ahead + behind, scores, state, prior, recall.wait
+    )
+    for pair in range(PAIRS):
+        row_total = jnp.sum(state[1, pair], axis=1, keepdims=True)
+        found = state[2, pair] / row_total
+        mixed[:, pair * LANES : (pair + 1) * LANES] = jnp.where(
+            attention.low, found[:TOKENS], found[TOKENS:]
+        ).astype(jnp.bfloat16)
     for fetch in fetches:
         fetch.wait()
 
@@ -235,16 +279,24 @@
 vmem = pl.BlockSpec(memory_space=pltpu.VMEM)
 smem = pl.BlockSpec(memory_space=pltpu.SMEM)
 anywhere = pl.BlockSpec(memory_space=pl.ANY)
-scratch = [
-    pltpu.VMEM((13 * TOKENS, 2 * WIDTH), jnp.bfloat16),
-    pltpu.VMEM((6, PAIRS, 2 * TOKENS, CHUNK), jnp.float32),
-    pltpu.VMEM((PAIRS, 2 * TOKENS, LANES), jnp.float32),
-    pltpu.VMEM((PAIRS, 2 * TOKENS, LANES), jnp.float32),
-    pltpu.VMEM((PAIRS, 2 * TOKENS, LANES), jnp.float32),
+hbm = pl.BlockSpec(memory_space=pltpu.HBM)
+running = (3, PAIRS, 2 * TOKENS, LANES)
+local_scratch = [
+    pltpu.VMEM((ROW, 2 * WIDTH), jnp.bfloat16),
+    pltpu.VMEM((4, TOKENS, WIDTH), jnp.bfloat16),
+    pltpu.VMEM((2, PAIRS, 2 * TOKENS, CHUNK), jnp.float32),
+    pltpu.VMEM((2,) + running, jnp.float32),
+    pltpu.SemaphoreType.DMA((12,)),
+]
+rows_scratch = [
+    pltpu.VMEM((2 * ROW, 2 * WIDTH), jnp.bfloat16),
+    pltpu.VMEM((TOKENS, WIDTH), jnp.bfloat16),
+    pltpu.VMEM(running, jnp.float32),
+    pltpu.VMEM((4, PAIRS, 2 * TOKENS, CHUNK), jnp.float32),
+    pltpu.VMEM(running, jnp.float32),
     pltpu.VMEM((2, 4, 2, ROW, LANES), jnp.bfloat16),
     pltpu.VMEM((TOKENS, WIDTH), jnp.bfloat16),
-    pltpu.VMEM((TOKENS, WIDTH), jnp.bfloat16),
-    pltpu.SemaphoreType.DMA((15,)),
+    pltpu.SemaphoreType.DMA((12,)),
 ]
 
 
@@ -286,9 +338,11 @@
     for turn in (1, 2, 3):
         pieces.append(shift(packed[turn], -turn))
     ring = 2 * lax.axis_size("z")
-    keys = jnp.concatenate([piece[:, WIDTH:] for piece in pieces], axis=0)
-    after = shift(keys, -1, ("h", "z"), ring)
-    before = shift(keys, 1, ("h", "z"), ring)
+    own_after = shift(packed[0][:, WIDTH:], -1, ("h", "z"), ring)
+    own_before = shift(packed[0][:, WIDTH:], 1, ("h", "z"), ring)
+    keys = jnp.concatenate([piece[:, WIDTH:] for piece in pieces[1:]], axis=0)
+    rest_after = shift(keys, -1, ("h", "z"), ring)
+    rest_before = shift(keys, 1, ("h", "z"), ring)
 
     ring_weights = lax.all_to_all(
         jnp.broadcast_to(teacher_new[None], (16,) + teacher_new.shape), ("h", "z"), 0, 0, tiled=True
@@ -298,18 +352,32 @@
         jnp.broadcast_to(ring_weights[None], (4,) + ring_weights.shape), "x", 0, 0, tiled=True
     )
     other_weights = shift(own_weights, 1, "c", 2)
+
+    local = pl.pallas_call(
+        local_kernel,
+        out_shape=(array(*running, dtype=jnp.float32),) * 4,
+        in_specs=[smem, smem] + [hbm] * 4,
+        out_specs=(hbm,) * 4,
+        scratch_shapes=local_scratch,
+        compiler_params=limit(16),
+        cost_estimate=cost(1 << 30, 8 << 20, 2 << 20),
+        name="local",
+    )(lengths, place, *pieces)
 
     def rows_of(offset, dtype):
         return pl.pallas_call(
             functools.partial(rows_kernel, offset),
             out_shape=array(TOKENS, D, dtype=dtype),
-            in_specs=[smem, smem] + [anywhere] * 8,
+            in_specs=[smem, smem] + [anywhere] * 2 + [hbm] + [anywhere] * 4 + [hbm],
             out_specs=vmem,
-            scratch_shapes=scratch,
-            compiler_params=limit(24),
+            scratch_shapes=rows_scratch,
+            compiler_params=limit(20),
             cost_estimate=cost(1 << 29, 4 << 20, 1 << 20),
             name="rows",
-        )(lengths, place, own_weights, other_weights, *pieces, before, after)
+        )(
+            lengths, place, own_weights, other_weights, pieces[offset],
+            own_before, rest_before, own_after, rest_after, local[offset],
+        )
 
     arrived = []
     for offset in (2, 1, 3):

time: 139 us -> 138 us (level)
  the two profiles are of different devices: /device:TPU:40 before, /device:TPU:32 now
where the time goes in v2:
time: 138 us; the launch traced here: 137 us
  waiting for transfers between devices  38.2 us (28%)
  starting transfers between devices  37.4 us (27%)
  blocking collectives  32.9 us (24%)
  Pallas kernels  25.7 us (19%)
    ppermute x11, waiting for transfers between devices, shift(): lax.ppermute(value, axis, [(i, (i + amount) % size) for i in range(size)])  37.3 us
    ppermute x11, starting transfers between devices, shift(): lax.ppermute(value, axis, [(i, (i + amount) % size) for i in range(size)])  33.1 us
    all_to_all x1, blocking collectives, block(): lax.all_to_all(jnp.broadcast_to(teacher_new[None], (16,) + teacher_new.sh...  32.9 us
    pallas_call x4, Pallas kernels, rows_of(): pl.pallas_call(functools.partial(rows_kernel, offset), out_shape=array(TO...  13.2 us
    pallas_call x1, Pallas kernels, block(): pl.pallas_call(local_kernel, out_shape=(array(*running, dtype=jnp.float32...  7.27 us
    all_to_all x1, starting transfers between devices, block(): lax.all_to_all(jnp.broadcast_to(ring_weights[None], (4,) + ring_weights.s...  4.29 us
    pallas_call x1, Pallas kernels, block(): pl.pallas_call(pack_kernel, grid=(TOKENS // PACKED,), out_shape=(array(TO...  2.98 us
  transfers between devices with their start and end apart: 12, of which 6 were waited for; matrix products, arithmetic and copies ran while one was open for 0% of the time, Pallas kernels for 15%

profile of v2, /device:TPU:32, one launch (start us, length us, event | category | flops | bytes accessed | tf_op | source)
XLA Modules:
  0.0 137.2 jit_solution(7141464116976662511)
XLA Ops:
  0.6 0.7 add_convert_fusion
  1.4 0.0 copy-start.4
  1.4 32.9 %all_to_all.10 = bf16[16,64,128]{2,1,0:T(8,128)(2,1)S(1)} all-to-all(bf16[16,64,128]{2,1,0:T(8,128)(2,1)S(1)} %broadcast_in_dim.16), channel_id=1, replica_groups=mesh['h'=2,'x'=4,'c'=2,'z'=8,'y'=4] {'h','z'}, dimensions={0} | all-to-all | bytes 524288 | tf_op jit(solution)/shard_map/all_to_all | solution.py:347
  34.4 1.1 broadcast_in_dim.18
  35.5 4.3 %all-to-all-start.1 = ((bf16[4,2,512,128]{3,2,1,0:T(8,128)(2,1)}), bf16[4,2,512,128]{3,2,1,0:T(8,128)(2,1)S(1)}, u32[]{:S(2)}, u32[]{:S(2)}) async-start(bf16[4,2,512,128]{3,2,1,0:T(8,128)(2,1)} %broadcast_in_dim.18), calls=%async_computation.1 | async-start | bytes 2097152 | tf_op jit(solution)/shard_map/all_to_all | solution.py:351
  39.8 0.1 pad_add_fusion.place_ref
  39.8 3.0 %pack.1 = (bf16[128,1536]{1,0:T(8,128)(2,1)S(1)}, bf16[128,1536]{1,0:T(8,128)(2,1)}, bf16[128,1536]{1,0:T(8,128)(2,1)}, bf16[128,1536]{1,0:T(8,128)(2,1)S(1)}) custom-call(s32[3]{0:T(128)S(1)} %pad_add_fusion.place_ref, bf16[128,6144]{1,0:T(8,128)(2,1)S(1)} %bitcast.8), custom_call_target="tpu_custom_call" | custom-call | bytes 3145728 | tf_op jit(solution)/shard_map/pack/pallas_call | solution.py:326
  42.8 4.9 %collective-permute-start.2 = (bf16[128,1536]{1,0:T(8,128)(2,1)}, bf16[128,1536]{1,0:T(8,128)(2,1)S(1)}, u32[]{:S(2)}, u32[]{:S(2)}) collective-permute-start(bf16[128,1536]{1,0:T(8,128)(2,1)} %get-tuple-element.11), channel_id=1, source_target_pairs={{0,3},{1,0},{2,1},{3,2},{4,7},{5,4},{6,5},{7,6},{8,11},{9,8},{10,9... | collective-permute-start | bytes 1179656 | tf_op jit(solution)/shard_map/ppermute | solution.py:316
  47.7 2.5 %collective-permute-start.3 = (bf16[128,1536]{1,0:T(8,128)(2,1)}, bf16[128,1536]{1,0:T(8,128)(2,1)S(1)}, u32[]{:S(2)}, u32[]{:S(2)}) collective-permute-start(bf16[128,1536]{1,0:T(8,128)(2,1)} %get-tuple-element.12), channel_id=1, source_target_pairs={{0,2},{1,3},{2,0},{3,1},{4,6},{5,7},{6,4},{7,5},{8,10},{9,11},{10,... | collective-permute-start | bytes 1179656 | tf_op jit(solution)/shard_map/ppermute | solution.py:316
  50.3 2.9 %collective-permute-start.4 = (bf16[128,1536]{1,0:T(8,128)(2,1)S(1)}, bf16[128,1536]{1,0:T(8,128)(2,1)S(1)}, u32[]{:S(2)}, u32[]{:S(2)}) collective-permute-start(bf16[128,1536]{1,0:T(8,128)(2,1)S(1)} %get-tuple-element.13), channel_id=1, source_target_pairs={{0,1},{1,2},{2,3},{3,0},{4,5},{5,6},{6,7},{7,4},{8,9},{9,10},{10,1... | collective-permute-start | bytes 1179656 | tf_op jit(solution)/shard_map/ppermute | solution.py:316
  53.2 0.9 all-to-all-done.1.own_weights
  54.1 1.9 %collective-permute-start = (bf16[4,2,512,128]{3,2,1,0:T(8,128)(2,1)S(1)}, bf16[4,2,512,128]{3,2,1,0:T(8,128)(2,1)S(1)}, u32[]{:S(2)}, u32[]{:S(2)}) collective-permute-start(bf16[4,2,512,128]{3,2,1,0:T(8,128)(2,1)S(1)} %all-to-all-done.1.own_weights), channel_id=1, source_target_pairs={{0,32},{32,0},{1,33},{33,1},{2,34},{34,2},{3,35},{35,3},{4,36},{36... | collective-permute-start | bytes 3145736 | tf_op jit(solution)/shard_map/ppermute | solution.py:316
  56.0 7.8 %collective-permute-done.2.next_piece.queries = bf16[128,1536]{1,0:T(8,128)(2,1)S(1)} collective-permute-done((bf16[128,1536]{1,0:T(8,128)(2,1)}, bf16[128,1536]{1,0:T(8,128)(2,1)S(1)}, u32[]{:S(2)}, u32[]{:S(2)}) %collective-permute-start.2) | collective-permute-done | bytes 393248 | tf_op jit(solution)/shard_map/ppermute | solution.py:316
  63.8 0.0 copy-start.3
  63.8 5.4 %collective-permute-done.4.last.queries = bf16[128,1536]{1,0:T(8,128)(2,1)S(1)} collective-permute-done((bf16[128,1536]{1,0:T(8,128)(2,1)S(1)}, bf16[128,1536]{1,0:T(8,128)(2,1)S(1)}, u32[]{:S(2)}, u32[]{:S(2)}) %collective-permute-start.4) | collective-permute-done | bytes 393248 | tf_op jit(solution)/shard_map/ppermute | solution.py:316
  69.3 0.1 pad_maximum_fusion
  69.4 1.9 %collective-permute-start.5 = (bf16[384,1024]{1,0:T(8,128)(2,1)S(1)}, bf16[384,1024]{1,0:T(8,128)(2,1)S(1)}, u32[]{:S(2)}, u32[]{:S(2)}) collective-permute-start(bf16[384,1024]{1,0:T(8,128)(2,1)S(1)} %pad_maximum_fusion), channel_id=1, source_target_pairs={{0,4},{4,8},{8,12},{12,16},{16,20},{20,24},{24,28},{28,256},{256,2... | collective-permute-start | bytes 2359304 | tf_op jit(solution)/shard_map/ppermute | solution.py:316
  71.3 3.9 %collective-permute-start.7 = (bf16[384,1024]{1,0:T(8,128)(2,1)S(1)}, bf16[384,1024]{1,0:T(8,128)(2,1)S(1)}, u32[]{:S(2)}, u32[]{:S(2)}) collective-permute-start(bf16[384,1024]{1,0:T(8,128)(2,1)S(1)} %pad_maximum_fusion), channel_id=1, source_target_pairs={{0,284},{4,0},{8,4},{12,8},{16,12},{20,16},{24,20},{28,24},{256,28... | collective-permute-start | bytes 2359304 | tf_op jit(solution)/shard_map/ppermute | solution.py:316
  75.2 2.4 %collective-permute-start.1 = (bf16[128,1024]{1,0:T(8,128)(2,1)S(1)}, bf16[128,1024]{1,0:T(8,128)(2,1)S(1)}, u32[]{:S(2)}, u32[]{:S(2)}) collective-permute-start(bf16[128,1024]{1,0:T(8,128)(2,1)S(1)} %slice.13), channel_id=1, source_target_pairs={{0,4},{4,8},{8,12},{12,16},{16,20},{20,24},{24,28},{28,256},{256,2... | collective-permute-start | bytes 786440 | tf_op jit(solution)/shard_map/ppermute | solution.py:316
  77.6 3.5 %collective-permute-start.6 = (bf16[128,1024]{1,0:T(8,128)(2,1)S(1)}, bf16[128,1024]{1,0:T(8,128)(2,1)S(1)}, u32[]{:S(2)}, u32[]{:S(2)}) collective-permute-start(bf16[128,1024]{1,0:T(8,128)(2,1)S(1)} %slice.13), channel_id=1, source_target_pairs={{0,284},{4,0},{8,4},{12,8},{16,12},{20,16},{24,20},{28,24},{256,28... | collective-permute-start | bytes 786440 | tf_op jit(solution)/shard_map/ppermute | solution.py:316
  81.1 7.3 %local.1 = (f32[3,4,256,128]{3,2,1,0:T(8,128)S(1)}, f32[3,4,256,128]{3,2,1,0:T(8,128)S(1)}, f32[3,4,256,128]{3,2,1,0:T(8,128)S(1)}, f32[3,4,256,128]{3,2,1,0:T(8,128)S(1)}) custom-call(s32[1,12]{1,0:T(1,128)S(1)} %copy-done.3, s32[3]{0:T(128)S(1)} %pad_add_fusion.place_ref, bf16[128,1536]{1,0:T(8,128)(2,1)S(1)} %get-tuple-element.10.own.queries, ...), custom_call_target="tpu_custom_call" | custom-call | flops 1073741824 | bytes 8388608 | tf_op jit(solution)/shard_map/local/pallas_call | solution.py:356
  88.4 7.9 %collective-permute-done.1.own_before = bf16[128,1024]{1,0:T(8,128)(2,1)S(1)} collective-permute-done((bf16[128,1024]{1,0:T(8,128)(2,1)S(1)}, bf16[128,1024]{1,0:T(8,128)(2,1)S(1)}, u32[]{:S(2)}, u32[]{:S(2)}) %collective-permute-start.1) | collective-permute-done | bytes 262176 | tf_op jit(solution)/shard_map/ppermute | solution.py:316
  96.3 2.4 %collective-permute-done.6.own_after = bf16[128,1024]{1,0:T(8,128)(2,1)S(1)} collective-permute-done((bf16[128,1024]{1,0:T(8,128)(2,1)S(1)}, bf16[128,1024]{1,0:T(8,128)(2,1)S(1)}, u32[]{:S(2)}, u32[]{:S(2)}) %collective-permute-start.6) | collective-permute-done | bytes 262176 | tf_op jit(solution)/shard_map/ppermute | solution.py:316
  98.7 3.5 %rows.7 = bf16[128,2048]{1,0:T(8,128)(2,1)S(1)} custom-call(s32[1,12]{1,0:T(1,128)S(1)} %copy-done.3, s32[3]{0:T(128)S(1)} %pad_add_fusion.place_ref, bf16[4,2,512,128]{3,2,1,0:T(8,128)(2,1)S(1)} %all-to-all-done.1.own_weights, bf16[4,2,512,128]{3,2,1,0:T(8,128)(2,1)S(1)} %collective-permute-done.other_weights, ...), custom_call_target="tpu_custom_call" | custom-call | flops 536870912 | bytes 4194304 | tf_op jit(solution)/shard_map/rows/pallas_call | solution.py:368
  102.2 2.2 %collective-permute-start.10 = (bf16[128,2048]{1,0:T(8,128)(2,1)S(1)}, bf16[128,2048]{1,0:T(8,128)(2,1)S(1)}, u32[]{:S(2)}, u32[]{:S(2)}) collective-permute-start(bf16[128,2048]{1,0:T(8,128)(2,1)S(1)} %rows.7), channel_id=1, source_target_pairs={{0,3},{1,0},{2,1},{3,2},{4,7},{5,4},{6,5},{7,6},{8,11},{9,8},{10,9... | collective-permute-start | bytes 1572872 | tf_op jit(solution)/shard_map/ppermute | solution.py:316
  104.3 2.8 %rows.6 = bf16[128,2048]{1,0:T(8,128)(2,1)S(1)} custom-call(s32[1,12]{1,0:T(1,128)S(1)} %copy-done.3, s32[3]{0:T(128)S(1)} %pad_add_fusion.place_ref, bf16[4,2,512,128]{3,2,1,0:T(8,128)(2,1)S(1)} %all-to-all-done.1.own_weights, bf16[4,2,512,128]{3,2,1,0:T(8,128)(2,1)S(1)} %collective-permute-done.other_weights, ...), custom_call_target="tpu_custom_call" | custom-call | flops 536870912 | bytes 4194304 | tf_op jit(solution)/shard_map/rows/pallas_call | solution.py:368
  107.1 5.1 %collective-permute-start.9 = (bf16[128,2048]{1,0:T(8,128)(2,1)S(1)}, bf16[128,2048]{1,0:T(8,128)(2,1)S(1)}, u32[]{:S(2)}, u32[]{:S(2)}) collective-permute-start(bf16[128,2048]{1,0:T(8,128)(2,1)S(1)} %rows.6), channel_id=1, source_target_pairs={{0,1},{1,2},{2,3},{3,0},{4,5},{5,6},{6,7},{7,4},{8,9},{9,10},{10,1... | collective-permute-start | bytes 1572872 | tf_op jit(solution)/shard_map/ppermute | solution.py:316
  112.2 4.2 %rows.5 = bf16[128,2048]{1,0:T(8,128)(2,1)S(1)} custom-call(s32[1,12]{1,0:T(1,128)S(1)} %copy-done.3, s32[3]{0:T(128)S(1)} %pad_add_fusion.place_ref, bf16[4,2,512,128]{3,2,1,0:T(8,128)(2,1)S(1)} %all-to-all-done.1.own_weights, bf16[4,2,512,128]{3,2,1,0:T(8,128)(2,1)S(1)} %collective-permute-done.other_weights, ...), custom_call_target="tpu_custom_call" | custom-call | flops 536870912 | bytes 4194304 | tf_op jit(solution)/shard_map/rows/pallas_call | solution.py:368
  116.4 1.9 %collective-permute-start.8 = (bf16[128,2048]{1,0:T(8,128)(2,1)S(1)}, bf16[128,2048]{1,0:T(8,128)(2,1)S(1)}, u32[]{:S(2)}, u32[]{:S(2)}) collective-permute-start(bf16[128,2048]{1,0:T(8,128)(2,1)S(1)} %rows.5), channel_id=1, source_target_pairs={{0,2},{1,3},{2,0},{3,1},{4,6},{5,7},{6,4},{7,5},{8,10},{9,11},{10,... | collective-permute-start | bytes 1572872 | tf_op jit(solution)/shard_map/ppermute | solution.py:316
  118.3 2.8 %rows.4.own_ref = f32[128,2048]{1,0:T(8,128)S(1)} custom-call(s32[1,12]{1,0:T(1,128)S(1)} %copy-done.3, s32[3]{0:T(128)S(1)} %pad_add_fusion.place_ref, bf16[4,2,512,128]{3,2,1,0:T(8,128)(2,1)S(1)} %all-to-all-done.1.own_weights, bf16[4,2,512,128]{3,2,1,0:T(8,128)(2,1)S(1)} %collective-permute-done.other_weights, ...), custom_call_target="tpu_custom_call" | custom-call | flops 536870912 | bytes 4194304 | tf_op jit(solution)/shard_map/rows/pallas_call | solution.py:368
  121.1 13.8 %collective-permute-done.9.two_ref = bf16[128,2048]{1,0:T(8,128)(2,1)S(1)} collective-permute-done((bf16[128,2048]{1,0:T(8,128)(2,1)S(1)}, bf16[128,2048]{1,0:T(8,128)(2,1)S(1)}, u32[]{:S(2)}, u32[]{:S(2)}) %collective-permute-start.9) | collective-permute-done | bytes 524320 | tf_op jit(solution)/shard_map/ppermute | solution.py:316
  134.9 2.3 %finish.1 = f32[128,2048]{1,0:T(8,128)} custom-call(f32[128,2048]{1,0:T(8,128)S(1)} %rows.4.own_ref, bf16[128,2048]{1,0:T(8,128)(2,1)S(1)} %collective-permute-done.8.one_ref, bf16[128,2048]{1,0:T(8,128)(2,1)S(1)} %collective-permute-done.9.two_ref, bf16[128,2048]{1,0:T(8,128)(2,1)S(1)} %collective-permute-done.10.three_ref, bf16[128,2048]{1,0:T(8,128)(2,1)S(1)} %bitcast.10, ...), custom_call_target="tpu_custom_call" | custom-call | flops 4194304 | bytes 5242880 | tf_op jit(solution)/shard_map/finish/pallas_call | solution.py:388
  (19 shorter events, 0.2 us)
Async XLA Ops:
  1.4 34.1 %copy-start.4 = (bf16[64,128]{1,0:T(8,128)(2,1)}, bf16[64,128]{1,0:T(8,128)(2,1)S(1)}, u32[]{:S(2)}) copy-start(bf16[64,128]{1,0:T(8,128)(2,1)S(1)} %add_convert_fusion) | copy-start | bytes 49156
  34.4 5.5 %copy-start = (bf16[1,128,6144]{2,1,0:T(8,128)(2,1)S(1)}, bf16[1,128,6144]{2,1,0:T(8,128)(2,1)}, u32[]{:S(2)}) copy-start(bf16[1,128,6144]{2,1,0:T(8,128)(2,1)} %param.6) | copy-start | bytes 4718596
  35.5 18.6 %all-to-all-start.1 = ((bf16[4,2,512,128]{3,2,1,0:T(8,128)(2,1)}), bf16[4,2,512,128]{3,2,1,0:T(8,128)(2,1)S(1)}, u32[]{:S(2)}, u32[]{:S(2)}) async-start(bf16[4,2,512,128]{3,2,1,0:T(8,128)(2,1)} %broadcast_in_dim.18), calls=%async_computation.1 | async-start | bytes 2097152 | tf_op jit(solution)/shard_map/all_to_all | solution.py:351
  42.8 20.9 %collective-permute-start.2 = (bf16[128,1536]{1,0:T(8,128)(2,1)}, bf16[128,1536]{1,0:T(8,128)(2,1)S(1)}, u32[]{:S(2)}, u32[]{:S(2)}) collective-permute-start(bf16[128,1536]{1,0:T(8,128)(2,1)} %get-tuple-element.11), channel_id=1, source_target_pairs={{0,3},{1,0},{2,1},{3,2},{4,7},{5,4},{6,5},{7,6},{8,11},{9,8},{10,9... | collective-permute-start | bytes 1179656 | tf_op jit(solution)/shard_map/ppermute | solution.py:316
  47.7 16.0 %collective-permute-start.3 = (bf16[128,1536]{1,0:T(8,128)(2,1)}, bf16[128,1536]{1,0:T(8,128)(2,1)S(1)}, u32[]{:S(2)}, u32[]{:S(2)}) collective-permute-start(bf16[128,1536]{1,0:T(8,128)(2,1)} %get-tuple-element.12), channel_id=1, source_target_pairs={{0,2},{1,3},{2,0},{3,1},{4,6},{5,7},{6,4},{7,5},{8,10},{9,11},{10,... | collective-permute-start | bytes 1179656 | tf_op jit(solution)/shard_map/ppermute | solution.py:316
  50.3 19.0 %collective-permute-start.4 = (bf16[128,1536]{1,0:T(8,128)(2,1)S(1)}, bf16[128,1536]{1,0:T(8,128)(2,1)S(1)}, u32[]{:S(2)}, u32[]{:S(2)}) collective-permute-start(bf16[128,1536]{1,0:T(8,128)(2,1)S(1)} %get-tuple-element.13), channel_id=1, source_target_pairs={{0,1},{1,2},{2,3},{3,0},{4,5},{5,6},{6,7},{7,4},{8,9},{9,10},{10,1... | collective-permute-start | bytes 1179656 | tf_op jit(solution)/shard_map/ppermute | solution.py:316
  54.1 44.6 %collective-permute-start = (bf16[4,2,512,128]{3,2,1,0:T(8,128)(2,1)S(1)}, bf16[4,2,512,128]{3,2,1,0:T(8,128)(2,1)S(1)}, u32[]{:S(2)}, u32[]{:S(2)}) collective-permute-start(bf16[4,2,512,128]{3,2,1,0:T(8,128)(2,1)S(1)} %all-to-all-done.1.own_weights), channel_id=1, source_target_pairs={{0,32},{32,0},{1,33},{33,1},{2,34},{34,2},{3,35},{35,3},{4,36},{36... | collective-permute-start | bytes 3145736 | tf_op jit(solution)/shard_map/ppermute | solution.py:316
  63.8 17.3 %copy-start.3 = (s32[1,12]{1,0:T(1,128)S(1)}, s32[1,12]{1,0:T(1,128)}, u32[]{:S(2)}) copy-start(s32[1,12]{1,0:T(1,128)} %lengths_ref.9) | copy-start | bytes 148
  69.4 29.3 %collective-permute-start.5 = (bf16[384,1024]{1,0:T(8,128)(2,1)S(1)}, bf16[384,1024]{1,0:T(8,128)(2,1)S(1)}, u32[]{:S(2)}, u32[]{:S(2)}) collective-permute-start(bf16[384,1024]{1,0:T(8,128)(2,1)S(1)} %pad_maximum_fusion), channel_id=1, source_target_pairs={{0,4},{4,8},{8,12},{12,16},{16,20},{20,24},{24,28},{28,256},{256,2... | collective-permute-start | bytes 2359304 | tf_op jit(solution)/shard_map/ppermute | solution.py:316
  71.3 27.4 %collective-permute-start.7 = (bf16[384,1024]{1,0:T(8,128)(2,1)S(1)}, bf16[384,1024]{1,0:T(8,128)(2,1)S(1)}, u32[]{:S(2)}, u32[]{:S(2)}) collective-permute-start(bf16[384,1024]{1,0:T(8,128)(2,1)S(1)} %pad_maximum_fusion), channel_id=1, source_target_pairs={{0,284},{4,0},{8,4},{12,8},{16,12},{20,16},{24,20},{28,24},{256,28... | collective-permute-start | bytes 2359304 | tf_op jit(solution)/shard_map/ppermute | solution.py:316
  75.2 21.1 %collective-permute-start.1 = (bf16[128,1024]{1,0:T(8,128)(2,1)S(1)}, bf16[128,1024]{1,0:T(8,128)(2,1)S(1)}, u32[]{:S(2)}, u32[]{:S(2)}) collective-permute-start(bf16[128,1024]{1,0:T(8,128)(2,1)S(1)} %slice.13), channel_id=1, source_target_pairs={{0,4},{4,8},{8,12},{12,16},{16,20},{20,24},{24,28},{28,256},{256,2... | collective-permute-start | bytes 786440 | tf_op jit(solution)/shard_map/ppermute | solution.py:316
  77.6 21.1 %collective-permute-start.6 = (bf16[128,1024]{1,0:T(8,128)(2,1)S(1)}, bf16[128,1024]{1,0:T(8,128)(2,1)S(1)}, u32[]{:S(2)}, u32[]{:S(2)}) collective-permute-start(bf16[128,1024]{1,0:T(8,128)(2,1)S(1)} %slice.13), channel_id=1, source_target_pairs={{0,284},{4,0},{8,4},{12,8},{16,12},{20,16},{24,20},{28,24},{256,28... | collective-permute-start | bytes 786440 | tf_op jit(solution)/shard_map/ppermute | solution.py:316
  102.2 18.9 %collective-permute-start.10 = (bf16[128,2048]{1,0:T(8,128)(2,1)S(1)}, bf16[128,2048]{1,0:T(8,128)(2,1)S(1)}, u32[]{:S(2)}, u32[]{:S(2)}) collective-permute-start(bf16[128,2048]{1,0:T(8,128)(2,1)S(1)} %rows.7), channel_id=1, source_target_pairs={{0,3},{1,0},{2,1},{3,2},{4,7},{5,4},{6,5},{7,6},{8,11},{9,8},{10,9... | collective-permute-start | bytes 1572872 | tf_op jit(solution)/shard_map/ppermute | solution.py:316
  107.1 27.8 %collective-permute-start.9 = (bf16[128,2048]{1,0:T(8,128)(2,1)S(1)}, bf16[128,2048]{1,0:T(8,128)(2,1)S(1)}, u32[]{:S(2)}, u32[]{:S(2)}) collective-permute-start(bf16[128,2048]{1,0:T(8,128)(2,1)S(1)} %rows.6), channel_id=1, source_target_pairs={{0,1},{1,2},{2,3},{3,0},{4,5},{5,6},{6,7},{7,4},{8,9},{9,10},{10,1... | collective-permute-start | bytes 1572872 | tf_op jit(solution)/shard_map/ppermute | solution.py:316
  116.4 18.5 %collective-permute-start.8 = (bf16[128,2048]{1,0:T(8,128)(2,1)S(1)}, bf16[128,2048]{1,0:T(8,128)(2,1)S(1)}, u32[]{:S(2)}, u32[]{:S(2)}) collective-permute-start(bf16[128,2048]{1,0:T(8,128)(2,1)S(1)} %rows.5), channel_id=1, source_target_pairs={{0,2},{1,3},{2,0},{3,1},{4,6},{5,7},{6,4},{7,5},{8,10},{9,11},{10,... | collective-permute-start | bytes 1572872 | tf_op jit(solution)/shard_map/ppermute | solution.py:316
  118.3 16.6 %copy-start.1 = (f32[1,128,2048]{2,1,0:T(8,128)S(1)}, f32[1,128,2048]{2,1,0:T(8,128)}, u32[]{:S(2)}) copy-start(f32[1,128,2048]{2,1,0:T(8,128)} %param.8) | copy-start | bytes 3145732
  118.3 16.6 %copy-start.2 = (bf16[1,128,2048]{2,1,0:T(8,128)(2,1)S(1)}, bf16[1,128,2048]{2,1,0:T(8,128)(2,1)}, u32[]{:S(2)}) copy-start(bf16[1,128,2048]{2,1,0:T(8,128)(2,1)} %param.7) | copy-start | bytes 1572868

commit v3 on v2

--- a/solution.py
+++ b/solution.py
@@ -77,14 +77,14 @@
 
     def attend(self, which, queries, kv, step_of, count, scores, state, prior=None, ready=None):
         low = self.low
-        tops, totals, sums = (state.at[i] for i in range(3))
+        tops, totals, sums = (state.at[pl.ds(PAIRS * i, PAIRS)] for i in range(3))
         row_segment = self.segments(
             self.row_start + which * TOKENS + lax.broadcasted_iota(jnp.int32, (TOKENS, LANES), 0)
         )
         row_segment = jnp.concatenate([row_segment, row_segment], axis=1)
         stacked = []
         for pair in range(PAIRS):
-            one = queries[:, pair * LANES : (pair + 1) * LANES]
+            one = queries[pair]
             zero = jnp.zeros_like(one)
             stacked.append(
                 jnp.concatenate([jnp.where(low, one, zero), jnp.where(low, zero, one)], axis=0)
@@ -123,11 +123,11 @@
                 totals[pair] = jnp.zeros((2 * TOKENS, LANES), jnp.float32)
                 sums[pair] = jnp.zeros((2 * TOKENS, LANES), jnp.float32)
             else:
-                top = jnp.maximum(top, prior[0, pair])
+                top = jnp.maximum(top, prior[pair])
                 tops[pair] = top
-                factor = jnp.exp(prior[0, pair] - top)
-                totals[pair] = prior[1, pair] * factor
-                sums[pair] = prior[2, pair] * factor
+                factor = jnp.exp(prior[pair] - top)
+                totals[pair] = prior[PAIRS + pair] * factor
+                sums[pair] = prior[2 * PAIRS + pair] * factor
 
         def mix(turn, carry):
             _, place = step_of(turn)
@@ -149,8 +149,12 @@
         lax.fori_loop(0, count, mix, 0)
 
 
+def query_place(pair):
+    return 3 * PAIRS + pair // 2, slice(pair % 2 * TOKENS, (pair % 2 + 1) * TOKENS)
+
+
 def local_kernel(lengths_ref, place_ref, own, next_piece, far, last, *rest):
-    outs, (kv, queries, scores, states, sems) = rest[:4], rest[4:]
+    out, (kv, queries, scores, states, sems) = rest[0], rest[1:]
     attention = Attention(lengths_ref, place_ref)
     pieces = (own, next_piece, far, last)
     asks, copies = [], []
@@ -179,12 +183,16 @@
         which = lax.rem(attention.y + offset, 4)
         start, stop = attention.steps_of(which)
         start, stop = jnp.maximum(start, 2), jnp.minimum(stop, 4)
+        state = states.at[i % 2]
+        asked = [queries[offset, :, pair * LANES : (pair + 1) * LANES] for pair in range(PAIRS)]
+        for pair in range(PAIRS):
+            state[query_place(pair)] = asked[pair].astype(jnp.float32)
         attention.attend(
-            which, queries[offset], kv,
+            which, asked, kv,
             lambda turn: (start + turn, start + turn - 2), stop - start,
-            scores, states.at[i % 2],
+            scores, state,
         )
-        stores.append(pltpu.make_async_copy(states.at[i % 2], outs[offset], sems.at[8 + i]))
+        stores.append(pltpu.make_async_copy(state, out.at[offset], sems.at[8 + i]))
         stores[i].start()
     stores[2].wait()
     stores[3].wait()
@@ -201,9 +209,9 @@
 
 
 def rows_kernel(
-    offset, lengths_ref, place_ref, own_weights, other_weights, queries,
+    offset, lengths_ref, place_ref, own_weights, other_weights,
     own_before, rest_before, own_after, rest_after, prior_hbm, out_ref,
-    kv, asked, prior, scores, state, weights, mixed, sems,
+    kv, prior, scores, state, weights, mixed, sems,
 ):
     core = place_ref[2]
     fetches = [
@@ -226,8 +234,9 @@
                 sems.at[4 * side + turn],
             )
             copies.append((half < behind if side else half >= 2 - ahead, copy))
-    ask = pltpu.make_async_copy(queries.at[:, pl.ds(0, WIDTH)], asked, sems.at[10])
-    recall = pltpu.make_async_copy(prior_hbm, prior, sems.at[11])
+    asked, rest = pl.ds(3 * PAIRS, 2), pl.ds(0, 3 * PAIRS)
+    ask = pltpu.make_async_copy(prior_hbm.at[offset, asked], prior.at[asked], sems.at[10])
+    recall = pltpu.make_async_copy(prior_hbm.at[offset, rest], prior.at[rest], sems.at[11])
     ask.start()
     for wanted, copy in copies:
         @pl.when(wanted)
@@ -247,12 +256,13 @@
         step = jnp.where(early, 2 - ahead + turn, 4 + turn - ahead)
         return step, jnp.where(early, step, step - 2)
 
+    queries = [prior[query_place(pair)].astype(jnp.bfloat16) for pair in range(PAIRS)]
     attention.attend(
-        which, asked[...], kv, step_of, ahead + behind, scores, state, prior, recall.wait
+        which, queries, kv, step_of, ahead + behind, scores, state, prior, recall.wait
     )
     for pair in range(PAIRS):
-        row_total = jnp.sum(state[1, pair], axis=1, keepdims=True)
-        found = state[2, pair] / row_total
+        row_total = jnp.sum(state[PAIRS + pair], axis=1, keepdims=True)
+        found = state[2 * PAIRS + pair] / row_total
         mixed[:, pair * LANES : (pair + 1) * LANES] = jnp.where(
             attention.low, found[:TOKENS], found[TOKENS:]
         ).astype(jnp.bfloat16)
@@ -279,8 +289,7 @@
 vmem = pl.BlockSpec(memory_space=pltpu.VMEM)
 smem = pl.BlockSpec(memory_space=pltpu.SMEM)
 anywhere = pl.BlockSpec(memory_space=pl.ANY)
-hbm = pl.BlockSpec(memory_space=pltpu.HBM)
-running = (3, PAIRS, 2 * TOKENS, LANES)
+running = (3 * PAIRS + 2, 2 * TOKENS, LANES)
 local_scratch = [
     pltpu.VMEM((ROW, 2 * WIDTH), jnp.bfloat16),
     pltpu.VMEM((4, TOKENS, WIDTH), jnp.bfloat16),
@@ -290,7 +299,6 @@
 ]
 rows_scratch = [
     pltpu.VMEM((2 * ROW, 2 * WIDTH), jnp.bfloat16),
-    pltpu.VMEM((TOKENS, WIDTH), jnp.bfloat16),
     pltpu.VMEM(running, jnp.float32),
     pltpu.VMEM((4, PAIRS, 2 * TOKENS, CHUNK), jnp.float32),
     pltpu.VMEM(running, jnp.float32),
@@ -323,7 +331,7 @@
     ).astype(jnp.bfloat16)
     place = jnp.stack([lax.axis_index(name) for name in ("z", "y", "c")]).astype(jnp.int32)
 
-    packed = pl.pallas_call(
+    pack = pl.pallas_call(
         pack_kernel,
         grid=(TOKENS // PACKED,),
         out_shape=(array(TOKENS, 3 * WIDTH),) * 4,
@@ -332,7 +340,8 @@
         compiler_params=limit(12),
         cost_estimate=cost(0, 3 << 20),
         name="pack",
-    )(place, qkv[0])
+    )
+    packed = pack(place, qkv[0])
 
     pieces = [packed[0]]
     for turn in (1, 2, 3):
@@ -355,9 +364,9 @@
 
     local = pl.pallas_call(
         local_kernel,
-        out_shape=(array(*running, dtype=jnp.float32),) * 4,
-        in_specs=[smem, smem] + [hbm] * 4,
-        out_specs=(hbm,) * 4,
+        out_shape=array(4, *running, dtype=jnp.float32),
+        in_specs=[smem, smem] + [anywhere] * 4,
+        out_specs=anywhere,
         scratch_shapes=local_scratch,
         compiler_params=limit(16),
         cost_estimate=cost(1 << 30, 8 << 20, 2 << 20),
@@ -368,15 +377,15 @@
         return pl.pallas_call(
             functools.partial(rows_kernel, offset),
             out_shape=array(TOKENS, D, dtype=dtype),
-            in_specs=[smem, smem] + [anywhere] * 2 + [hbm] + [anywhere] * 4 + [hbm],
+            in_specs=[smem, smem] + [anywhere] * 7,
             out_specs=vmem,
             scratch_shapes=rows_scratch,
-            compiler_params=limit(20),
+            compiler_params=limit(48),
             cost_estimate=cost(1 << 29, 4 << 20, 1 << 20),
             name="rows",
         )(
-            lengths, place, own_weights, other_weights, pieces[offset],
-            own_before, rest_before, own_after, rest_after, local[offset],
+            lengths, place, own_weights, other_weights,
+            own_before, rest_before, own_after, rest_after, local,
         )
 
     arrived = []

time: 138 us -> 134 us (0.971)
  the two profiles are of different devices: /device:TPU:32 before, /device:TPU:1 now
where the time goes in v3:
time: 134 us; the launch traced here: 133 us
  starting transfers between devices  47.9 us (36%)
  blocking collectives  29.3 us (22%)
  Pallas kernels  26.3 us (20%)
  waiting for transfers between devices  23.6 us (18%)
  local copies, waits for them, and re-layouts  4.19 us (3%)
    ppermute x11, starting transfers between devices, shift(): lax.ppermute(value, axis, [(i, (i + amount) % size) for i in range(size)])  43.9 us
    all_to_all x1, blocking collectives, block(): lax.all_to_all(jnp.broadcast_to(teacher_new[None], (16,) + teacher_new.sh...  29.3 us
    ppermute x11, waiting for transfers between devices, shift(): lax.ppermute(value, axis, [(i, (i + amount) % size) for i in range(size)])  23.6 us
    pallas_call x4, Pallas kernels, rows_of(): pl.pallas_call(functools.partial(rows_kernel, offset), out_shape=array(TO...  13.2 us
    pallas_call x1, Pallas kernels, block(): pl.pallas_call(local_kernel, out_shape=array(4, *running, dtype=jnp.float...  7.76 us
    all_to_all x1, starting transfers between devices, block(): lax.all_to_all(jnp.broadcast_to(ring_weights[None], (4,) + ring_weights.s...  4.01 us
    pallas_call x1, Pallas kernels, block(): packed = pack(place, qkv[0])  2.99 us
    unnamed x12, local copies, waits for them, and re-layouts  2.97 us
  transfers between devices with their start and end apart: 12, of which 4 were waited for; matrix products, arithmetic and copies ran while one was open for 0% of the time, Pallas kernels for 16%

profile of v3, /device:TPU:1, one launch (start us, length us, event | category | flops | bytes accessed | tf_op | source)
XLA Modules:
  0.0 133.1 jit_solution(12990634332744065733)
XLA Ops:
  0.6 0.7 add_convert_fusion
  1.4 0.0 copy-start.5
  1.4 29.3 %all_to_all.10 = bf16[16,64,128]{2,1,0:T(8,128)(2,1)S(1)} all-to-all(bf16[16,64,128]{2,1,0:T(8,128)(2,1)S(1)} %broadcast_in_dim.16), channel_id=1, replica_groups=mesh['h'=2,'x'=4,'c'=2,'z'=8,'y'=4] {'h','z'}, dimensions={0} | all-to-all | bytes 524288 | tf_op jit(solution)/shard_map/all_to_all | solution.py:356
  30.8 1.1 broadcast_in_dim.18
  31.9 4.0 %all-to-all-start.1 = ((bf16[4,2,512,128]{3,2,1,0:T(8,128)(2,1)}), bf16[4,2,512,128]{3,2,1,0:T(8,128)(2,1)S(1)}, u32[]{:S(2)}, u32[]{:S(2)}) async-start(bf16[4,2,512,128]{3,2,1,0:T(8,128)(2,1)} %broadcast_in_dim.18), calls=%async_computation.1 | async-start | bytes 2097152 | tf_op jit(solution)/shard_map/all_to_all | solution.py:360
  35.9 0.1 pad_add_fusion.place_ref
  36.0 3.0 %pack.1 = (bf16[128,1536]{1,0:T(8,128)(2,1)S(1)}, bf16[128,1536]{1,0:T(8,128)(2,1)}, bf16[128,1536]{1,0:T(8,128)(2,1)}, bf16[128,1536]{1,0:T(8,128)(2,1)S(1)}) custom-call(s32[3]{0:T(128)S(1)} %pad_add_fusion.place_ref, bf16[128,6144]{1,0:T(8,128)(2,1)S(1)} %bitcast.8), custom_call_target="tpu_custom_call" | custom-call | bytes 3145728 | tf_op jit(solution)/shard_map/pack/pallas_call | solution.py:344
  38.9 4.6 %collective-permute-start.2 = (bf16[128,1536]{1,0:T(8,128)(2,1)}, bf16[128,1536]{1,0:T(8,128)(2,1)S(1)}, u32[]{:S(2)}, u32[]{:S(2)}) collective-permute-start(bf16[128,1536]{1,0:T(8,128)(2,1)} %get-tuple-element.7), channel_id=1, source_target_pairs={{0,3},{1,0},{2,1},{3,2},{4,7},{5,4},{6,5},{7,6},{8,11},{9,8},{10,9... | collective-permute-start | bytes 1179656 | tf_op jit(solution)/shard_map/ppermute | solution.py:324
  43.6 2.3 %collective-permute-start.3 = (bf16[128,1536]{1,0:T(8,128)(2,1)}, bf16[128,1536]{1,0:T(8,128)(2,1)S(1)}, u32[]{:S(2)}, u32[]{:S(2)}) collective-permute-start(bf16[128,1536]{1,0:T(8,128)(2,1)} %get-tuple-element.8), channel_id=1, source_target_pairs={{0,2},{1,3},{2,0},{3,1},{4,6},{5,7},{6,4},{7,5},{8,10},{9,11},{10,... | collective-permute-start | bytes 1179656 | tf_op jit(solution)/shard_map/ppermute | solution.py:324
  45.8 2.6 %collective-permute-start.4 = (bf16[128,1536]{1,0:T(8,128)(2,1)S(1)}, bf16[128,1536]{1,0:T(8,128)(2,1)S(1)}, u32[]{:S(2)}, u32[]{:S(2)}) collective-permute-start(bf16[128,1536]{1,0:T(8,128)(2,1)S(1)} %get-tuple-element.9), channel_id=1, source_target_pairs={{0,1},{1,2},{2,3},{3,0},{4,5},{5,6},{6,7},{7,4},{8,9},{9,10},{10,1... | collective-permute-start | bytes 1179656 | tf_op jit(solution)/shard_map/ppermute | solution.py:324
  48.5 8.6 %collective-permute-start = (bf16[4,2,512,128]{3,2,1,0:T(8,128)(2,1)S(1)}, bf16[4,2,512,128]{3,2,1,0:T(8,128)(2,1)S(1)}, u32[]{:S(2)}, u32[]{:S(2)}) collective-permute-start(bf16[4,2,512,128]{3,2,1,0:T(8,128)(2,1)S(1)} %all-to-all-done.1.own_weights), channel_id=1, source_target_pairs={{0,32},{32,0},{1,33},{33,1},{2,34},{34,2},{3,35},{35,3},{4,36},{36... | collective-permute-start | bytes 3145736 | tf_op jit(solution)/shard_map/ppermute | solution.py:324
  57.1 0.0 copy-start.4
  57.2 6.2 %collective-permute-done.4.last = bf16[128,1536]{1,0:T(8,128)(2,1)S(1)} collective-permute-done((bf16[128,1536]{1,0:T(8,128)(2,1)S(1)}, bf16[128,1536]{1,0:T(8,128)(2,1)S(1)}, u32[]{:S(2)}, u32[]{:S(2)}) %collective-permute-start.4) | collective-permute-done | bytes 393248 | tf_op jit(solution)/shard_map/ppermute | solution.py:324
  63.4 0.1 pad_maximum_fusion
  63.4 9.7 %collective-permute-start.7 = (bf16[384,1024]{1,0:T(8,128)(2,1)S(1)}, bf16[384,1024]{1,0:T(8,128)(2,1)S(1)}, u32[]{:S(2)}, u32[]{:S(2)}) collective-permute-start(bf16[384,1024]{1,0:T(8,128)(2,1)S(1)} %pad_maximum_fusion), channel_id=1, source_target_pairs={{0,284},{4,0},{8,4},{12,8},{16,12},{20,16},{24,20},{28,24},{256,28... | collective-permute-start | bytes 2359304 | tf_op jit(solution)/shard_map/ppermute | solution.py:324
  73.2 2.7 %collective-permute-start.5 = (bf16[384,1024]{1,0:T(8,128)(2,1)S(1)}, bf16[384,1024]{1,0:T(8,128)(2,1)S(1)}, u32[]{:S(2)}, u32[]{:S(2)}) collective-permute-start(bf16[384,1024]{1,0:T(8,128)(2,1)S(1)} %pad_maximum_fusion), channel_id=1, source_target_pairs={{0,4},{4,8},{8,12},{12,16},{16,20},{20,24},{24,28},{28,256},{256,2... | collective-permute-start | bytes 2359304 | tf_op jit(solution)/shard_map/ppermute | solution.py:324
  75.9 3.8 %collective-permute-start.6 = (bf16[128,1024]{1,0:T(8,128)(2,1)S(1)}, bf16[128,1024]{1,0:T(8,128)(2,1)S(1)}, u32[]{:S(2)}, u32[]{:S(2)}) collective-permute-start(bf16[128,1024]{1,0:T(8,128)(2,1)S(1)} %slice.13), channel_id=1, source_target_pairs={{0,284},{4,0},{8,4},{12,8},{16,12},{20,16},{24,20},{28,24},{256,28... | collective-permute-start | bytes 786440 | tf_op jit(solution)/shard_map/ppermute | solution.py:324
  79.7 1.9 %collective-permute-start.1 = (bf16[128,1024]{1,0:T(8,128)(2,1)S(1)}, bf16[128,1024]{1,0:T(8,128)(2,1)S(1)}, u32[]{:S(2)}, u32[]{:S(2)}) collective-permute-start(bf16[128,1024]{1,0:T(8,128)(2,1)S(1)} %slice.13), channel_id=1, source_target_pairs={{0,4},{4,8},{8,12},{12,16},{16,20},{20,24},{24,28},{28,256},{256,2... | collective-permute-start | bytes 786440 | tf_op jit(solution)/shard_map/ppermute | solution.py:324
  81.6 7.8 %local.1.prior_hbm = f32[4,14,256,128]{3,2,1,0:T(8,128)S(1)} custom-call(s32[1,12]{1,0:T(1,128)S(1)} %copy-done.4, s32[3]{0:T(128)S(1)} %pad_add_fusion.place_ref, bf16[128,1536]{1,0:T(8,128)(2,1)S(1)} %get-tuple-element.6.own, bf16[128,1536]{1,0:T(8,128)(2,1)S(1)} %collective-permute-done.2.next_piece, bf16[128,1536]{1,0:T(8,128)(2,1)S(1)} %collective-permute-done.3.far, ...), custom_call_target="tpu_custom_call" | custom-call | flops 1073741824 | bytes 8388608 | tf_op jit(solution)/shard_map/local/pallas_call | solution.py:365
  89.4 2.9 %copy-done = f32[4,14,256,128]{3,2,1,0:T(8,128)} copy-done((f32[4,14,256,128]{3,2,1,0:T(8,128)}, f32[4,14,256,128]{3,2,1,0:T(8,128)S(1)}, u32[]{:S(2)}) %copy-start) | copy-done | bytes 7340056
  92.3 4.6 %collective-permute-done.6.own_after = bf16[128,1024]{1,0:T(8,128)(2,1)S(1)} collective-permute-done((bf16[128,1024]{1,0:T(8,128)(2,1)S(1)}, bf16[128,1024]{1,0:T(8,128)(2,1)S(1)}, u32[]{:S(2)}, u32[]{:S(2)}) %collective-permute-start.6) | collective-permute-done | bytes 262176 | tf_op jit(solution)/shard_map/ppermute | solution.py:324
  97.0 2.2 %collective-permute-done.1.own_before = bf16[128,1024]{1,0:T(8,128)(2,1)S(1)} collective-permute-done((bf16[128,1024]{1,0:T(8,128)(2,1)S(1)}, bf16[128,1024]{1,0:T(8,128)(2,1)S(1)}, u32[]{:S(2)}, u32[]{:S(2)}) %collective-permute-start.1) | collective-permute-done | bytes 262176 | tf_op jit(solution)/shard_map/ppermute | solution.py:324
  99.2 3.1 %rows.5 = bf16[128,2048]{1,0:T(8,128)(2,1)S(1)} custom-call(s32[1,12]{1,0:T(1,128)S(1)} %copy-done.4, s32[3]{0:T(128)S(1)} %pad_add_fusion.place_ref, bf16[4,2,512,128]{3,2,1,0:T(8,128)(2,1)S(1)} %all-to-all-done.1.own_weights, bf16[4,2,512,128]{3,2,1,0:T(8,128)(2,1)S(1)} %collective-permute-done.other_weights, ...), custom_call_target="tpu_custom_call" | custom-call | flops 536870912 | bytes 4194304 | tf_op jit(solution)/shard_map/rows/pallas_call | solution.py:377
  102.3 1.9 %collective-permute-start.8 = (bf16[128,2048]{1,0:T(8,128)(2,1)S(1)}, bf16[128,2048]{1,0:T(8,128)(2,1)S(1)}, u32[]{:S(2)}, u32[]{:S(2)}) collective-permute-start(bf16[128,2048]{1,0:T(8,128)(2,1)S(1)} %rows.5), channel_id=1, source_target_pairs={{0,2},{1,3},{2,0},{3,1},{4,6},{5,7},{6,4},{7,5},{8,10},{9,11},{10,... | collective-permute-start | bytes 1572872 | tf_op jit(solution)/shard_map/ppermute | solution.py:324
  104.2 3.1 %rows.6 = bf16[128,2048]{1,0:T(8,128)(2,1)S(1)} custom-call(s32[1,12]{1,0:T(1,128)S(1)} %copy-done.4, s32[3]{0:T(128)S(1)} %pad_add_fusion.place_ref, bf16[4,2,512,128]{3,2,1,0:T(8,128)(2,1)S(1)} %all-to-all-done.1.own_weights, bf16[4,2,512,128]{3,2,1,0:T(8,128)(2,1)S(1)} %collective-permute-done.other_weights, ...), custom_call_target="tpu_custom_call" | custom-call | flops 536870912 | bytes 4194304 | tf_op jit(solution)/shard_map/rows/pallas_call | solution.py:377
  107.3 1.9 %collective-permute-start.9 = (bf16[128,2048]{1,0:T(8,128)(2,1)S(1)}, bf16[128,2048]{1,0:T(8,128)(2,1)S(1)}, u32[]{:S(2)}, u32[]{:S(2)}) collective-permute-start(bf16[128,2048]{1,0:T(8,128)(2,1)S(1)} %rows.6), channel_id=1, source_target_pairs={{0,1},{1,2},{2,3},{3,0},{4,5},{5,6},{6,7},{7,4},{8,9},{9,10},{10,1... | collective-permute-start | bytes 1572872 | tf_op jit(solution)/shard_map/ppermute | solution.py:324
  109.3 3.9 %rows.7 = bf16[128,2048]{1,0:T(8,128)(2,1)S(1)} custom-call(s32[1,12]{1,0:T(1,128)S(1)} %copy-done.4, s32[3]{0:T(128)S(1)} %pad_add_fusion.place_ref, bf16[4,2,512,128]{3,2,1,0:T(8,128)(2,1)S(1)} %all-to-all-done.1.own_weights, bf16[4,2,512,128]{3,2,1,0:T(8,128)(2,1)S(1)} %collective-permute-done.other_weights, ...), custom_call_target="tpu_custom_call" | custom-call | flops 536870912 | bytes 4194304 | tf_op jit(solution)/shard_map/rows/pallas_call | solution.py:377
  113.2 0.0 copy-start.3
  113.2 3.9 %collective-permute-start.10 = (bf16[128,2048]{1,0:T(8,128)(2,1)S(1)}, bf16[128,2048]{1,0:T(8,128)(2,1)S(1)}, u32[]{:S(2)}, u32[]{:S(2)}) collective-permute-start(bf16[128,2048]{1,0:T(8,128)(2,1)S(1)} %rows.7), channel_id=1, source_target_pairs={{0,3},{1,0},{2,1},{3,2},{4,7},{5,4},{6,5},{7,6},{8,11},{9,8},{10,9... | collective-permute-start | bytes 1572872 | tf_op jit(solution)/shard_map/ppermute | solution.py:324
  117.1 3.1 %rows.4.own_ref = f32[128,2048]{1,0:T(8,128)S(1)} custom-call(s32[1,12]{1,0:T(1,128)S(1)} %copy-done.4, s32[3]{0:T(128)S(1)} %pad_add_fusion.place_ref, bf16[4,2,512,128]{3,2,1,0:T(8,128)(2,1)S(1)} %all-to-all-done.1.own_weights, bf16[4,2,512,128]{3,2,1,0:T(8,128)(2,1)S(1)} %collective-permute-done.other_weights, ...), custom_call_target="tpu_custom_call" | custom-call | flops 536870912 | bytes 4194304 | tf_op jit(solution)/shard_map/rows/pallas_call | solution.py:377
  120.2 10.5 %collective-permute-done.9.two_ref = bf16[128,2048]{1,0:T(8,128)(2,1)S(1)} collective-permute-done((bf16[128,2048]{1,0:T(8,128)(2,1)S(1)}, bf16[128,2048]{1,0:T(8,128)(2,1)S(1)}, u32[]{:S(2)}, u32[]{:S(2)}) %collective-permute-start.9) | collective-permute-done | bytes 524320 | tf_op jit(solution)/shard_map/ppermute | solution.py:324
  130.8 2.3 %finish.1 = f32[128,2048]{1,0:T(8,128)} custom-call(f32[128,2048]{1,0:T(8,128)S(1)} %rows.4.own_ref, bf16[128,2048]{1,0:T(8,128)(2,1)S(1)} %collective-permute-done.8.one_ref, bf16[128,2048]{1,0:T(8,128)(2,1)S(1)} %collective-permute-done.9.two_ref, bf16[128,2048]{1,0:T(8,128)(2,1)S(1)} %collective-permute-done.10.three_ref, bf16[128,2048]{1,0:T(8,128)(2,1)S(1)} %bitcast.10, ...), custom_call_target="tpu_custom_call" | custom-call | flops 4194304 | bytes 5242880 | tf_op jit(solution)/shard_map/finish/pallas_call | solution.py:397
  (21 shorter events, 0.2 us)
Async XLA Ops:
  1.4 30.5 %copy-start.5 = (bf16[64,128]{1,0:T(8,128)(2,1)}, bf16[64,128]{1,0:T(8,128)(2,1)S(1)}, u32[]{:S(2)}) copy-start(bf16[64,128]{1,0:T(8,128)(2,1)S(1)} %add_convert_fusion) | copy-start | bytes 49156
  30.8 5.2 %copy-start.1 = (bf16[1,128,6144]{2,1,0:T(8,128)(2,1)S(1)}, bf16[1,128,6144]{2,1,0:T(8,128)(2,1)}, u32[]{:S(2)}) copy-start(bf16[1,128,6144]{2,1,0:T(8,128)(2,1)} %param.6) | copy-start | bytes 4718596
  31.9 16.6 %all-to-all-start.1 = ((bf16[4,2,512,128]{3,2,1,0:T(8,128)(2,1)}), bf16[4,2,512,128]{3,2,1,0:T(8,128)(2,1)S(1)}, u32[]{:S(2)}, u32[]{:S(2)}) async-start(bf16[4,2,512,128]{3,2,1,0:T(8,128)(2,1)} %broadcast_in_dim.18), calls=%async_computation.1 | async-start | bytes 2097152 | tf_op jit(solution)/shard_map/all_to_all | solution.py:360
  38.9 18.1 %collective-permute-start.2 = (bf16[128,1536]{1,0:T(8,128)(2,1)}, bf16[128,1536]{1,0:T(8,128)(2,1)S(1)}, u32[]{:S(2)}, u32[]{:S(2)}) collective-permute-start(bf16[128,1536]{1,0:T(8,128)(2,1)} %get-tuple-element.7), channel_id=1, source_target_pairs={{0,3},{1,0},{2,1},{3,2},{4,7},{5,4},{6,5},{7,6},{8,11},{9,8},{10,9... | collective-permute-start | bytes 1179656 | tf_op jit(solution)/shard_map/ppermute | solution.py:324
  43.6 13.5 %collective-permute-start.3 = (bf16[128,1536]{1,0:T(8,128)(2,1)}, bf16[128,1536]{1,0:T(8,128)(2,1)S(1)}, u32[]{:S(2)}, u32[]{:S(2)}) collective-permute-start(bf16[128,1536]{1,0:T(8,128)(2,1)} %get-tuple-element.8), channel_id=1, source_target_pairs={{0,2},{1,3},{2,0},{3,1},{4,6},{5,7},{6,4},{7,5},{8,10},{9,11},{10,... | collective-permute-start | bytes 1179656 | tf_op jit(solution)/shard_map/ppermute | solution.py:324
  45.8 17.5 %collective-permute-start.4 = (bf16[128,1536]{1,0:T(8,128)(2,1)S(1)}, bf16[128,1536]{1,0:T(8,128)(2,1)S(1)}, u32[]{:S(2)}, u32[]{:S(2)}) collective-permute-start(bf16[128,1536]{1,0:T(8,128)(2,1)S(1)} %get-tuple-element.9), channel_id=1, source_target_pairs={{0,1},{1,2},{2,3},{3,0},{4,5},{5,6},{6,7},{7,4},{8,9},{9,10},{10,1... | collective-permute-start | bytes 1179656 | tf_op jit(solution)/shard_map/ppermute | solution.py:324
  48.5 50.7 %collective-permute-start = (bf16[4,2,512,128]{3,2,1,0:T(8,128)(2,1)S(1)}, bf16[4,2,512,128]{3,2,1,0:T(8,128)(2,1)S(1)}, u32[]{:S(2)}, u32[]{:S(2)}) collective-permute-start(bf16[4,2,512,128]{3,2,1,0:T(8,128)(2,1)S(1)} %all-to-all-done.1.own_weights), channel_id=1, source_target_pairs={{0,32},{32,0},{1,33},{33,1},{2,34},{34,2},{3,35},{35,3},{4,36},{36... | collective-permute-start | bytes 3145736 | tf_op jit(solution)/shard_map/ppermute | solution.py:324
  57.1 24.5 %copy-start.4 = (s32[1,12]{1,0:T(1,128)S(1)}, s32[1,12]{1,0:T(1,128)}, u32[]{:S(2)}) copy-start(s32[1,12]{1,0:T(1,128)} %lengths_ref.9) | copy-start | bytes 148
  63.4 35.7 %collective-permute-start.7 = (bf16[384,1024]{1,0:T(8,128)(2,1)S(1)}, bf16[384,1024]{1,0:T(8,128)(2,1)S(1)}, u32[]{:S(2)}, u32[]{:S(2)}) collective-permute-start(bf16[384,1024]{1,0:T(8,128)(2,1)S(1)} %pad_maximum_fusion), channel_id=1, source_target_pairs={{0,284},{4,0},{8,4},{12,8},{16,12},{20,16},{24,20},{28,24},{256,28... | collective-permute-start | bytes 2359304 | tf_op jit(solution)/shard_map/ppermute | solution.py:324
  73.2 26.0 %collective-permute-start.5 = (bf16[384,1024]{1,0:T(8,128)(2,1)S(1)}, bf16[384,1024]{1,0:T(8,128)(2,1)S(1)}, u32[]{:S(2)}, u32[]{:S(2)}) collective-permute-start(bf16[384,1024]{1,0:T(8,128)(2,1)S(1)} %pad_maximum_fusion), channel_id=1, source_target_pairs={{0,4},{4,8},{8,12},{12,16},{16,20},{20,24},{24,28},{28,256},{256,2... | collective-permute-start | bytes 2359304 | tf_op jit(solution)/shard_map/ppermute | solution.py:324
  75.9 21.1 %collective-permute-start.6 = (bf16[128,1024]{1,0:T(8,128)(2,1)S(1)}, bf16[128,1024]{1,0:T(8,128)(2,1)S(1)}, u32[]{:S(2)}, u32[]{:S(2)}) collective-permute-start(bf16[128,1024]{1,0:T(8,128)(2,1)S(1)} %slice.13), channel_id=1, source_target_pairs={{0,284},{4,0},{8,4},{12,8},{16,12},{20,16},{24,20},{28,24},{256,28... | collective-permute-start | bytes 786440 | tf_op jit(solution)/shard_map/ppermute | solution.py:324
  79.7 19.5 %collective-permute-start.1 = (bf16[128,1024]{1,0:T(8,128)(2,1)S(1)}, bf16[128,1024]{1,0:T(8,128)(2,1)S(1)}, u32[]{:S(2)}, u32[]{:S(2)}) collective-permute-start(bf16[128,1024]{1,0:T(8,128)(2,1)S(1)} %slice.13), channel_id=1, source_target_pairs={{0,4},{4,8},{8,12},{12,16},{16,20},{20,24},{24,28},{28,256},{256,2... | collective-permute-start | bytes 786440 | tf_op jit(solution)/shard_map/ppermute | solution.py:324
  89.4 2.9 %copy-start = (f32[4,14,256,128]{3,2,1,0:T(8,128)}, f32[4,14,256,128]{3,2,1,0:T(8,128)S(1)}, u32[]{:S(2)}) copy-start(f32[4,14,256,128]{3,2,1,0:T(8,128)S(1)} %local.1.prior_hbm) | copy-start | bytes 22020100
  102.3 17.9 %collective-permute-start.8 = (bf16[128,2048]{1,0:T(8,128)(2,1)S(1)}, bf16[128,2048]{1,0:T(8,128)(2,1)S(1)}, u32[]{:S(2)}, u32[]{:S(2)}) collective-permute-start(bf16[128,2048]{1,0:T(8,128)(2,1)S(1)} %rows.5), channel_id=1, source_target_pairs={{0,2},{1,3},{2,0},{3,1},{4,6},{5,7},{6,4},{7,5},{8,10},{9,11},{10,... | collective-permute-start | bytes 1572872 | tf_op jit(solution)/shard_map/ppermute | solution.py:324
  107.3 23.4 %collective-permute-start.9 = (bf16[128,2048]{1,0:T(8,128)(2,1)S(1)}, bf16[128,2048]{1,0:T(8,128)(2,1)S(1)}, u32[]{:S(2)}, u32[]{:S(2)}) collective-permute-start(bf16[128,2048]{1,0:T(8,128)(2,1)S(1)} %rows.6), channel_id=1, source_target_pairs={{0,1},{1,2},{2,3},{3,0},{4,5},{5,6},{6,7},{7,4},{8,9},{9,10},{10,1... | collective-permute-start | bytes 1572872 | tf_op jit(solution)/shard_map/ppermute | solution.py:324
  113.2 17.6 %copy-start.2 = (f32[1,128,2048]{2,1,0:T(8,128)S(1)}, f32[1,128,2048]{2,1,0:T(8,128)}, u32[]{:S(2)}) copy-start(f32[1,128,2048]{2,1,0:T(8,128)} %param.8) | copy-start | bytes 3145732
  113.2 17.6 %copy-start.3 = (bf16[1,128,2048]{2,1,0:T(8,128)(2,1)S(1)}, bf16[1,128,2048]{2,1,0:T(8,128)(2,1)}, u32[]{:S(2)}) copy-start(bf16[1,128,2048]{2,1,0:T(8,128)(2,1)} %param.7) | copy-start | bytes 1572868
  113.2 17.5 %collective-permute-start.10 = (bf16[128,2048]{1,0:T(8,128)(2,1)S(1)}, bf16[128,2048]{1,0:T(8,128)(2,1)S(1)}, u32[]{:S(2)}, u32[]{:S(2)}) collective-permute-start(bf16[128,2048]{1,0:T(8,128)(2,1)S(1)} %rows.7), channel_id=1, source_target_pairs={{0,3},{1,0},{2,1},{3,2},{4,7},{5,4},{6,5},{7,6},{8,11},{9,8},{10,9... | collective-permute-start | bytes 1572872 | tf_op jit(solution)/shard_map/ppermute | solution.py:324

commit v4 on v3

--- a/solution.py
+++ b/solution.py
@@ -18,6 +18,8 @@
 WIDTH = 512
 CHUNK = 256
 PAIRS = WIDTH // LANES
+LOCAL_LIMIT = 58
+ROWS_LIMIT = 48
 PACKED = 32
 
 ema_decay = 0.9
@@ -57,6 +59,7 @@
             total = total + lengths_ref[0, j]
             self.ends.append(total)
         self.low = lax.broadcasted_iota(jnp.int32, (TOKENS, LANES), 1) < HEAD_DIM
+        self.middle = lax.broadcasted_iota(jnp.int32, (2 * TOKENS, LANES), 1) == HEAD_DIM
 
     def steps_of(self, which):
         first = self.row_start + which * TOKENS
@@ -75,7 +78,7 @@
             found = found + (frames >= end).astype(jnp.int32)
         return jnp.where(frames < 0, -1, found)
 
-    def attend(self, which, queries, kv, step_of, count, scores, state, prior=None, ready=None):
+    def attend(self, which, queries, kv, step_of, count, scores, state, prior=None):
         low = self.low
         tops, totals, sums = (state.at[pl.ds(PAIRS * i, PAIRS)] for i in range(3))
         row_segment = self.segments(
@@ -113,8 +116,6 @@
             return carry
 
         lax.fori_loop(0, count, score, 0)
-        if ready is not None:
-            ready()
         for pair in range(PAIRS):
             top = jnp.max(tops[pair], axis=1, keepdims=True)
             top = jnp.broadcast_to(top, (2 * TOKENS, LANES))
@@ -123,11 +124,14 @@
                 totals[pair] = jnp.zeros((2 * TOKENS, LANES), jnp.float32)
                 sums[pair] = jnp.zeros((2 * TOKENS, LANES), jnp.float32)
             else:
-                top = jnp.maximum(top, prior[pair])
+                stats = jnp.concatenate([prior[2 * pair], prior[2 * pair + 1]], axis=0)
+                old = jnp.broadcast_to(stats[:, :1], (2 * TOKENS, LANES))
+                top = jnp.maximum(top, old)
                 tops[pair] = top
-                factor = jnp.exp(prior[pair] - top)
-                totals[pair] = prior[PAIRS + pair] * factor
-                sums[pair] = prior[2 * PAIRS + pair] * factor
+                factor = jnp.exp(old - top)
+                totals[pair] = jnp.where(self.middle, stats * factor, 0.0)
+                known = prior[2 * PAIRS + pair]
+                sums[pair] = jnp.concatenate([known, known], axis=0) * factor
 
         def mix(turn, carry):
             _, place = step_of(turn)
@@ -149,12 +153,8 @@
         lax.fori_loop(0, count, mix, 0)
 
 
-def query_place(pair):
-    return 3 * PAIRS + pair // 2, slice(pair % 2 * TOKENS, (pair % 2 + 1) * TOKENS)
-
-
-def local_kernel(lengths_ref, place_ref, own, next_piece, far, last, *rest):
-    out, (kv, queries, scores, states, sems) = rest[0], rest[1:]
+def local_kernel(lengths_ref, place_ref, own, next_piece, far, last, out, *rest):
+    kv, queries, scores, state, packed, sems = rest
     attention = Attention(lengths_ref, place_ref)
     pieces = (own, next_piece, far, last)
     asks, copies = [], []
@@ -178,101 +178,103 @@
         copy.wait()
     stores = []
     for i, offset in enumerate((2, 1, 3, 0)):
-        if i >= 2:
-            stores[i - 2].wait()
         which = lax.rem(attention.y + offset, 4)
         start, stop = attention.steps_of(which)
         start, stop = jnp.maximum(start, 2), jnp.minimum(stop, 4)
-        state = states.at[i % 2]
         asked = [queries[offset, :, pair * LANES : (pair + 1) * LANES] for pair in range(PAIRS)]
-        for pair in range(PAIRS):
-            state[query_place(pair)] = asked[pair].astype(jnp.float32)
         attention.attend(
             which, asked, kv,
             lambda turn: (start + turn, start + turn - 2), stop - start,
             scores, state,
         )
-        stores.append(pltpu.make_async_copy(state, out.at[offset], sems.at[8 + i]))
+        if i >= 2:
+            stores[i - 2].wait()
+        tiles = packed.at[i % 2]
+        for pair in range(PAIRS):
+            total = jnp.sum(state[PAIRS + pair], axis=1, keepdims=True)
+            total = jnp.broadcast_to(total, (2 * TOKENS, LANES))
+            top, found = state[pair], state[2 * PAIRS + pair]
+            tiles[2 * pair] = jnp.where(attention.low, top[:TOKENS], total[:TOKENS])
+            tiles[2 * pair + 1] = jnp.where(attention.low, top[TOKENS:], total[TOKENS:])
+            tiles[2 * PAIRS + pair] = jnp.where(attention.low, found[:TOKENS], found[TOKENS:])
+            tiles[3 * PAIRS + pair] = asked[pair].astype(jnp.float32)
+        stores.append(pltpu.make_async_copy(tiles, out.at[offset], sems.at[8 + i]))
         stores[i].start()
     stores[2].wait()
     stores[3].wait()
 
 
-def project(mixed, weights_ref, store):
+def project(mixed, core, own_weights, other_weights, store):
     for tile in range(8):
         high, place = divmod(tile, 4)
-        both = jnp.concatenate([weights_ref[0, place, high], weights_ref[1, place, high]], axis=1)
-        store(tile * PAIR, jnp.dot(mixed, both, preferred_element_type=jnp.float32))
-
-
-PAIR = 2 * LANES
+        both = jnp.concatenate([own_weights[place, high], other_weights[place, high]], axis=1)
+        found = jnp.dot(mixed, both, preferred_element_type=jnp.float32)
+        start = tile * 2 * LANES
+        store(pl.multiple_of(start + core * LANES, LANES), found[:, :LANES])
+        store(pl.multiple_of(start + (1 - core) * LANES, LANES), found[:, LANES:])
 
 
 def rows_kernel(
-    offset, lengths_ref, place_ref, own_weights, other_weights,
-    own_before, rest_before, own_after, rest_after, prior_hbm, out_ref,
-    kv, prior, scores, state, weights, mixed, sems,
+    offsets, lengths_ref, place_ref, own_weights, other_weights, before, after, prior_hbm, *rest
 ):
-    core = place_ref[2]
-    fetches = [
-        pltpu.make_async_copy(own_weights, weights.at[core], sems.at[8]),
-        pltpu.make_async_copy(other_weights, weights.at[1 - core], sems.at[9]),
-    ]
+    outs, (kv, priors, scores, state, mixed, sems) = rest[: len(offsets)], rest[len(offsets) :]
     attention = Attention(lengths_ref, place_ref)
-    which = lax.rem(attention.y + offset, 4)
-    start, stop = attention.steps_of(which)
-    ahead = jnp.maximum(2 - start, 0)
-    behind = jnp.maximum(stop - 4, 0)
+    whiches, aheads, behinds, recalls = [], [], [], []
+    for i, offset in enumerate(offsets):
+        which = lax.rem(attention.y + offset, 4)
+        start, stop = attention.steps_of(which)
+        whiches.append(which)
+        aheads.append(jnp.maximum(2 - start, 0))
+        behinds.append(jnp.maximum(stop - 4, 0))
+        recalls.append(pltpu.make_async_copy(prior_hbm.at[offset], priors.at[i], sems.at[8 + i]))
+    recalls[0].start()
+    most_ahead = functools.reduce(jnp.maximum, aheads)
+    most_behind = functools.reduce(jnp.maximum, behinds)
     copies = []
-    for side, (first, others) in enumerate(((own_before, rest_before), (own_after, rest_after))):
+    for side, source in enumerate((before, after)):
         for turn in range(4):
             slot = lax.rem(attention.y + turn, 4)
             half = lax.div(slot, 2)
             copy = pltpu.make_async_copy(
-                others.at[pl.ds((turn - 1) * TOKENS, TOKENS)] if turn else first,
+                source.at[pl.ds(turn * TOKENS, TOKENS)],
                 kv.at[pl.ds(pl.multiple_of((4 * side + slot) * TOKENS, TOKENS), TOKENS)],
                 sems.at[4 * side + turn],
             )
-            copies.append((half < behind if side else half >= 2 - ahead, copy))
-    asked, rest = pl.ds(3 * PAIRS, 2), pl.ds(0, 3 * PAIRS)
-    ask = pltpu.make_async_copy(prior_hbm.at[offset, asked], prior.at[asked], sems.at[10])
-    recall = pltpu.make_async_copy(prior_hbm.at[offset, rest], prior.at[rest], sems.at[11])
-    ask.start()
+            copies.append((half < most_behind if side else half >= 2 - most_ahead, copy))
     for wanted, copy in copies:
         @pl.when(wanted)
         def _():
             copy.start()
-    recall.start()
-    for fetch in fetches:
-        fetch.start()
-    ask.wait()
+    for recall in recalls[1:]:
+        recall.start()
     for wanted, copy in copies:
         @pl.when(wanted)
         def _():
             copy.wait()
-
-    def step_of(turn):
-        early = turn < ahead
-        step = jnp.where(early, 2 - ahead + turn, 4 + turn - ahead)
-        return step, jnp.where(early, step, step - 2)
-
-    queries = [prior[query_place(pair)].astype(jnp.bfloat16) for pair in range(PAIRS)]
-    attention.attend(
-        which, queries, kv, step_of, ahead + behind, scores, state, prior, recall.wait
-    )
-    for pair in range(PAIRS):
-        row_total = jnp.sum(state[PAIRS + pair], axis=1, keepdims=True)
-        found = state[2 * PAIRS + pair] / row_total
-        mixed[:, pair * LANES : (pair + 1) * LANES] = jnp.where(
-            attention.low, found[:TOKENS], found[TOKENS:]
-        ).astype(jnp.bfloat16)
-    for fetch in fetches:
-        fetch.wait()
+    for i, which in enumerate(whiches):
+        ahead, behind, prior = aheads[i], behinds[i], priors.at[i]
+        recalls[i].wait()
+
+        def step_of(turn):
+            early = turn < ahead
+            step = jnp.where(early, 2 - ahead + turn, 4 + turn - ahead)
+            return step, jnp.where(early, step, step - 2)
+
+        queries = [prior[3 * PAIRS + pair].astype(jnp.bfloat16) for pair in range(PAIRS)]
+        attention.attend(which, queries, kv, step_of, ahead + behind, scores, state, prior)
+        for pair in range(PAIRS):
+            row_total = jnp.sum(state[PAIRS + pair], axis=1, keepdims=True)
+            found = state[2 * PAIRS + pair] / row_total
+            mixed[i * TOKENS : (i + 1) * TOKENS, pair * LANES : (pair + 1) * LANES] = jnp.where(
+                attention.low, found[:TOKENS], found[TOKENS:]
+            ).astype(jnp.bfloat16)
 
     def store(start, value):
-        out_ref[:, start : start + PAIR] = value.astype(out_ref.dtype)
-
-    project(mixed[...], weights, store)
+        for i, out_ref in enumerate(outs):
+            part = value[i * TOKENS : (i + 1) * TOKENS]
+            out_ref[:, pl.ds(start, LANES)] = part.astype(out_ref.dtype)
+
+    project(mixed[...], place_ref[2], own_weights, other_weights, store)
 
 
 def finish_kernel(own_ref, one_ref, two_ref, three_ref, resid_ref, earlier_ref, out_ref):
@@ -289,21 +291,14 @@
 vmem = pl.BlockSpec(memory_space=pltpu.VMEM)
 smem = pl.BlockSpec(memory_space=pltpu.SMEM)
 anywhere = pl.BlockSpec(memory_space=pl.ANY)
-running = (3 * PAIRS + 2, 2 * TOKENS, LANES)
+running = (3 * PAIRS, 2 * TOKENS, LANES)
+handed = (4 * PAIRS, TOKENS, LANES)
 local_scratch = [
     pltpu.VMEM((ROW, 2 * WIDTH), jnp.bfloat16),
     pltpu.VMEM((4, TOKENS, WIDTH), jnp.bfloat16),
     pltpu.VMEM((2, PAIRS, 2 * TOKENS, CHUNK), jnp.float32),
-    pltpu.VMEM((2,) + running, jnp.float32),
-    pltpu.SemaphoreType.DMA((12,)),
-]
-rows_scratch = [
-    pltpu.VMEM((2 * ROW, 2 * WIDTH), jnp.bfloat16),
     pltpu.VMEM(running, jnp.float32),
-    pltpu.VMEM((4, PAIRS, 2 * TOKENS, CHUNK), jnp.float32),
-    pltpu.VMEM(running, jnp.float32),
-    pltpu.VMEM((2, 4, 2, ROW, LANES), jnp.bfloat16),
-    pltpu.VMEM((TOKENS, WIDTH), jnp.bfloat16),
+    pltpu.VMEM((2,) + handed, jnp.float32),
     pltpu.SemaphoreType.DMA((12,)),
 ]
 
@@ -347,11 +342,9 @@
     for turn in (1, 2, 3):
         pieces.append(shift(packed[turn], -turn))
     ring = 2 * lax.axis_size("z")
-    own_after = shift(packed[0][:, WIDTH:], -1, ("h", "z"), ring)
-    own_before = shift(packed[0][:, WIDTH:], 1, ("h", "z"), ring)
-    keys = jnp.concatenate([piece[:, WIDTH:] for piece in pieces[1:]], axis=0)
-    rest_after = shift(keys, -1, ("h", "z"), ring)
-    rest_before = shift(keys, 1, ("h", "z"), ring)
+    keys = jnp.concatenate([piece[:, WIDTH:] for piece in pieces], axis=0)
+    after = shift(keys, -1, ("h", "z"), ring)
+    before = shift(keys, 1, ("h", "z"), ring)
 
     ring_weights = lax.all_to_all(
         jnp.broadcast_to(teacher_new[None], (16,) + teacher_new.shape), ("h", "z"), 0, 0, tiled=True
@@ -364,35 +357,41 @@
 
     local = pl.pallas_call(
         local_kernel,
-        out_shape=array(4, *running, dtype=jnp.float32),
+        out_shape=array(4, *handed, dtype=jnp.float32),
         in_specs=[smem, smem] + [anywhere] * 4,
         out_specs=anywhere,
         scratch_shapes=local_scratch,
-        compiler_params=limit(16),
+        compiler_params=limit(LOCAL_LIMIT),
         cost_estimate=cost(1 << 30, 8 << 20, 2 << 20),
         name="local",
     )(lengths, place, *pieces)
 
-    def rows_of(offset, dtype):
+    def rows_of(offsets, dtype):
+        count = len(offsets)
         return pl.pallas_call(
-            functools.partial(rows_kernel, offset),
-            out_shape=array(TOKENS, D, dtype=dtype),
-            in_specs=[smem, smem] + [anywhere] * 7,
-            out_specs=vmem,
-            scratch_shapes=rows_scratch,
-            compiler_params=limit(48),
-            cost_estimate=cost(1 << 29, 4 << 20, 1 << 20),
+            functools.partial(rows_kernel, offsets),
+            out_shape=(array(TOKENS, D, dtype=dtype),) * count,
+            in_specs=[smem, smem, vmem, vmem] + [anywhere] * 3,
+            out_specs=(vmem,) * count,
+            scratch_shapes=[
+                pltpu.VMEM((2 * ROW, 2 * WIDTH), jnp.bfloat16),
+                pltpu.VMEM((count,) + handed, jnp.float32),
+                pltpu.VMEM((4, PAIRS, 2 * TOKENS, CHUNK), jnp.float32),
+                pltpu.VMEM(running, jnp.float32),
+                pltpu.VMEM((count * TOKENS, WIDTH), jnp.bfloat16),
+                pltpu.SemaphoreType.DMA((10,)),
+            ],
+            compiler_params=limit(ROWS_LIMIT),
+            cost_estimate=cost(count << 29, 4 << 20, count << 20),
             name="rows",
-        )(
-            lengths, place, own_weights, other_weights,
-            own_before, rest_before, own_after, rest_after, local,
-        )
-
-    arrived = []
-    for offset in (2, 1, 3):
-        part = rows_of(offset, jnp.bfloat16)
-        arrived.append(shift(part, offset))
-    own = rows_of(0, jnp.float32)
+        )(lengths, place, own_weights, other_weights, before, after, local)
+
+    (far,) = rows_of((2,), jnp.bfloat16)
+    far = shift(far, 2)
+    up, down = rows_of((1, 3), jnp.bfloat16)
+    up = shift(up, 1)
+    down = shift(down, 3)
+    (own,) = rows_of((0,), jnp.float32)
     rows = pl.BlockSpec((32, D), lambda i: (i, 0))
     targets = pl.pallas_call(
         finish_kernel,
@@ -403,7 +402,7 @@
         compiler_params=limit(12),
         cost_estimate=cost(1 << 22, 5 << 20),
         name="finish",
-    )(own, *arrived, resid[0], earlier[0])
+    )(own, far, up, down, resid[0], earlier[0])
     return (targets[None], teacher_new)
 
 

time: 134 us -> 139 us (1.037)
  the two profiles are of different devices: /device:TPU:1 before, /device:TPU:56 now
where the time goes in v4:
time: 139 us; the launch traced here: 138 us
  waiting for transfers between devices  38.6 us (28%)
  blocking collectives  33.1 us (24%)
  starting transfers between devices  32.8 us (24%)
  Pallas kernels  28.9 us (21%)
  local copies, waits for them, and re-layouts  2.03 us (1%)
  other arithmetic  1.88 us (1%)
    ppermute x9, waiting for transfers between devices, shift(): lax.ppermute(value, axis, [(i, (i + amount) % size) for i in range(size)])  38.6 us
    all_to_all x1, blocking collectives, block(): lax.all_to_all(jnp.broadcast_to(teacher_new[None], (16,) + teacher_new.sh...  33.1 us
    ppermute x9, starting transfers between devices, shift(): lax.ppermute(value, axis, [(i, (i + amount) % size) for i in range(size)])  28.5 us
    pallas_call x3, Pallas kernels, rows_of(): pl.pallas_call(functools.partial(rows_kernel, offsets), out_shape=(array(...  14.5 us
    pallas_call x1, Pallas kernels, block(): pl.pallas_call(local_kernel, out_shape=array(4, *handed, dtype=jnp.float3...  9.79 us
    all_to_all x1, starting transfers between devices, block(): lax.all_to_all(jnp.broadcast_to(ring_weights[None], (4,) + ring_weights.s...  4.29 us
  transfers between devices with their start and end apart: 10, of which 6 were waited for; matrix products, arithmetic and copies ran while one was open for 1% of the time, Pallas kernels for 14%

profile of v4, /device:TPU:56, one launch (start us, length us, event | category | flops | bytes accessed | tf_op | source)
XLA Modules:
  0.0 138.1 jit_solution(4673282099806372589)
XLA Ops:
  0.6 0.7 add_convert_fusion
  1.4 0.0 copy-start.10
  1.4 0.0 copy-start
  1.5 33.1 %all_to_all.10 = bf16[16,64,128]{2,1,0:T(8,128)(2,1)S(1)} all-to-all(bf16[16,64,128]{2,1,0:T(8,128)(2,1)S(1)} %broadcast_in_dim.16), channel_id=1, replica_groups=mesh['h'=2,'x'=4,'c'=2,'z'=8,'y'=4] {'h','z'}, dimensions={0} | all-to-all | bytes 524288 | tf_op jit(solution)/shard_map/all_to_all | solution.py:349
  34.5 1.1 broadcast_in_dim.18
  35.6 4.3 %all-to-all-start.1 = ((bf16[4,2,512,128]{3,2,1,0:T(8,128)(2,1)}), bf16[4,2,512,128]{3,2,1,0:T(8,128)(2,1)S(1)}, u32[]{:S(2)}, u32[]{:S(2)}) async-start(bf16[4,2,512,128]{3,2,1,0:T(8,128)(2,1)} %broadcast_in_dim.18), calls=%async_computation.1 | async-start | bytes 2097152 | tf_op jit(solution)/shard_map/all_to_all | solution.py:353
  39.9 0.1 pad_add_fusion.place_ref
  40.0 2.2 %pack.1 = (bf16[128,1536]{1,0:T(8,128)(2,1)S(1)}, bf16[128,1536]{1,0:T(8,128)(2,1)S(1)}, bf16[128,1536]{1,0:T(8,128)(2,1)S(1)}, bf16[128,1536]{1,0:T(8,128)(2,1)S(1)}) custom-call(s32[3]{0:T(128)S(1)} %pad_add_fusion.place_ref, bf16[128,6144]{1,0:T(8,128)(2,1)S(1)} %bitcast.8), custom_call_target="tpu_custom_call" | custom-call | bytes 3145728 | tf_op jit(solution)/shard_map/pack/pallas_call | solution.py:339
  42.2 2.7 %collective-permute-start.1 = (bf16[128,1536]{1,0:T(8,128)(2,1)S(1)}, bf16[128,1536]{1,0:T(8,128)(2,1)S(1)}, u32[]{:S(2)}, u32[]{:S(2)}) collective-permute-start(bf16[128,1536]{1,0:T(8,128)(2,1)S(1)} %get-tuple-element.9), channel_id=1, source_target_pairs={{0,3},{1,0},{2,1},{3,2},{4,7},{5,4},{6,5},{7,6},{8,11},{9,8},{10,9... | collective-permute-start | bytes 1179656 | tf_op jit(solution)/shard_map/ppermute | solution.py:319
  44.9 2.8 %collective-permute-start.2 = (bf16[128,1536]{1,0:T(8,128)(2,1)S(1)}, bf16[128,1536]{1,0:T(8,128)(2,1)S(1)}, u32[]{:S(2)}, u32[]{:S(2)}) collective-permute-start(bf16[128,1536]{1,0:T(8,128)(2,1)S(1)} %get-tuple-element.10), channel_id=1, source_target_pairs={{0,2},{1,3},{2,0},{3,1},{4,6},{5,7},{6,4},{7,5},{8,10},{9,11},{10,... | collective-permute-start | bytes 1179656 | tf_op jit(solution)/shard_map/ppermute | solution.py:319
  47.7 4.1 %collective-permute-start.3 = (bf16[128,1536]{1,0:T(8,128)(2,1)S(1)}, bf16[128,1536]{1,0:T(8,128)(2,1)S(1)}, u32[]{:S(2)}, u32[]{:S(2)}) collective-permute-start(bf16[128,1536]{1,0:T(8,128)(2,1)S(1)} %get-tuple-element.11), channel_id=1, source_target_pairs={{0,1},{1,2},{2,3},{3,0},{4,5},{5,6},{6,7},{7,4},{8,9},{9,10},{10,1... | collective-permute-start | bytes 1179656 | tf_op jit(solution)/shard_map/ppermute | solution.py:319
  51.8 11.7 %collective-permute-done.1.next_piece = bf16[128,1536]{1,0:T(8,128)(2,1)S(1)} collective-permute-done((bf16[128,1536]{1,0:T(8,128)(2,1)S(1)}, bf16[128,1536]{1,0:T(8,128)(2,1)S(1)}, u32[]{:S(2)}, u32[]{:S(2)}) %collective-permute-start.1) | collective-permute-done | bytes 393248 | tf_op jit(solution)/shard_map/ppermute | solution.py:319
  63.6 2.5 %collective-permute-done.3.last = bf16[128,1536]{1,0:T(8,128)(2,1)S(1)} collective-permute-done((bf16[128,1536]{1,0:T(8,128)(2,1)S(1)}, bf16[128,1536]{1,0:T(8,128)(2,1)S(1)}, u32[]{:S(2)}, u32[]{:S(2)}) %collective-permute-start.3) | collective-permute-done | bytes 393248 | tf_op jit(solution)/shard_map/ppermute | solution.py:319
  66.0 0.8 copy-done.9
  66.8 1.1 pad_maximum_fusion
  67.9 2.0 %collective-permute-start.4 = (bf16[512,1024]{1,0:T(8,128)(2,1)}, bf16[512,1024]{1,0:T(8,128)(2,1)S(1)}, u32[]{:S(2)}, u32[]{:S(2)}) collective-permute-start(bf16[512,1024]{1,0:T(8,128)(2,1)} %pad_maximum_fusion), channel_id=1, source_target_pairs={{0,4},{4,8},{8,12},{12,16},{16,20},{20,24},{24,28},{28,256},{256,2... | collective-permute-start | bytes 3145736 | tf_op jit(solution)/shard_map/ppermute | solution.py:319
  69.9 3.9 %collective-permute-start.5 = (bf16[512,1024]{1,0:T(8,128)(2,1)}, bf16[512,1024]{1,0:T(8,128)(2,1)S(1)}, u32[]{:S(2)}, u32[]{:S(2)}) collective-permute-start(bf16[512,1024]{1,0:T(8,128)(2,1)} %pad_maximum_fusion), channel_id=1, source_target_pairs={{0,284},{4,0},{8,4},{12,8},{16,12},{20,16},{24,20},{28,24},{256,28... | collective-permute-start | bytes 3145736 | tf_op jit(solution)/shard_map/ppermute | solution.py:319
  73.9 1.9 %collective-permute-start = (bf16[4,2,512,128]{3,2,1,0:T(8,128)(2,1)S(1)}, bf16[4,2,512,128]{3,2,1,0:T(8,128)(2,1)S(1)}, u32[]{:S(2)}, u32[]{:S(2)}) collective-permute-start(bf16[4,2,512,128]{3,2,1,0:T(8,128)(2,1)S(1)} %all-to-all-done.1.own_weights), channel_id=1, source_target_pairs={{0,32},{32,0},{1,33},{33,1},{2,34},{34,2},{3,35},{35,3},{4,36},{36... | collective-permute-start | bytes 3145736 | tf_op jit(solution)/shard_map/ppermute | solution.py:319
  75.8 9.8 %local.1.prior_hbm = f32[4,16,128,128]{3,2,1,0:T(8,128)} custom-call(s32[1,12]{1,0:T(1,128)} %lengths_ref.7, s32[3]{0:T(128)} %copy-done.4, bf16[128,1536]{1,0:T(8,128)(2,1)} %copy-done.1, bf16[128,1536]{1,0:T(8,128)(2,1)} %copy-done.7, bf16[128,1536]{1,0:T(8,128)(2,1)} %copy-done.8, bf16[128,1536]{1,0:T(8,128)(2,1)} %copy-done.9), custom_call_target="tpu_custom_call" | custom-call | flops 1073741824 | bytes 8388608 | tf_op jit(solution)/shard_map/local/pallas_call | solution.py:358
  85.6 8.5 %collective-permute-done.4.before = bf16[512,1024]{1,0:T(8,128)(2,1)S(1)} collective-permute-done((bf16[512,1024]{1,0:T(8,128)(2,1)}, bf16[512,1024]{1,0:T(8,128)(2,1)S(1)}, u32[]{:S(2)}, u32[]{:S(2)}) %collective-permute-start.4) | collective-permute-done | bytes 1048608 | tf_op jit(solution)/shard_map/ppermute | solution.py:319
  94.1 2.4 %collective-permute-done.5.after = bf16[512,1024]{1,0:T(8,128)(2,1)S(1)} collective-permute-done((bf16[512,1024]{1,0:T(8,128)(2,1)}, bf16[512,1024]{1,0:T(8,128)(2,1)S(1)}, u32[]{:S(2)}, u32[]{:S(2)}) %collective-permute-start.5) | collective-permute-done | bytes 1048608 | tf_op jit(solution)/shard_map/ppermute | solution.py:319
  96.5 6.6 %rows.5 = (bf16[128,2048]{1,0:T(8,128)(2,1)S(1)}, bf16[128,2048]{1,0:T(8,128)(2,1)S(1)}) custom-call(s32[1,12]{1,0:T(1,128)S(1)} %copy-done.6, s32[3]{0:T(128)S(1)} %copy-done.5, bf16[4,2,512,128]{3,2,1,0:T(8,128)(2,1)S(1)} %all-to-all-done.1.own_weights, bf16[4,2,512,128]{3,2,1,0:T(8,128)(2,1)S(1)} %collective-permute-done.other_weights, ...), custom_call_target="tpu_custom_call" | custom-call | flops 1073741824 | bytes 4194304 | tf_op jit(solution)/shard_map/rows/pallas_call | solution.py:371
  103.1 5.0 %collective-permute-start.7 = (bf16[128,2048]{1,0:T(8,128)(2,1)S(1)}, bf16[128,2048]{1,0:T(8,128)(2,1)S(1)}, u32[]{:S(2)}, u32[]{:S(2)}) collective-permute-start(bf16[128,2048]{1,0:T(8,128)(2,1)S(1)} %get-tuple-element.12), channel_id=1, source_target_pairs={{0,1},{1,2},{2,3},{3,0},{4,5},{5,6},{6,7},{7,4},{8,9},{9,10},{10,1... | collective-permute-start | bytes 1572872 | tf_op jit(solution)/shard_map/ppermute | solution.py:319
  108.1 1.9 %collective-permute-start.8 = (bf16[128,2048]{1,0:T(8,128)(2,1)S(1)}, bf16[128,2048]{1,0:T(8,128)(2,1)S(1)}, u32[]{:S(2)}, u32[]{:S(2)}) collective-permute-start(bf16[128,2048]{1,0:T(8,128)(2,1)S(1)} %get-tuple-element.13), channel_id=1, source_target_pairs={{0,3},{1,0},{2,1},{3,2},{4,7},{5,4},{6,5},{7,6},{8,11},{9,8},{10,9... | collective-permute-start | bytes 1572872 | tf_op jit(solution)/shard_map/ppermute | solution.py:319
  110.0 3.7 %rows.4 = bf16[128,2048]{1,0:T(8,128)(2,1)S(1)} custom-call(s32[1,12]{1,0:T(1,128)S(1)} %copy-done.6, s32[3]{0:T(128)S(1)} %copy-done.5, bf16[4,2,512,128]{3,2,1,0:T(8,128)(2,1)S(1)} %all-to-all-done.1.own_weights, bf16[4,2,512,128]{3,2,1,0:T(8,128)(2,1)S(1)} %collective-permute-done.other_weights, bf16[512,1024]{1,0:T(8,128)(2,1)S(1)} %collective-permute-done.4.before, ...), custom_call_target="tpu_custom_call" | custom-call | flops 536870912 | bytes 4194304 | tf_op jit(solution)/shard_map/rows/pallas_call | solution.py:371
  113.7 0.0 copy-start.2
  113.7 0.0 copy-start.3
  113.7 4.1 %collective-permute-start.6 = (bf16[128,2048]{1,0:T(8,128)(2,1)S(1)}, bf16[128,2048]{1,0:T(8,128)(2,1)S(1)}, u32[]{:S(2)}, u32[]{:S(2)}) collective-permute-start(bf16[128,2048]{1,0:T(8,128)(2,1)S(1)} %rows.4), channel_id=1, source_target_pairs={{0,2},{1,3},{2,0},{3,1},{4,6},{5,7},{6,4},{7,5},{8,10},{9,11},{10,... | collective-permute-start | bytes 1572872 | tf_op jit(solution)/shard_map/ppermute | solution.py:319
  117.9 4.3 %rows.3.own_ref = f32[128,2048]{1,0:T(8,128)S(1)} custom-call(s32[1,12]{1,0:T(1,128)S(1)} %copy-done.6, s32[3]{0:T(128)S(1)} %copy-done.5, bf16[4,2,512,128]{3,2,1,0:T(8,128)(2,1)S(1)} %all-to-all-done.1.own_weights, bf16[4,2,512,128]{3,2,1,0:T(8,128)(2,1)S(1)} %collective-permute-done.other_weights, bf16[512,1024]{1,0:T(8,128)(2,1)S(1)} %collective-permute-done.4.before, ...), custom_call_target="tpu_custom_call" | custom-call | flops 536870912 | bytes 4194304 | tf_op jit(solution)/shard_map/rows/pallas_call | solution.py:371
  122.2 8.3 %collective-permute-done.7.two_ref = bf16[128,2048]{1,0:T(8,128)(2,1)S(1)} collective-permute-done((bf16[128,2048]{1,0:T(8,128)(2,1)S(1)}, bf16[128,2048]{1,0:T(8,128)(2,1)S(1)}, u32[]{:S(2)}, u32[]{:S(2)}) %collective-permute-start.7) | collective-permute-done | bytes 524320 | tf_op jit(solution)/shard_map/ppermute | solution.py:319
  130.5 5.3 %collective-permute-done.8.three_ref = bf16[128,2048]{1,0:T(8,128)(2,1)S(1)} collective-permute-done((bf16[128,2048]{1,0:T(8,128)(2,1)S(1)}, bf16[128,2048]{1,0:T(8,128)(2,1)S(1)}, u32[]{:S(2)}, u32[]{:S(2)}) %collective-permute-start.8) | collective-permute-done | bytes 524320 | tf_op jit(solution)/shard_map/ppermute | solution.py:319
  135.8 2.3 %finish.1 = f32[128,2048]{1,0:T(8,128)} custom-call(f32[128,2048]{1,0:T(8,128)S(1)} %rows.3.own_ref, bf16[128,2048]{1,0:T(8,128)(2,1)S(1)} %collective-permute-done.6.one_ref, bf16[128,2048]{1,0:T(8,128)(2,1)S(1)} %collective-permute-done.7.two_ref, bf16[128,2048]{1,0:T(8,128)(2,1)S(1)} %collective-permute-done.8.three_ref, bf16[128,2048]{1,0:T(8,128)(2,1)S(1)} %bitcast.10, ...), custom_call_target="tpu_custom_call" | custom-call | flops 4194304 | bytes 5242880 | tf_op jit(solution)/shard_map/finish/pallas_call | solution.py:396
  (26 shorter events, 0.2 us)
Async XLA Ops:
  1.4 33.1 %copy-start.10 = (bf16[64,128]{1,0:T(8,128)(2,1)}, bf16[64,128]{1,0:T(8,128)(2,1)S(1)}, u32[]{:S(2)}) copy-start(bf16[64,128]{1,0:T(8,128)(2,1)S(1)} %add_convert_fusion) | copy-start | bytes 49156
  1.4 38.6 %copy-start = (bf16[1,128,6144]{2,1,0:T(8,128)(2,1)S(1)}, bf16[1,128,6144]{2,1,0:T(8,128)(2,1)}, u32[]{:S(2)}) copy-start(bf16[1,128,6144]{2,1,0:T(8,128)(2,1)} %param.6) | copy-start | bytes 4718596
  35.6 38.3 %all-to-all-start.1 = ((bf16[4,2,512,128]{3,2,1,0:T(8,128)(2,1)}), bf16[4,2,512,128]{3,2,1,0:T(8,128)(2,1)S(1)}, u32[]{:S(2)}, u32[]{:S(2)}) async-start(bf16[4,2,512,128]{3,2,1,0:T(8,128)(2,1)} %broadcast_in_dim.18), calls=%async_computation.1 | async-start | bytes 2097152 | tf_op jit(solution)/shard_map/all_to_all | solution.py:353
  40.0 27.9 %copy-start.4 = (s32[3]{0:T(128)}, s32[3]{0:T(128)S(1)}, u32[]{:S(2)}) copy-start(s32[3]{0:T(128)S(1)} %pad_add_fusion.place_ref) | copy-start | bytes 40
  42.2 25.7 %copy-start.1 = (bf16[128,1536]{1,0:T(8,128)(2,1)}, bf16[128,1536]{1,0:T(8,128)(2,1)S(1)}, u32[]{:S(2)}) copy-start(bf16[128,1536]{1,0:T(8,128)(2,1)S(1)} %get-tuple-element.8.own) | copy-start | bytes 1179652
  42.2 21.3 %collective-permute-start.1 = (bf16[128,1536]{1,0:T(8,128)(2,1)S(1)}, bf16[128,1536]{1,0:T(8,128)(2,1)S(1)}, u32[]{:S(2)}, u32[]{:S(2)}) collective-permute-start(bf16[128,1536]{1,0:T(8,128)(2,1)S(1)} %get-tuple-element.9), channel_id=1, source_target_pairs={{0,3},{1,0},{2,1},{3,2},{4,7},{5,4},{6,5},{7,6},{8,11},{9,8},{10,9... | collective-permute-start | bytes 1179656 | tf_op jit(solution)/shard_map/ppermute | solution.py:319
  44.9 18.7 %collective-permute-start.2 = (bf16[128,1536]{1,0:T(8,128)(2,1)S(1)}, bf16[128,1536]{1,0:T(8,128)(2,1)S(1)}, u32[]{:S(2)}, u32[]{:S(2)}) collective-permute-start(bf16[128,1536]{1,0:T(8,128)(2,1)S(1)} %get-tuple-element.10), channel_id=1, source_target_pairs={{0,2},{1,3},{2,0},{3,1},{4,6},{5,7},{6,4},{7,5},{8,10},{9,11},{10,... | collective-permute-start | bytes 1179656 | tf_op jit(solution)/shard_map/ppermute | solution.py:319
  47.7 18.3 %collective-permute-start.3 = (bf16[128,1536]{1,0:T(8,128)(2,1)S(1)}, bf16[128,1536]{1,0:T(8,128)(2,1)S(1)}, u32[]{:S(2)}, u32[]{:S(2)}) collective-permute-start(bf16[128,1536]{1,0:T(8,128)(2,1)S(1)} %get-tuple-element.11), channel_id=1, source_target_pairs={{0,1},{1,2},{2,3},{3,0},{4,5},{5,6},{6,7},{7,4},{8,9},{9,10},{10,1... | collective-permute-start | bytes 1179656 | tf_op jit(solution)/shard_map/ppermute | solution.py:319
  63.5 12.3 %copy-start.7 = (bf16[128,1536]{1,0:T(8,128)(2,1)}, bf16[128,1536]{1,0:T(8,128)(2,1)S(1)}, u32[]{:S(2)}) copy-start(bf16[128,1536]{1,0:T(8,128)(2,1)S(1)} %collective-permute-done.1.next_piece) | copy-start | bytes 1179652
  63.5 2.5 %copy-start.8 = (bf16[128,1536]{1,0:T(8,128)(2,1)}, bf16[128,1536]{1,0:T(8,128)(2,1)S(1)}, u32[]{:S(2)}) copy-start(bf16[128,1536]{1,0:T(8,128)(2,1)S(1)} %collective-permute-done.2.far) | copy-start | bytes 1179652
  66.0 0.8 copy-start.9
  67.9 28.6 %copy-start.6 = (s32[1,12]{1,0:T(1,128)S(1)}, s32[1,12]{1,0:T(1,128)}, u32[]{:S(2)}) copy-start(s32[1,12]{1,0:T(1,128)} %lengths_ref.7) | copy-start | bytes 148
  67.9 26.2 %collective-permute-start.4 = (bf16[512,1024]{1,0:T(8,128)(2,1)}, bf16[512,1024]{1,0:T(8,128)(2,1)S(1)}, u32[]{:S(2)}, u32[]{:S(2)}) collective-permute-start(bf16[512,1024]{1,0:T(8,128)(2,1)} %pad_maximum_fusion), channel_id=1, source_target_pairs={{0,4},{4,8},{8,12},{12,16},{16,20},{20,24},{24,28},{28,256},{256,2... | collective-permute-start | bytes 3145736 | tf_op jit(solution)/shard_map/ppermute | solution.py:319
  69.9 26.6 %copy-start.5 = (s32[3]{0:T(128)S(1)}, s32[3]{0:T(128)}, u32[]{:S(2)}) copy-start(s32[3]{0:T(128)} %copy-done.4) | copy-start | bytes 40
  69.9 26.6 %collective-permute-start.5 = (bf16[512,1024]{1,0:T(8,128)(2,1)}, bf16[512,1024]{1,0:T(8,128)(2,1)S(1)}, u32[]{:S(2)}, u32[]{:S(2)}) collective-permute-start(bf16[512,1024]{1,0:T(8,128)(2,1)} %pad_maximum_fusion), channel_id=1, source_target_pairs={{0,284},{4,0},{8,4},{12,8},{16,12},{20,16},{24,20},{28,24},{256,28... | collective-permute-start | bytes 3145736 | tf_op jit(solution)/shard_map/ppermute | solution.py:319
  73.9 22.6 %collective-permute-start = (bf16[4,2,512,128]{3,2,1,0:T(8,128)(2,1)S(1)}, bf16[4,2,512,128]{3,2,1,0:T(8,128)(2,1)S(1)}, u32[]{:S(2)}, u32[]{:S(2)}) collective-permute-start(bf16[4,2,512,128]{3,2,1,0:T(8,128)(2,1)S(1)} %all-to-all-done.1.own_weights), channel_id=1, source_target_pairs={{0,32},{32,0},{1,33},{33,1},{2,34},{34,2},{3,35},{35,3},{4,36},{36... | collective-permute-start | bytes 3145736 | tf_op jit(solution)/shard_map/ppermute | solution.py:319
  103.1 27.4 %collective-permute-start.7 = (bf16[128,2048]{1,0:T(8,128)(2,1)S(1)}, bf16[128,2048]{1,0:T(8,128)(2,1)S(1)}, u32[]{:S(2)}, u32[]{:S(2)}) collective-permute-start(bf16[128,2048]{1,0:T(8,128)(2,1)S(1)} %get-tuple-element.12), channel_id=1, source_target_pairs={{0,1},{1,2},{2,3},{3,0},{4,5},{5,6},{6,7},{7,4},{8,9},{9,10},{10,1... | collective-permute-start | bytes 1572872 | tf_op jit(solution)/shard_map/ppermute | solution.py:319
  108.1 27.7 %collective-permute-start.8 = (bf16[128,2048]{1,0:T(8,128)(2,1)S(1)}, bf16[128,2048]{1,0:T(8,128)(2,1)S(1)}, u32[]{:S(2)}, u32[]{:S(2)}) collective-permute-start(bf16[128,2048]{1,0:T(8,128)(2,1)S(1)} %get-tuple-element.13), channel_id=1, source_target_pairs={{0,3},{1,0},{2,1},{3,2},{4,7},{5,4},{6,5},{7,6},{8,11},{9,8},{10,9... | collective-permute-start | bytes 1572872 | tf_op jit(solution)/shard_map/ppermute | solution.py:319
  113.7 22.1 %copy-start.2 = (f32[1,128,2048]{2,1,0:T(8,128)S(1)}, f32[1,128,2048]{2,1,0:T(8,128)}, u32[]{:S(2)}) copy-start(f32[1,128,2048]{2,1,0:T(8,128)} %param.8) | copy-start | bytes 3145732
  113.7 22.1 %copy-start.3 = (bf16[1,128,2048]{2,1,0:T(8,128)(2,1)S(1)}, bf16[1,128,2048]{2,1,0:T(8,128)(2,1)}, u32[]{:S(2)}) copy-start(bf16[1,128,2048]{2,1,0:T(8,128)(2,1)} %param.7) | copy-start | bytes 1572868
  113.7 22.0 %collective-permute-start.6 = (bf16[128,2048]{1,0:T(8,128)(2,1)S(1)}, bf16[128,2048]{1,0:T(8,128)(2,1)S(1)}, u32[]{:S(2)}, u32[]{:S(2)}) collective-permute-start(bf16[128,2048]{1,0:T(8,128)(2,1)S(1)} %rows.4), channel_id=1, source_target_pairs={{0,2},{1,3},{2,0},{3,1},{4,6},{5,7},{6,4},{7,5},{8,10},{9,11},{10,... | collective-permute-start | bytes 1572872 | tf_op jit(solution)/shard_map/ppermute | solution.py:319

commit v5 on v4

--- a/solution.py
+++ b/solution.py
@@ -19,7 +19,7 @@
 CHUNK = 256
 PAIRS = WIDTH // LANES
 LOCAL_LIMIT = 58
-ROWS_LIMIT = 48
+ROWS_LIMIT = 24
 PACKED = 32
 
 ema_decay = 0.9
@@ -153,8 +153,8 @@
         lax.fori_loop(0, count, mix, 0)
 
 
-def local_kernel(lengths_ref, place_ref, own, next_piece, far, last, out, *rest):
-    kv, queries, scores, state, packed, sems = rest
+def local_kernel(lengths_ref, place_ref, own, next_piece, far, last, *rest):
+    outs, (kv, queries, scores, state, packed, sems) = rest[:4], rest[4:]
     attention = Attention(lengths_ref, place_ref)
     pieces = (own, next_piece, far, last)
     asks, copies = [], []
@@ -198,7 +198,7 @@
             tiles[2 * pair + 1] = jnp.where(attention.low, top[TOKENS:], total[TOKENS:])
             tiles[2 * PAIRS + pair] = jnp.where(attention.low, found[:TOKENS], found[TOKENS:])
             tiles[3 * PAIRS + pair] = asked[pair].astype(jnp.float32)
-        stores.append(pltpu.make_async_copy(tiles, out.at[offset], sems.at[8 + i]))
+        stores.append(pltpu.make_async_copy(tiles, outs[offset], sems.at[8 + i]))
         stores[i].start()
     stores[2].wait()
     stores[3].wait()
@@ -214,20 +214,15 @@
         store(pl.multiple_of(start + (1 - core) * LANES, LANES), found[:, LANES:])
 
 
-def rows_kernel(
-    offsets, lengths_ref, place_ref, own_weights, other_weights, before, after, prior_hbm, *rest
-):
-    outs, (kv, priors, scores, state, mixed, sems) = rest[: len(offsets)], rest[len(offsets) :]
+def attend_rows(offsets, lengths_ref, place_ref, before, after, priors, kv, scores, state, mixed, sems):
     attention = Attention(lengths_ref, place_ref)
-    whiches, aheads, behinds, recalls = [], [], [], []
-    for i, offset in enumerate(offsets):
+    whiches, aheads, behinds = [], [], []
+    for offset in offsets:
         which = lax.rem(attention.y + offset, 4)
         start, stop = attention.steps_of(which)
         whiches.append(which)
         aheads.append(jnp.maximum(2 - start, 0))
         behinds.append(jnp.maximum(stop - 4, 0))
-        recalls.append(pltpu.make_async_copy(prior_hbm.at[offset], priors.at[i], sems.at[8 + i]))
-    recalls[0].start()
     most_ahead = functools.reduce(jnp.maximum, aheads)
     most_behind = functools.reduce(jnp.maximum, behinds)
     copies = []
@@ -245,15 +240,12 @@
         @pl.when(wanted)
         def _():
             copy.start()
-    for recall in recalls[1:]:
-        recall.start()
     for wanted, copy in copies:
         @pl.when(wanted)
         def _():
             copy.wait()
     for i, which in enumerate(whiches):
-        ahead, behind, prior = aheads[i], behinds[i], priors.at[i]
-        recalls[i].wait()
+        ahead, behind, prior = aheads[i], behinds[i], priors[i]
 
         def step_of(turn):
             early = turn < ahead
@@ -268,6 +260,33 @@
             mixed[i * TOKENS : (i + 1) * TOKENS, pair * LANES : (pair + 1) * LANES] = jnp.where(
                 attention.low, found[:TOKENS], found[TOKENS:]
             ).astype(jnp.bfloat16)
+
+
+def attend_kernel(offsets, lengths_ref, place_ref, before, after, *rest):
+    count = len(offsets)
+    priors, (mixed, *scratch) = rest[:count], rest[count:]
+    kv, scores, state, sems = scratch
+    attend_rows(
+        offsets, lengths_ref, place_ref, before, after, priors, kv, scores, state, mixed, sems
+    )
+
+
+def project_kernel(place_ref, own_weights, other_weights, mixed, out_ref):
+    def store(start, value):
+        out_ref[:, pl.ds(start, LANES)] = value.astype(out_ref.dtype)
+
+    project(mixed[...], place_ref[2], own_weights, other_weights, store)
+
+
+def rows_kernel(
+    offsets, lengths_ref, place_ref, own_weights, other_weights, before, after, *rest
+):
+    count = len(offsets)
+    priors, outs, scratch = rest[:count], rest[count : 2 * count], rest[2 * count :]
+    kv, scores, state, sems, mixed = scratch
+    attend_rows(
+        offsets, lengths_ref, place_ref, before, after, priors, kv, scores, state, mixed, sems
+    )
 
     def store(start, value):
         for i, out_ref in enumerate(outs):
@@ -301,6 +320,12 @@
     pltpu.VMEM((2,) + handed, jnp.float32),
     pltpu.SemaphoreType.DMA((12,)),
 ]
+rows_scratch = [
+    pltpu.VMEM((2 * ROW, 2 * WIDTH), jnp.bfloat16),
+    pltpu.VMEM((4, PAIRS, 2 * TOKENS, CHUNK), jnp.float32),
+    pltpu.VMEM(running, jnp.float32),
+    pltpu.SemaphoreType.DMA((8,)),
+]
 
 
 def cost(flops, moved, exps=0):
@@ -357,9 +382,9 @@
 
     local = pl.pallas_call(
         local_kernel,
-        out_shape=array(4, *handed, dtype=jnp.float32),
+        out_shape=(array(*handed, dtype=jnp.float32),) * 4,
         in_specs=[smem, smem] + [anywhere] * 4,
-        out_specs=anywhere,
+        out_specs=(anywhere,) * 4,
         scratch_shapes=local_scratch,
         compiler_params=limit(LOCAL_LIMIT),
         cost_estimate=cost(1 << 30, 8 << 20, 2 << 20),
@@ -371,22 +396,36 @@
         return pl.pallas_call(
             functools.partial(rows_kernel, offsets),
             out_shape=(array(TOKENS, D, dtype=dtype),) * count,
-            in_specs=[smem, smem, vmem, vmem] + [anywhere] * 3,
+            in_specs=[smem, smem, vmem, vmem, anywhere, anywhere] + [vmem] * count,
             out_specs=(vmem,) * count,
-            scratch_shapes=[
-                pltpu.VMEM((2 * ROW, 2 * WIDTH), jnp.bfloat16),
-                pltpu.VMEM((count,) + handed, jnp.float32),
-                pltpu.VMEM((4, PAIRS, 2 * TOKENS, CHUNK), jnp.float32),
-                pltpu.VMEM(running, jnp.float32),
-                pltpu.VMEM((count * TOKENS, WIDTH), jnp.bfloat16),
-                pltpu.SemaphoreType.DMA((10,)),
-            ],
+            scratch_shapes=rows_scratch + [pltpu.VMEM((count * TOKENS, WIDTH), jnp.bfloat16)],
             compiler_params=limit(ROWS_LIMIT),
             cost_estimate=cost(count << 29, 4 << 20, count << 20),
             name="rows",
-        )(lengths, place, own_weights, other_weights, before, after, local)
-
-    (far,) = rows_of((2,), jnp.bfloat16)
+        )(
+            lengths, place, own_weights, other_weights, before, after,
+            *[local[offset] for offset in offsets],
+        )
+
+    mixed = pl.pallas_call(
+        functools.partial(attend_kernel, (2,)),
+        out_shape=array(TOKENS, WIDTH),
+        in_specs=[smem, smem, anywhere, anywhere, vmem],
+        out_specs=vmem,
+        scratch_shapes=rows_scratch,
+        compiler_params=limit(ROWS_LIMIT),
+        cost_estimate=cost(1 << 28, 3 << 20, 1 << 20),
+        name="attend",
+    )(lengths, place, before, after, local[2])
+    far = pl.pallas_call(
+        project_kernel,
+        out_shape=array(TOKENS, D),
+        in_specs=[smem, vmem, vmem, vmem],
+        out_specs=vmem,
+        compiler_params=limit(8),
+        cost_estimate=cost(2 * TOKENS * WIDTH * D, 3 << 20),
+        name="project",
+    )(place, own_weights, other_weights, mixed)
     far = shift(far, 2)
     up, down = rows_of((1, 3), jnp.bfloat16)
     up = shift(up, 1)

time: 139 us -> 141 us (1.014)
  waiting for transfers between devices: 38.6 us -> 41.8 us
  Pallas kernels: 28.9 us -> 26.1 us
  local copies, waits for them, and re-layouts: 2.03 us -> 3.86 us
    pallas_call x3 -> x2, Pallas kernels: 14.5 us -> 8.67 us  [rows_of(): pl.pallas_call(functools.partial(rows_kernel, offsets), out_shape=(array(...]
    ppermute x9, waiting for transfers between devices: 38.6 us -> 41.8 us  [shift(): lax.ppermute(value, axis, [(i, (i + amount) % size) for i in range(size)])]
    pallas_call x1 -> x3, Pallas kernels: 9.79 us -> 12.9 us  [the longest x1 9.76 us: block(): pl.pallas_call(local_kernel, out_shape=(array(*handed, dtype=jnp.float32)...]
    unnamed x22 -> x30, local copies, waits for them, and re-layouts: 0.8 us -> 2.64 us
  transfers between devices with their start and end apart: 10 -> 10, of which waited for: 6 -> 6; matrix products, arithmetic and copies ran while one was open for 1% -> 1% of each run, Pallas kernels for 14% -> 13%
where the time goes in v5:
time: 141 us
  waiting for transfers between devices  41.8 us (30%)
  starting transfers between devices  33.4 us (24%)
  blocking collectives  32.9 us (23%)
  Pallas kernels  26.1 us (19%)
  local copies, waits for them, and re-layouts  3.86 us (3%)
  other arithmetic  1.85 us (1%)
    ppermute x9, waiting for transfers between devices, shift(): lax.ppermute(value, axis, [(i, (i + amount) % size) for i in range(size)])  41.8 us
    all_to_all x1, blocking collectives, block(): lax.all_to_all(jnp.broadcast_to(teacher_new[None], (16,) + teacher_new.sh...  32.9 us
    ppermute x9, starting transfers between devices, shift(): lax.ppermute(value, axis, [(i, (i + amount) % size) for i in range(size)])  29.1 us
    pallas_call x1, Pallas kernels, block(): pl.pallas_call(local_kernel, out_shape=(array(*handed, dtype=jnp.float32)...  9.76 us
    pallas_call x2, Pallas kernels, rows_of(): pl.pallas_call(functools.partial(rows_kernel, offsets), out_shape=(array(...  8.67 us
    all_to_all x1, starting transfers between devices, block(): lax.all_to_all(jnp.broadcast_to(ring_weights[None], (4,) + ring_weights.s...  4.29 us
  transfers between devices with their start and end apart: 10, of which 6 were waited for; matrix products, arithmetic and copies ran while one was open for 1% of the time, Pallas kernels for 13%

profile of v5, /device:TPU:56, one launch (start us, length us, event | category | flops | bytes accessed | tf_op | source)
XLA Modules:
  0.0 140.8 jit_solution(15632278758990132422)
XLA Ops:
  0.6 0.7 add_convert_fusion
  1.4 0.0 copy-start.14
  1.4 0.6 copy-done.14
  2.0 32.9 %all_to_all.10 = bf16[16,64,128]{2,1,0:T(8,128)(2,1)S(1)} all-to-all(bf16[16,64,128]{2,1,0:T(8,128)(2,1)S(1)} %broadcast_in_dim.16), channel_id=1, replica_groups=mesh['h'=2,'x'=4,'c'=2,'z'=8,'y'=4] {'h','z'}, dimensions={0} | all-to-all | bytes 524288 | tf_op jit(solution)/shard_map/all_to_all | solution.py:374
  35.0 1.1 broadcast_in_dim.18
  36.1 4.3 %all-to-all-start.1 = ((bf16[4,2,512,128]{3,2,1,0:T(8,128)(2,1)}), bf16[4,2,512,128]{3,2,1,0:T(8,128)(2,1)S(1)}, u32[]{:S(2)}, u32[]{:S(2)}) async-start(bf16[4,2,512,128]{3,2,1,0:T(8,128)(2,1)} %broadcast_in_dim.18), calls=%async_computation.1 | async-start | bytes 2097152 | tf_op jit(solution)/shard_map/all_to_all | solution.py:378
  40.4 0.1 pad_add_fusion.place_ref
  40.4 2.2 %pack.1 = (bf16[128,1536]{1,0:T(8,128)(2,1)S(1)}, bf16[128,1536]{1,0:T(8,128)(2,1)S(1)}, bf16[128,1536]{1,0:T(8,128)(2,1)S(1)}, bf16[128,1536]{1,0:T(8,128)(2,1)S(1)}) custom-call(s32[3]{0:T(128)S(1)} %pad_add_fusion.place_ref, bf16[128,6144]{1,0:T(8,128)(2,1)S(1)} %bitcast.8), custom_call_target="tpu_custom_call" | custom-call | bytes 3145728 | tf_op jit(solution)/shard_map/pack/pallas_call | solution.py:364
  42.7 2.7 %collective-permute-start.1 = (bf16[128,1536]{1,0:T(8,128)(2,1)S(1)}, bf16[128,1536]{1,0:T(8,128)(2,1)S(1)}, u32[]{:S(2)}, u32[]{:S(2)}) collective-permute-start(bf16[128,1536]{1,0:T(8,128)(2,1)S(1)} %get-tuple-element.13), channel_id=1, source_target_pairs={{0,3},{1,0},{2,1},{3,2},{4,7},{5,4},{6,5},{7,6},{8,11},{9,8},{10,9... | collective-permute-start | bytes 1179656 | tf_op jit(solution)/shard_map/ppermute | solution.py:344
  45.3 2.8 %collective-permute-start.2 = (bf16[128,1536]{1,0:T(8,128)(2,1)S(1)}, bf16[128,1536]{1,0:T(8,128)(2,1)S(1)}, u32[]{:S(2)}, u32[]{:S(2)}) collective-permute-start(bf16[128,1536]{1,0:T(8,128)(2,1)S(1)} %get-tuple-element.14), channel_id=1, source_target_pairs={{0,2},{1,3},{2,0},{3,1},{4,6},{5,7},{6,4},{7,5},{8,10},{9,11},{10,... | collective-permute-start | bytes 1179656 | tf_op jit(solution)/shard_map/ppermute | solution.py:344
  48.2 4.1 %collective-permute-start.3 = (bf16[128,1536]{1,0:T(8,128)(2,1)S(1)}, bf16[128,1536]{1,0:T(8,128)(2,1)S(1)}, u32[]{:S(2)}, u32[]{:S(2)}) collective-permute-start(bf16[128,1536]{1,0:T(8,128)(2,1)S(1)} %get-tuple-element.15), channel_id=1, source_target_pairs={{0,1},{1,2},{2,3},{3,0},{4,5},{5,6},{6,7},{7,4},{8,9},{9,10},{10,1... | collective-permute-start | bytes 1179656 | tf_op jit(solution)/shard_map/ppermute | solution.py:344
  52.3 11.7 %collective-permute-done.1.next_piece = bf16[128,1536]{1,0:T(8,128)(2,1)S(1)} collective-permute-done((bf16[128,1536]{1,0:T(8,128)(2,1)S(1)}, bf16[128,1536]{1,0:T(8,128)(2,1)S(1)}, u32[]{:S(2)}, u32[]{:S(2)}) %collective-permute-start.1) | collective-permute-done | bytes 393248 | tf_op jit(solution)/shard_map/ppermute | solution.py:344
  64.0 2.5 %collective-permute-done.3.last = bf16[128,1536]{1,0:T(8,128)(2,1)S(1)} collective-permute-done((bf16[128,1536]{1,0:T(8,128)(2,1)S(1)}, bf16[128,1536]{1,0:T(8,128)(2,1)S(1)}, u32[]{:S(2)}, u32[]{:S(2)}) %collective-permute-start.3) | collective-permute-done | bytes 393248 | tf_op jit(solution)/shard_map/ppermute | solution.py:344
  66.5 0.8 copy-done.13
  67.3 1.0 pad_maximum_fusion
  68.3 1.9 %collective-permute-start.4 = (bf16[512,1024]{1,0:T(8,128)(2,1)}, bf16[512,1024]{1,0:T(8,128)(2,1)S(1)}, u32[]{:S(2)}, u32[]{:S(2)}) collective-permute-start(bf16[512,1024]{1,0:T(8,128)(2,1)} %pad_maximum_fusion), channel_id=1, source_target_pairs={{0,4},{4,8},{8,12},{12,16},{16,20},{20,24},{24,28},{28,256},{256,2... | collective-permute-start | bytes 3145736 | tf_op jit(solution)/shard_map/ppermute | solution.py:344
  70.3 3.9 %collective-permute-start.5 = (bf16[512,1024]{1,0:T(8,128)(2,1)}, bf16[512,1024]{1,0:T(8,128)(2,1)S(1)}, u32[]{:S(2)}, u32[]{:S(2)}) collective-permute-start(bf16[512,1024]{1,0:T(8,128)(2,1)} %pad_maximum_fusion), channel_id=1, source_target_pairs={{0,284},{4,0},{8,4},{12,8},{16,12},{20,16},{24,20},{28,24},{256,28... | collective-permute-start | bytes 3145736 | tf_op jit(solution)/shard_map/ppermute | solution.py:344
  74.2 1.9 %collective-permute-start = (bf16[4,2,512,128]{3,2,1,0:T(8,128)(2,1)S(1)}, bf16[4,2,512,128]{3,2,1,0:T(8,128)(2,1)S(1)}, u32[]{:S(2)}, u32[]{:S(2)}) collective-permute-start(bf16[4,2,512,128]{3,2,1,0:T(8,128)(2,1)S(1)} %all-to-all-done.1.own_weights), channel_id=1, source_target_pairs={{0,32},{32,0},{1,33},{33,1},{2,34},{34,2},{3,35},{35,3},{4,36},{36... | collective-permute-start | bytes 3145736 | tf_op jit(solution)/shard_map/ppermute | solution.py:344
  76.1 9.8 %local.1 = (f32[16,128,128]{2,1,0:T(8,128)}, f32[16,128,128]{2,1,0:T(8,128)}, f32[16,128,128]{2,1,0:T(8,128)}, f32[16,128,128]{2,1,0:T(8,128)}) custom-call(s32[1,12]{1,0:T(1,128)} %lengths_ref.7, s32[3]{0:T(128)} %copy-done.8, bf16[128,1536]{1,0:T(8,128)(2,1)} %copy-done.7, bf16[128,1536]{1,0:T(8,128)(2,1)} %copy-done.11, bf16[128,1536]{1,0:T(8,128)(2,1)} %copy-done.12, ...), custom_call_target="tpu_custom_call" | custom-call | flops 1073741824 | bytes 8388608 | tf_op jit(solution)/shard_map/local/pallas_call | solution.py:383
  85.9 8.6 %collective-permute-done.4.before = bf16[512,1024]{1,0:T(8,128)(2,1)S(1)} collective-permute-done((bf16[512,1024]{1,0:T(8,128)(2,1)}, bf16[512,1024]{1,0:T(8,128)(2,1)S(1)}, u32[]{:S(2)}, u32[]{:S(2)}) %collective-permute-start.4) | collective-permute-done | bytes 1048608 | tf_op jit(solution)/shard_map/ppermute | solution.py:344
  94.5 2.4 %collective-permute-done.5.after = bf16[512,1024]{1,0:T(8,128)(2,1)S(1)} collective-permute-done((bf16[512,1024]{1,0:T(8,128)(2,1)}, bf16[512,1024]{1,0:T(8,128)(2,1)S(1)}, u32[]{:S(2)}, u32[]{:S(2)}) %collective-permute-start.5) | collective-permute-done | bytes 1048608 | tf_op jit(solution)/shard_map/ppermute | solution.py:344
  96.8 1.2 copy-done.2
  98.1 2.1 %attend.1.mixed = bf16[128,512]{1,0:T(8,128)(2,1)S(1)} custom-call(s32[1,12]{1,0:T(1,128)S(1)} %copy-done.10, s32[3]{0:T(128)S(1)} %copy-done.9, bf16[512,1024]{1,0:T(8,128)(2,1)S(1)} %collective-permute-done.4.before, bf16[512,1024]{1,0:T(8,128)(2,1)S(1)} %collective-permute-done.5.after, f32[16,128,128]{2,1,0:T(8,128)S(1)} %copy-done.2), custom_call_target="tpu_custom_call" | custom-call | flops 268435456 | bytes 3145728 | tf_op jit(solution)/shard_map/attend/pallas_call | solution.py:410
  100.2 5.4 %rows.3 = (bf16[128,2048]{1,0:T(8,128)(2,1)S(1)}, bf16[128,2048]{1,0:T(8,128)(2,1)S(1)}) custom-call(s32[1,12]{1,0:T(1,128)S(1)} %copy-done.10, s32[3]{0:T(128)S(1)} %copy-done.9, bf16[4,2,512,128]{3,2,1,0:T(8,128)(2,1)S(1)} %all-to-all-done.1.own_weights, bf16[4,2,512,128]{3,2,1,0:T(8,128)(2,1)S(1)} %collective-permute-done.other_weights, ...), custom_call_target="tpu_custom_call" | custom-call | flops 1073741824 | bytes 4194304 | tf_op jit(solution)/shard_map/rows/pallas_call | solution.py:396
  105.7 6.4 %collective-permute-start.7 = (bf16[128,2048]{1,0:T(8,128)(2,1)S(1)}, bf16[128,2048]{1,0:T(8,128)(2,1)S(1)}, u32[]{:S(2)}, u32[]{:S(2)}) collective-permute-start(bf16[128,2048]{1,0:T(8,128)(2,1)S(1)} %get-tuple-element.20), channel_id=1, source_target_pairs={{0,1},{1,2},{2,3},{3,0},{4,5},{5,6},{6,7},{7,4},{8,9},{9,10},{10,1... | collective-permute-start | bytes 1572872 | tf_op jit(solution)/shard_map/ppermute | solution.py:344
  112.1 1.9 %collective-permute-start.8 = (bf16[128,2048]{1,0:T(8,128)(2,1)S(1)}, bf16[128,2048]{1,0:T(8,128)(2,1)S(1)}, u32[]{:S(2)}, u32[]{:S(2)}) collective-permute-start(bf16[128,2048]{1,0:T(8,128)(2,1)S(1)} %get-tuple-element.21), channel_id=1, source_target_pairs={{0,3},{1,0},{2,1},{3,2},{4,7},{5,4},{6,5},{7,6},{8,11},{9,8},{10,9... | collective-permute-start | bytes 1572872 | tf_op jit(solution)/shard_map/ppermute | solution.py:344
  114.0 1.0 project.1
  115.1 3.4 %collective-permute-start.6 = (bf16[128,2048]{1,0:T(8,128)(2,1)S(1)}, bf16[128,2048]{1,0:T(8,128)(2,1)S(1)}, u32[]{:S(2)}, u32[]{:S(2)}) collective-permute-start(bf16[128,2048]{1,0:T(8,128)(2,1)S(1)} %project.1), channel_id=1, source_target_pairs={{0,2},{1,3},{2,0},{3,1},{4,6},{5,7},{6,4},{7,5},{8,10},{9,11},{10,... | collective-permute-start | bytes 1572872 | tf_op jit(solution)/shard_map/ppermute | solution.py:344
  118.5 3.2 %rows.2.own_ref = f32[128,2048]{1,0:T(8,128)S(1)} custom-call(s32[1,12]{1,0:T(1,128)S(1)} %copy-done.10, s32[3]{0:T(128)S(1)} %copy-done.9, bf16[4,2,512,128]{3,2,1,0:T(8,128)(2,1)S(1)} %all-to-all-done.1.own_weights, bf16[4,2,512,128]{3,2,1,0:T(8,128)(2,1)S(1)} %collective-permute-done.other_weights, bf16[512,1024]{1,0:T(8,128)(2,1)S(1)} %collective-permute-done.4.before, ...), custom_call_target="tpu_custom_call" | custom-call | flops 536870912 | bytes 4194304 | tf_op jit(solution)/shard_map/rows/pallas_call | solution.py:396
  121.7 11.4 %collective-permute-done.7.two_ref = bf16[128,2048]{1,0:T(8,128)(2,1)S(1)} collective-permute-done((bf16[128,2048]{1,0:T(8,128)(2,1)S(1)}, bf16[128,2048]{1,0:T(8,128)(2,1)S(1)}, u32[]{:S(2)}, u32[]{:S(2)}) %collective-permute-start.7) | collective-permute-done | bytes 524320 | tf_op jit(solution)/shard_map/ppermute | solution.py:344
  133.1 5.3 %collective-permute-done.8.three_ref = bf16[128,2048]{1,0:T(8,128)(2,1)S(1)} collective-permute-done((bf16[128,2048]{1,0:T(8,128)(2,1)S(1)}, bf16[128,2048]{1,0:T(8,128)(2,1)S(1)}, u32[]{:S(2)}, u32[]{:S(2)}) %collective-permute-start.8) | collective-permute-done | bytes 524320 | tf_op jit(solution)/shard_map/ppermute | solution.py:344
  138.5 2.3 %finish.1 = f32[128,2048]{1,0:T(8,128)} custom-call(f32[128,2048]{1,0:T(8,128)S(1)} %rows.2.own_ref, bf16[128,2048]{1,0:T(8,128)(2,1)S(1)} %collective-permute-done.6.one_ref, bf16[128,2048]{1,0:T(8,128)(2,1)S(1)} %collective-permute-done.7.two_ref, bf16[128,2048]{1,0:T(8,128)(2,1)S(1)} %collective-permute-done.8.three_ref, bf16[128,2048]{1,0:T(8,128)(2,1)S(1)} %bitcast.10, ...), custom_call_target="tpu_custom_call" | custom-call | flops 4194304 | bytes 5242880 | tf_op jit(solution)/shard_map/finish/pallas_call | solution.py:435
  (35 shorter events, 0.2 us)
Async XLA Ops:
  1.4 0.6 copy-start.14
  35.0 5.5 %copy-start = (bf16[1,128,6144]{2,1,0:T(8,128)(2,1)S(1)}, bf16[1,128,6144]{2,1,0:T(8,128)(2,1)}, u32[]{:S(2)}) copy-start(bf16[1,128,6144]{2,1,0:T(8,128)(2,1)} %param.6) | copy-start | bytes 4718596
  36.1 38.1 %all-to-all-start.1 = ((bf16[4,2,512,128]{3,2,1,0:T(8,128)(2,1)}), bf16[4,2,512,128]{3,2,1,0:T(8,128)(2,1)S(1)}, u32[]{:S(2)}, u32[]{:S(2)}) async-start(bf16[4,2,512,128]{3,2,1,0:T(8,128)(2,1)} %broadcast_in_dim.18), calls=%async_computation.1 | async-start | bytes 2097152 | tf_op jit(solution)/shard_map/all_to_all | solution.py:378
  40.4 23.6 %copy-start.8 = (s32[3]{0:T(128)}, s32[3]{0:T(128)S(1)}, u32[]{:S(2)}) copy-start(s32[3]{0:T(128)S(1)} %pad_add_fusion.place_ref) | copy-start | bytes 40
  42.6 25.7 %copy-start.7 = (bf16[128,1536]{1,0:T(8,128)(2,1)}, bf16[128,1536]{1,0:T(8,128)(2,1)S(1)}, u32[]{:S(2)}) copy-start(bf16[128,1536]{1,0:T(8,128)(2,1)S(1)} %get-tuple-element.12.own) | copy-start | bytes 1179652
  42.7 21.3 %collective-permute-start.1 = (bf16[128,1536]{1,0:T(8,128)(2,1)S(1)}, bf16[128,1536]{1,0:T(8,128)(2,1)S(1)}, u32[]{:S(2)}, u32[]{:S(2)}) collective-permute-start(bf16[128,1536]{1,0:T(8,128)(2,1)S(1)} %get-tuple-element.13), channel_id=1, source_target_pairs={{0,3},{1,0},{2,1},{3,2},{4,7},{5,4},{6,5},{7,6},{8,11},{9,8},{10,9... | collective-permute-start | bytes 1179656 | tf_op jit(solution)/shard_map/ppermute | solution.py:344
  45.3 18.7 %collective-permute-start.2 = (bf16[128,1536]{1,0:T(8,128)(2,1)S(1)}, bf16[128,1536]{1,0:T(8,128)(2,1)S(1)}, u32[]{:S(2)}, u32[]{:S(2)}) collective-permute-start(bf16[128,1536]{1,0:T(8,128)(2,1)S(1)} %get-tuple-element.14), channel_id=1, source_target_pairs={{0,2},{1,3},{2,0},{3,1},{4,6},{5,7},{6,4},{7,5},{8,10},{9,11},{10,... | collective-permute-start | bytes 1179656 | tf_op jit(solution)/shard_map/ppermute | solution.py:344
  48.2 18.3 %collective-permute-start.3 = (bf16[128,1536]{1,0:T(8,128)(2,1)S(1)}, bf16[128,1536]{1,0:T(8,128)(2,1)S(1)}, u32[]{:S(2)}, u32[]{:S(2)}) collective-permute-start(bf16[128,1536]{1,0:T(8,128)(2,1)S(1)} %get-tuple-element.15), channel_id=1, source_target_pairs={{0,1},{1,2},{2,3},{3,0},{4,5},{5,6},{6,7},{7,4},{8,9},{9,10},{10,1... | collective-permute-start | bytes 1179656 | tf_op jit(solution)/shard_map/ppermute | solution.py:344
  64.0 4.4 %copy-start.11 = (bf16[128,1536]{1,0:T(8,128)(2,1)}, bf16[128,1536]{1,0:T(8,128)(2,1)S(1)}, u32[]{:S(2)}) copy-start(bf16[128,1536]{1,0:T(8,128)(2,1)S(1)} %collective-permute-done.1.next_piece) | copy-start | bytes 1179652
  64.0 2.5 %copy-start.12 = (bf16[128,1536]{1,0:T(8,128)(2,1)}, bf16[128,1536]{1,0:T(8,128)(2,1)S(1)}, u32[]{:S(2)}) copy-start(bf16[128,1536]{1,0:T(8,128)(2,1)S(1)} %collective-permute-done.2.far) | copy-start | bytes 1179652
  66.5 0.8 copy-start.13
  68.3 28.5 %copy-start.9 = (s32[3]{0:T(128)S(1)}, s32[3]{0:T(128)}, u32[]{:S(2)}) copy-start(s32[3]{0:T(128)} %copy-done.8) | copy-start | bytes 40
  68.3 28.5 %copy-start.10 = (s32[1,12]{1,0:T(1,128)S(1)}, s32[1,12]{1,0:T(1,128)}, u32[]{:S(2)}) copy-start(s32[1,12]{1,0:T(1,128)} %lengths_ref.7) | copy-start | bytes 148
  68.3 26.1 %collective-permute-start.4 = (bf16[512,1024]{1,0:T(8,128)(2,1)}, bf16[512,1024]{1,0:T(8,128)(2,1)S(1)}, u32[]{:S(2)}, u32[]{:S(2)}) collective-permute-start(bf16[512,1024]{1,0:T(8,128)(2,1)} %pad_maximum_fusion), channel_id=1, source_target_pairs={{0,4},{4,8},{8,12},{12,16},{16,20},{20,24},{24,28},{28,256},{256,2... | collective-permute-start | bytes 3145736 | tf_op jit(solution)/shard_map/ppermute | solution.py:344
  70.3 26.6 %collective-permute-start.5 = (bf16[512,1024]{1,0:T(8,128)(2,1)}, bf16[512,1024]{1,0:T(8,128)(2,1)S(1)}, u32[]{:S(2)}, u32[]{:S(2)}) collective-permute-start(bf16[512,1024]{1,0:T(8,128)(2,1)} %pad_maximum_fusion), channel_id=1, source_target_pairs={{0,284},{4,0},{8,4},{12,8},{16,12},{20,16},{24,20},{28,24},{256,28... | collective-permute-start | bytes 3145736 | tf_op jit(solution)/shard_map/ppermute | solution.py:344
  74.2 26.0 %collective-permute-start = (bf16[4,2,512,128]{3,2,1,0:T(8,128)(2,1)S(1)}, bf16[4,2,512,128]{3,2,1,0:T(8,128)(2,1)S(1)}, u32[]{:S(2)}, u32[]{:S(2)}) collective-permute-start(bf16[4,2,512,128]{3,2,1,0:T(8,128)(2,1)S(1)} %all-to-all-done.1.own_weights), channel_id=1, source_target_pairs={{0,32},{32,0},{1,33},{33,1},{2,34},{34,2},{3,35},{35,3},{4,36},{36... | collective-permute-start | bytes 3145736 | tf_op jit(solution)/shard_map/ppermute | solution.py:344
  96.8 1.2 copy-start.2
  98.1 2.1 %copy-start.4 = (f32[16,128,128]{2,1,0:T(8,128)S(1)}, f32[16,128,128]{2,1,0:T(8,128)}, u32[]{:S(2)}) copy-start(f32[16,128,128]{2,1,0:T(8,128)} %get-tuple-element.18.rest_0_) | copy-start | bytes 3145732
  98.1 2.1 %copy-start.5 = (f32[16,128,128]{2,1,0:T(8,128)S(1)}, f32[16,128,128]{2,1,0:T(8,128)}, u32[]{:S(2)}) copy-start(f32[16,128,128]{2,1,0:T(8,128)} %get-tuple-element.19.rest_1_) | copy-start | bytes 3145732
  105.7 12.8 %copy-start.3 = (f32[16,128,128]{2,1,0:T(8,128)S(1)}, f32[16,128,128]{2,1,0:T(8,128)}, u32[]{:S(2)}) copy-start(f32[16,128,128]{2,1,0:T(8,128)} %get-tuple-element.16.rest_0_) | copy-start | bytes 3145732
  105.7 27.5 %collective-permute-start.7 = (bf16[128,2048]{1,0:T(8,128)(2,1)S(1)}, bf16[128,2048]{1,0:T(8,128)(2,1)S(1)}, u32[]{:S(2)}, u32[]{:S(2)}) collective-permute-start(bf16[128,2048]{1,0:T(8,128)(2,1)S(1)} %get-tuple-element.20), channel_id=1, source_target_pairs={{0,1},{1,2},{2,3},{3,0},{4,5},{5,6},{6,7},{7,4},{8,9},{9,10},{10,1... | collective-permute-start | bytes 1572872 | tf_op jit(solution)/shard_map/ppermute | solution.py:344
  112.1 26.3 %collective-permute-start.8 = (bf16[128,2048]{1,0:T(8,128)(2,1)S(1)}, bf16[128,2048]{1,0:T(8,128)(2,1)S(1)}, u32[]{:S(2)}, u32[]{:S(2)}) collective-permute-start(bf16[128,2048]{1,0:T(8,128)(2,1)S(1)} %get-tuple-element.21), channel_id=1, source_target_pairs={{0,3},{1,0},{2,1},{3,2},{4,7},{5,4},{6,5},{7,6},{8,11},{9,8},{10,9... | collective-permute-start | bytes 1572872 | tf_op jit(solution)/shard_map/ppermute | solution.py:344
  115.1 23.4 %collective-permute-start.6 = (bf16[128,2048]{1,0:T(8,128)(2,1)S(1)}, bf16[128,2048]{1,0:T(8,128)(2,1)S(1)}, u32[]{:S(2)}, u32[]{:S(2)}) collective-permute-start(bf16[128,2048]{1,0:T(8,128)(2,1)S(1)} %project.1), channel_id=1, source_target_pairs={{0,2},{1,3},{2,0},{3,1},{4,6},{5,7},{6,4},{7,5},{8,10},{9,11},{10,... | collective-permute-start | bytes 1572872 | tf_op jit(solution)/shard_map/ppermute | solution.py:344
  118.5 20.0 %copy-start.1 = (f32[1,128,2048]{2,1,0:T(8,128)S(1)}, f32[1,128,2048]{2,1,0:T(8,128)}, u32[]{:S(2)}) copy-start(f32[1,128,2048]{2,1,0:T(8,128)} %param.8) | copy-start | bytes 3145732
  118.5 20.0 %copy-start.6 = (bf16[1,128,2048]{2,1,0:T(8,128)(2,1)S(1)}, bf16[1,128,2048]{2,1,0:T(8,128)(2,1)}, u32[]{:S(2)}) copy-start(bf16[1,128,2048]{2,1,0:T(8,128)(2,1)} %param.7) | copy-start | bytes 1572868

commit v6 on v5

--- a/solution.py
+++ b/solution.py
@@ -20,6 +20,7 @@
 PAIRS = WIDTH // LANES
 LOCAL_LIMIT = 58
 ROWS_LIMIT = 24
+PACK_LIMIT = 61
 PACKED = 32
 
 ema_decay = 0.9
@@ -27,25 +28,59 @@
 masked_score = -1e30
 
 
-def pack_kernel(place_ref, qkv_ref, *outs):
+def pack_kernel(place_ref, teacher_ref, student_ref, qkv_hbm, *rest):
+    targets, (new_ref, copies_ref), (qkv, outs, sems) = rest[:4], rest[4:6], rest[6:]
+
+    def fetch(step):
+        span = pl.ds(pl.multiple_of(step * PACKED, PACKED), PACKED)
+        return pltpu.make_async_copy(qkv_hbm.at[span], qkv.at[step], sems.at[4, step])
+
+    def deliver(step, turn):
+        span = pl.ds(pl.multiple_of(step * PACKED, PACKED), PACKED)
+        return pltpu.make_async_copy(
+            outs.at[turn, span], targets[turn].at[span], sems.at[turn, step]
+        )
+
+    for step in range(TOKENS // PACKED):
+        fetch(step).start()
+    teacher_new = (
+        ema_decay * teacher_ref[...].astype(jnp.float32)
+        + (1.0 - ema_decay) * student_ref[...].astype(jnp.float32)
+    ).astype(jnp.bfloat16)
+    new_ref[...] = teacher_new
+    for i in range(copies_ref.shape[0]):
+        copies_ref[i] = teacher_new
     y = place_ref[1]
     low = lax.broadcasted_iota(jnp.int32, (PACKED, LANES), 1) < HEAD_DIM
-    for turn in range(4):
-        target = lax.rem(y + 4 - turn, 4)
-        odd = lax.rem(target, 2) == 1
-        half = lax.div(target, 2) * LANES
-        for part in range(3):
-            for pair in range(PAIRS):
-                base = part * D + pair * 512
-                first = qkv_ref[:, pl.ds(pl.multiple_of(base + half, LANES), LANES)].astype(jnp.float32)
-                second = qkv_ref[:, pl.ds(pl.multiple_of(base + 256 + half, LANES), LANES)].astype(jnp.float32)
-                left = jnp.where(odd, pltpu.roll(first, HEAD_DIM, 1), first)
-                right = jnp.where(odd, second, pltpu.roll(second, HEAD_DIM, 1))
-                both = jnp.where(low, left, right)
-                if part == 0:
-                    both = both * (1.0 / math.sqrt(HEAD_DIM))
-                start = part * WIDTH + pair * LANES
-                outs[turn][:, start : start + LANES] = both.astype(jnp.bfloat16)
+
+    def pack(step, carry):
+        fetch(step).wait()
+        rows = pl.ds(pl.multiple_of(step * PACKED, PACKED), PACKED)
+        for turn in range(4):
+            target = lax.rem(y + 4 - turn, 4)
+            odd = lax.rem(target, 2) == 1
+            half = lax.div(target, 2) * LANES
+            for part in range(3):
+                for pair in range(PAIRS):
+                    base = part * D + pair * 512
+                    here = pl.ds(pl.multiple_of(base + half, LANES), LANES)
+                    there = pl.ds(pl.multiple_of(base + 256 + half, LANES), LANES)
+                    first = qkv[step, :, here].astype(jnp.float32)
+                    second = qkv[step, :, there].astype(jnp.float32)
+                    left = jnp.where(odd, pltpu.roll(first, HEAD_DIM, 1), first)
+                    right = jnp.where(odd, second, pltpu.roll(second, HEAD_DIM, 1))
+                    both = jnp.where(low, left, right)
+                    if part == 0:
+                        both = both * (1.0 / math.sqrt(HEAD_DIM))
+                    start = part * WIDTH + pair * LANES
+                    outs[turn, rows, start : start + LANES] = both.astype(jnp.bfloat16)
+            deliver(step, turn).start()
+        return carry
+
+    lax.fori_loop(0, TOKENS // PACKED, pack, 0)
+    for step in range(TOKENS // PACKED):
+        for turn in range(4):
+            deliver(step, turn).wait()
 
 
 class Attention:
@@ -210,8 +245,8 @@
         both = jnp.concatenate([own_weights[place, high], other_weights[place, high]], axis=1)
         found = jnp.dot(mixed, both, preferred_element_type=jnp.float32)
         start = tile * 2 * LANES
-        store(pl.multiple_of(start + core * LANES, LANES), found[:, :LANES])
-        store(pl.multiple_of(start + (1 - core) * LANES, LANES), found[:, LANES:])
+        store(tile, pl.multiple_of(start + core * LANES, LANES), found[:, :LANES])
+        store(tile, pl.multiple_of(start + (1 - core) * LANES, LANES), found[:, LANES:])
 
 
 def attend_rows(offsets, lengths_ref, place_ref, before, after, priors, kv, scores, state, mixed, sems):
@@ -271,33 +306,38 @@
     )
 
 
-def project_kernel(place_ref, own_weights, other_weights, mixed, out_ref):
-    def store(start, value):
+HALF = D // 2
+
+
+def project_kernel(place_ref, own_weights, other_weights, mixed, first_ref, second_ref):
+    def store(tile, start, value):
+        out_ref = first_ref if tile < 4 else second_ref
+        start = pl.multiple_of(start - tile // 4 * HALF, LANES)
         out_ref[:, pl.ds(start, LANES)] = value.astype(out_ref.dtype)
 
     project(mixed[...], place_ref[2], own_weights, other_weights, store)
 
 
 def rows_kernel(
-    offsets, lengths_ref, place_ref, own_weights, other_weights, before, after, *rest
+    offset, lengths_ref, place_ref, own_weights, other_weights, before, after, prior, *rest
 ):
-    count = len(offsets)
-    priors, outs, scratch = rest[:count], rest[count : 2 * count], rest[2 * count :]
-    kv, scores, state, sems, mixed = scratch
+    passed, (out_ref, kv, scores, state, sems, mixed) = rest[:-6], rest[-6:]
     attend_rows(
-        offsets, lengths_ref, place_ref, before, after, priors, kv, scores, state, mixed, sems
-    )
-
-    def store(start, value):
-        for i, out_ref in enumerate(outs):
-            part = value[i * TOKENS : (i + 1) * TOKENS]
-            out_ref[:, pl.ds(start, LANES)] = part.astype(out_ref.dtype)
+        (offset,), lengths_ref, place_ref, before, after, (prior,), kv, scores, state, mixed, sems
+    )
+
+    def store(tile, start, value):
+        if passed and tile >= 4:
+            more = passed[0][:, pl.ds(pl.multiple_of(start - HALF, LANES), LANES)]
+            value = value + more.astype(jnp.float32)
+        out_ref[:, pl.ds(start, LANES)] = value.astype(out_ref.dtype)
 
     project(mixed[...], place_ref[2], own_weights, other_weights, store)
 
 
 def finish_kernel(own_ref, one_ref, two_ref, three_ref, resid_ref, earlier_ref, out_ref):
-    branch = own_ref[...] + one_ref[...].astype(jnp.float32)
+    far = one_ref[...].astype(jnp.float32)
+    branch = own_ref[...] + jnp.concatenate([far, jnp.zeros_like(far)], axis=1)
     branch = branch + two_ref[...].astype(jnp.float32)
     branch = branch + three_ref[...].astype(jnp.float32)
     summed = resid_ref[...].astype(jnp.float32) + branch * (1.0 / math.sqrt(D))
@@ -345,35 +385,33 @@
 
 
 def block(qkv, resid, earlier, lengths, teacher_out, student_out):
-    teacher_new = (
-        ema_decay * teacher_out.astype(jnp.float32)
-        + (1.0 - ema_decay) * student_out.astype(jnp.float32)
-    ).astype(jnp.bfloat16)
     place = jnp.stack([lax.axis_index(name) for name in ("z", "y", "c")]).astype(jnp.int32)
-
+    ring = 2 * lax.axis_size("z")
     pack = pl.pallas_call(
         pack_kernel,
-        grid=(TOKENS // PACKED,),
-        out_shape=(array(TOKENS, 3 * WIDTH),) * 4,
-        in_specs=[smem, pl.BlockSpec((PACKED, 3 * D), lambda i: (i, 0))],
-        out_specs=(pl.BlockSpec((PACKED, 3 * WIDTH), lambda i: (i, 0)),) * 4,
-        compiler_params=limit(12),
+        out_shape=(array(TOKENS, 3 * WIDTH),) * 4
+        + (array(*teacher_out.shape), array(ring, *teacher_out.shape)),
+        in_specs=[smem, vmem, vmem, anywhere],
+        out_specs=(anywhere,) * 4 + (vmem,) * 2,
+        scratch_shapes=[
+            pltpu.VMEM((TOKENS // PACKED, PACKED, 3 * D), jnp.bfloat16),
+            pltpu.VMEM((4, TOKENS, 3 * WIDTH), jnp.bfloat16),
+            pltpu.SemaphoreType.DMA((5, TOKENS // PACKED)),
+        ],
+        compiler_params=limit(PACK_LIMIT),
         cost_estimate=cost(0, 3 << 20),
         name="pack",
     )
-    packed = pack(place, qkv[0])
+    *packed, teacher_new, copies = pack(place, teacher_out, student_out, qkv[0])
 
     pieces = [packed[0]]
     for turn in (1, 2, 3):
         pieces.append(shift(packed[turn], -turn))
-    ring = 2 * lax.axis_size("z")
     keys = jnp.concatenate([piece[:, WIDTH:] for piece in pieces], axis=0)
     after = shift(keys, -1, ("h", "z"), ring)
     before = shift(keys, 1, ("h", "z"), ring)
 
-    ring_weights = lax.all_to_all(
-        jnp.broadcast_to(teacher_new[None], (16,) + teacher_new.shape), ("h", "z"), 0, 0, tiled=True
-    )
+    ring_weights = lax.all_to_all(copies, ("h", "z"), 0, 0, tiled=True)
     ring_weights = ring_weights.reshape(2, ROW, LANES)
     own_weights = lax.all_to_all(
         jnp.broadcast_to(ring_weights[None], (4,) + ring_weights.shape), "x", 0, 0, tiled=True
@@ -391,21 +429,17 @@
         name="local",
     )(lengths, place, *pieces)
 
-    def rows_of(offsets, dtype):
-        count = len(offsets)
+    def rows_of(offset, dtype, *passed):
         return pl.pallas_call(
-            functools.partial(rows_kernel, offsets),
-            out_shape=(array(TOKENS, D, dtype=dtype),) * count,
-            in_specs=[smem, smem, vmem, vmem, anywhere, anywhere] + [vmem] * count,
-            out_specs=(vmem,) * count,
-            scratch_shapes=rows_scratch + [pltpu.VMEM((count * TOKENS, WIDTH), jnp.bfloat16)],
+            functools.partial(rows_kernel, offset),
+            out_shape=array(TOKENS, D, dtype=dtype),
+            in_specs=[smem, smem, vmem, vmem, anywhere, anywhere, vmem] + [vmem] * len(passed),
+            out_specs=vmem,
+            scratch_shapes=rows_scratch + [pltpu.VMEM((TOKENS, WIDTH), jnp.bfloat16)],
             compiler_params=limit(ROWS_LIMIT),
-            cost_estimate=cost(count << 29, 4 << 20, count << 20),
+            cost_estimate=cost(1 << 29, 4 << 20, 1 << 20),
             name="rows",
-        )(
-            lengths, place, own_weights, other_weights, before, after,
-            *[local[offset] for offset in offsets],
-        )
+        )(lengths, place, own_weights, other_weights, before, after, local[offset], *passed)
 
     mixed = pl.pallas_call(
         functools.partial(attend_kernel, (2,)),
@@ -417,26 +451,28 @@
         cost_estimate=cost(1 << 28, 3 << 20, 1 << 20),
         name="attend",
     )(lengths, place, before, after, local[2])
-    far = pl.pallas_call(
+    far, passed = pl.pallas_call(
         project_kernel,
-        out_shape=array(TOKENS, D),
+        out_shape=(array(TOKENS, HALF),) * 2,
         in_specs=[smem, vmem, vmem, vmem],
-        out_specs=vmem,
+        out_specs=(vmem,) * 2,
         compiler_params=limit(8),
         cost_estimate=cost(2 * TOKENS * WIDTH * D, 3 << 20),
         name="project",
     )(place, own_weights, other_weights, mixed)
+    passed = shift(passed, 3)
     far = shift(far, 2)
-    up, down = rows_of((1, 3), jnp.bfloat16)
+    up = rows_of(1, jnp.bfloat16)
     up = shift(up, 1)
+    down = rows_of(3, jnp.bfloat16, passed)
     down = shift(down, 3)
-    (own,) = rows_of((0,), jnp.float32)
+    own = rows_of(0, jnp.float32)
     rows = pl.BlockSpec((32, D), lambda i: (i, 0))
     targets = pl.pallas_call(
         finish_kernel,
         grid=(4,),
         out_shape=array(TOKENS, D, dtype=jnp.float32),
-        in_specs=[rows] * 6,
+        in_specs=[rows, pl.BlockSpec((32, HALF), lambda i: (i, 0))] + [rows] * 4,
         out_specs=rows,
         compiler_params=limit(12),
         cost_estimate=cost(1 << 22, 5 << 20),

time: 141 us -> 142 us (level)
  the two profiles are of different devices: /device:TPU:56 before, /device:TPU:28 now
where the time goes in v6:
time: 142 us
  starting transfers between devices  40.6 us (29%)
  waiting for transfers between devices  36.5 us (26%)
  blocking collectives  33.6 us (24%)
  Pallas kernels  25.4 us (18%)
  local copies, waits for them, and re-layouts  3.17 us (2%)
  other arithmetic  1.68 us (1%)
    ppermute x10, waiting for transfers between devices, shift(): lax.ppermute(value, axis, [(i, (i + amount) % size) for i in range(size)])  36.5 us
    ppermute x10, starting transfers between devices, shift(): lax.ppermute(value, axis, [(i, (i + amount) % size) for i in range(size)])  35.8 us
    all_to_all x1, blocking collectives, block(): ring_weights = lax.all_to_all(copies, ('h', 'z'), 0, 0, tiled=True)  33.6 us
    pallas_call x1, Pallas kernels, block(): pl.pallas_call(local_kernel, out_shape=(array(*handed, dtype=jnp.float32)...  10.4 us
    pallas_call x3, Pallas kernels, rows_of(): pl.pallas_call(functools.partial(rows_kernel, offset), out_shape=array(TO...  5.63 us
    all_to_all x1, starting transfers between devices, block(): lax.all_to_all(jnp.broadcast_to(ring_weights[None], (4,) + ring_weights.s...  4.8 us
    pallas_call x1, Pallas kernels, block(): *packed, teacher_new, copies = pack(place, teacher_out, student_out, qkv[0])  4.59 us
  transfers between devices with their start and end apart: 11, of which 7 were waited for; matrix products, arithmetic and copies ran while one was open for 1% of the time, Pallas kernels for 12%

profile of v6, /device:TPU:28, one launch (start us, length us, event | category | flops | bytes accessed | tf_op | source)
XLA Modules:
  0.0 141.8 jit_solution(12174086063544658427)
XLA Ops:
  0.6 0.7 pad_add_fusion.place_ref
  1.3 4.6 %pack.1 = (bf16[128,1536]{1,0:T(8,128)(2,1)}, bf16[128,1536]{1,0:T(8,128)(2,1)}, bf16[128,1536]{1,0:T(8,128)(2,1)}, bf16[128,1536]{1,0:T(8,128)(2,1)}, bf16[64,1...) custom-call(s32[3]{0:T(128)} %pad_add_fusion.place_ref, bf16[64,128]{1,0:T(8,128)(2,1)} %teacher_ref.1, ...), custom_call_target="tpu_custom_call" | custom-call | bytes 3145728 | tf_op jit(solution)/shard_map/pack/pallas_call | solution.py:405
  5.9 33.6 %all_to_all.10 = bf16[16,64,128]{2,1,0:T(8,128)(2,1)S(1)} all-to-all(bf16[16,64,128]{2,1,0:T(8,128)(2,1)} %get-tuple-element.14), channel_id=1, replica_groups=mesh['h'=2,'x'=4,'c'=2,'z'=8,'y'=4] {'h','z'}, dimensions={0} | all-to-all | bytes 524288 | tf_op jit(solution)/shard_map/all_to_all | solution.py:414
  39.5 1.1 broadcast_in_dim.11
  40.6 4.8 %all-to-all-start.1 = ((bf16[4,2,512,128]{3,2,1,0:T(8,128)(2,1)}), bf16[4,2,512,128]{3,2,1,0:T(8,128)(2,1)S(1)}, u32[]{:S(2)}, u32[]{:S(2)}) async-start(bf16[4,2,512,128]{3,2,1,0:T(8,128)(2,1)} %broadcast_in_dim.11), calls=%async_computation.1 | async-start | bytes 2097152 | tf_op jit(solution)/shard_map/all_to_all | solution.py:416
  45.4 2.6 %collective-permute-start.1 = (bf16[128,1536]{1,0:T(8,128)(2,1)}, bf16[128,1536]{1,0:T(8,128)(2,1)S(1)}, u32[]{:S(2)}, u32[]{:S(2)}) collective-permute-start(bf16[128,1536]{1,0:T(8,128)(2,1)} %get-tuple-element.16), channel_id=1, source_target_pairs={{0,3},{1,0},{2,1},{3,2},{4,7},{5,4},{6,5},{7,6},{8,11},{9,8},{10,9... | collective-permute-start | bytes 1179656 | tf_op jit(solution)/shard_map/ppermute | solution.py:384
  48.0 2.8 %collective-permute-start.2 = (bf16[128,1536]{1,0:T(8,128)(2,1)S(1)}, bf16[128,1536]{1,0:T(8,128)(2,1)S(1)}, u32[]{:S(2)}, u32[]{:S(2)}) collective-permute-start(bf16[128,1536]{1,0:T(8,128)(2,1)S(1)} %copy-done.13), channel_id=1, source_target_pairs={{0,2},{1,3},{2,0},{3,1},{4,6},{5,7},{6,4},{7,5},{8,10},{9,11},{10,... | collective-permute-start | bytes 1179656 | tf_op jit(solution)/shard_map/ppermute | solution.py:384
  50.9 4.1 %collective-permute-start.3 = (bf16[128,1536]{1,0:T(8,128)(2,1)S(1)}, bf16[128,1536]{1,0:T(8,128)(2,1)S(1)}, u32[]{:S(2)}, u32[]{:S(2)}) collective-permute-start(bf16[128,1536]{1,0:T(8,128)(2,1)S(1)} %copy-done.12), channel_id=1, source_target_pairs={{0,1},{1,2},{2,3},{3,0},{4,5},{5,6},{6,7},{7,4},{8,9},{9,10},{10,1... | collective-permute-start | bytes 1179656 | tf_op jit(solution)/shard_map/ppermute | solution.py:384
  55.0 7.5 %collective-permute-done.1.next_piece = bf16[128,1536]{1,0:T(8,128)(2,1)S(1)} collective-permute-done((bf16[128,1536]{1,0:T(8,128)(2,1)}, bf16[128,1536]{1,0:T(8,128)(2,1)S(1)}, u32[]{:S(2)}, u32[]{:S(2)}) %collective-permute-start.1) | collective-permute-done | bytes 393248 | tf_op jit(solution)/shard_map/ppermute | solution.py:384
  62.6 2.3 %collective-permute-done.3.last = bf16[128,1536]{1,0:T(8,128)(2,1)S(1)} collective-permute-done((bf16[128,1536]{1,0:T(8,128)(2,1)S(1)}, bf16[128,1536]{1,0:T(8,128)(2,1)S(1)}, u32[]{:S(2)}, u32[]{:S(2)}) %collective-permute-start.3) | collective-permute-done | bytes 393248 | tf_op jit(solution)/shard_map/ppermute | solution.py:384
  64.9 0.7 copy-done.11
  65.7 1.0 pad_maximum_fusion
  66.7 7.5 %collective-permute-start.4 = (bf16[512,1024]{1,0:T(8,128)(2,1)}, bf16[512,1024]{1,0:T(8,128)(2,1)S(1)}, u32[]{:S(2)}, u32[]{:S(2)}) collective-permute-start(bf16[512,1024]{1,0:T(8,128)(2,1)} %pad_maximum_fusion), channel_id=1, source_target_pairs={{0,4},{4,8},{8,12},{12,16},{16,20},{20,24},{24,28},{28,256},{256,2... | collective-permute-start | bytes 3145736 | tf_op jit(solution)/shard_map/ppermute | solution.py:384
  74.2 2.2 %collective-permute-start.5 = (bf16[512,1024]{1,0:T(8,128)(2,1)}, bf16[512,1024]{1,0:T(8,128)(2,1)S(1)}, u32[]{:S(2)}, u32[]{:S(2)}) collective-permute-start(bf16[512,1024]{1,0:T(8,128)(2,1)} %pad_maximum_fusion), channel_id=1, source_target_pairs={{0,284},{4,0},{8,4},{12,8},{16,12},{20,16},{24,20},{28,24},{256,28... | collective-permute-start | bytes 3145736 | tf_op jit(solution)/shard_map/ppermute | solution.py:384
  76.5 1.9 %collective-permute-start = (bf16[4,2,512,128]{3,2,1,0:T(8,128)(2,1)S(1)}, bf16[4,2,512,128]{3,2,1,0:T(8,128)(2,1)S(1)}, u32[]{:S(2)}, u32[]{:S(2)}) collective-permute-start(bf16[4,2,512,128]{3,2,1,0:T(8,128)(2,1)S(1)} %all-to-all-done.1.own_weights), channel_id=1, source_target_pairs={{0,32},{32,0},{1,33},{33,1},{2,34},{34,2},{3,35},{35,3},{4,36},{36... | collective-permute-start | bytes 3145736 | tf_op jit(solution)/shard_map/ppermute | solution.py:384
  78.4 10.4 %local.1 = (f32[16,128,128]{2,1,0:T(8,128)}, f32[16,128,128]{2,1,0:T(8,128)}, f32[16,128,128]{2,1,0:T(8,128)}, f32[16,128,128]{2,1,0:T(8,128)}) custom-call(s32[1,12]{1,0:T(1,128)} %lengths_ref.9, s32[3]{0:T(128)} %pad_add_fusion.place_ref, bf16[128,1536]{1,0:T(8,128)(2,1)} %get-tuple-element.15.own, bf16[128,1536]{1,0:T(8,128)(2,1)} %copy-done.9, ...), custom_call_target="tpu_custom_call" | custom-call | flops 1073741824 | bytes 8388608 | tf_op jit(solution)/shard_map/local/pallas_call | solution.py:421
  88.8 7.3 %collective-permute-done.4.before = bf16[512,1024]{1,0:T(8,128)(2,1)S(1)} collective-permute-done((bf16[512,1024]{1,0:T(8,128)(2,1)}, bf16[512,1024]{1,0:T(8,128)(2,1)S(1)}, u32[]{:S(2)}, u32[]{:S(2)}) %collective-permute-start.4) | collective-permute-done | bytes 1048608 | tf_op jit(solution)/shard_map/ppermute | solution.py:384
  96.1 4.0 %collective-permute-done.5.after = bf16[512,1024]{1,0:T(8,128)(2,1)S(1)} collective-permute-done((bf16[512,1024]{1,0:T(8,128)(2,1)}, bf16[512,1024]{1,0:T(8,128)(2,1)S(1)}, u32[]{:S(2)}, u32[]{:S(2)}) %collective-permute-start.5) | collective-permute-done | bytes 1048608 | tf_op jit(solution)/shard_map/ppermute | solution.py:384
  100.1 1.2 copy-done.2
  101.3 1.4 %attend.1.mixed = bf16[128,512]{1,0:T(8,128)(2,1)S(1)} custom-call(s32[1,12]{1,0:T(1,128)S(1)} %copy-done.7, s32[3]{0:T(128)S(1)} %copy-done.6, bf16[512,1024]{1,0:T(8,128)(2,1)S(1)} %collective-permute-done.4.before, bf16[512,1024]{1,0:T(8,128)(2,1)S(1)} %collective-permute-done.5.after, f32[16,128,128]{2,1,0:T(8,128)S(1)} %copy-done.2), custom_call_target="tpu_custom_call" | custom-call | flops 268435456 | bytes 3145728 | tf_op jit(solution)/shard_map/attend/pallas_call | solution.py:444
  102.8 1.0 project.1
  103.8 3.4 %collective-permute-start.8 = (bf16[128,1024]{1,0:T(8,128)(2,1)S(1)}, bf16[128,1024]{1,0:T(8,128)(2,1)S(1)}, u32[]{:S(2)}, u32[]{:S(2)}) collective-permute-start(bf16[128,1024]{1,0:T(8,128)(2,1)S(1)} %get-tuple-element.24), channel_id=1, source_target_pairs={{0,3},{1,0},{2,1},{3,2},{4,7},{5,4},{6,5},{7,6},{8,11},{9,8},{10,9... | collective-permute-start | bytes 786440 | tf_op jit(solution)/shard_map/ppermute | solution.py:384
  107.2 1.9 %rows.4 = bf16[128,2048]{1,0:T(8,128)(2,1)S(1)} custom-call(s32[1,12]{1,0:T(1,128)S(1)} %copy-done.7, s32[3]{0:T(128)S(1)} %copy-done.6, bf16[4,2,512,128]{3,2,1,0:T(8,128)(2,1)S(1)} %all-to-all-done.1.own_weights, bf16[4,2,512,128]{3,2,1,0:T(8,128)(2,1)S(1)} %collective-permute-done.other_weights, bf16[512,1024]{1,0:T(8,128)(2,1)S(1)} %collective-permute-done.4.before, ...), custom_call_target="tpu_custom_call" | custom-call | flops 536870912 | bytes 4194304 | tf_op jit(solution)/shard_map/rows/pallas_call | solution.py:433
  109.1 4.1 %collective-permute-start.7 = (bf16[128,2048]{1,0:T(8,128)(2,1)S(1)}, bf16[128,2048]{1,0:T(8,128)(2,1)S(1)}, u32[]{:S(2)}, u32[]{:S(2)}) collective-permute-start(bf16[128,2048]{1,0:T(8,128)(2,1)S(1)} %rows.4), channel_id=1, source_target_pairs={{0,1},{1,2},{2,3},{3,0},{4,5},{5,6},{6,7},{7,4},{8,9},{9,10},{10,1... | collective-permute-start | bytes 1572872 | tf_op jit(solution)/shard_map/ppermute | solution.py:384
  113.2 2.2 %collective-permute-done.8.rest_0_ = bf16[128,1024]{1,0:T(8,128)(2,1)S(1)} collective-permute-done((bf16[128,1024]{1,0:T(8,128)(2,1)S(1)}, bf16[128,1024]{1,0:T(8,128)(2,1)S(1)}, u32[]{:S(2)}, u32[]{:S(2)}) %collective-permute-start.8) | collective-permute-done | bytes 262176 | tf_op jit(solution)/shard_map/ppermute | solution.py:384
  115.4 1.9 %rows.5 = bf16[128,2048]{1,0:T(8,128)(2,1)S(1)} custom-call(s32[1,12]{1,0:T(1,128)S(1)} %copy-done.7, s32[3]{0:T(128)S(1)} %copy-done.6, bf16[4,2,512,128]{3,2,1,0:T(8,128)(2,1)S(1)} %all-to-all-done.1.own_weights, bf16[4,2,512,128]{3,2,1,0:T(8,128)(2,1)S(1)} %collective-permute-done.other_weights, bf16[512,1024]{1,0:T(8,128)(2,1)S(1)} %collective-permute-done.4.before, ...), custom_call_target="tpu_custom_call" | custom-call | flops 536870912 | bytes 4194304 | tf_op jit(solution)/shard_map/rows/pallas_call | solution.py:433
  117.3 1.9 %collective-permute-start.9 = (bf16[128,2048]{1,0:T(8,128)(2,1)S(1)}, bf16[128,2048]{1,0:T(8,128)(2,1)S(1)}, u32[]{:S(2)}, u32[]{:S(2)}) collective-permute-start(bf16[128,2048]{1,0:T(8,128)(2,1)S(1)} %rows.5), channel_id=1, source_target_pairs={{0,3},{1,0},{2,1},{3,2},{4,7},{5,4},{6,5},{7,6},{8,11},{9,8},{10,9... | collective-permute-start | bytes 1572872 | tf_op jit(solution)/shard_map/ppermute | solution.py:384
  119.2 5.1 %collective-permute-start.6 = (bf16[128,1024]{1,0:T(8,128)(2,1)S(1)}, bf16[128,1024]{1,0:T(8,128)(2,1)S(1)}, u32[]{:S(2)}, u32[]{:S(2)}) collective-permute-start(bf16[128,1024]{1,0:T(8,128)(2,1)S(1)} %get-tuple-element.21), channel_id=1, source_target_pairs={{0,2},{1,3},{2,0},{3,1},{4,6},{5,7},{6,4},{7,5},{8,10},{9,11},{10,... | collective-permute-start | bytes 786440 | tf_op jit(solution)/shard_map/ppermute | solution.py:384
  124.4 1.9 %rows.3.own_ref = f32[128,2048]{1,0:T(8,128)S(1)} custom-call(s32[1,12]{1,0:T(1,128)S(1)} %copy-done.7, s32[3]{0:T(128)S(1)} %copy-done.6, bf16[4,2,512,128]{3,2,1,0:T(8,128)(2,1)S(1)} %all-to-all-done.1.own_weights, bf16[4,2,512,128]{3,2,1,0:T(8,128)(2,1)S(1)} %collective-permute-done.other_weights, bf16[512,1024]{1,0:T(8,128)(2,1)S(1)} %collective-permute-done.4.before, ...), custom_call_target="tpu_custom_call" | custom-call | flops 536870912 | bytes 4194304 | tf_op jit(solution)/shard_map/rows/pallas_call | solution.py:433
  126.2 13.0 %collective-permute-done.6.one_ref = bf16[128,1024]{1,0:T(8,128)(2,1)S(1)} collective-permute-done((bf16[128,1024]{1,0:T(8,128)(2,1)S(1)}, bf16[128,1024]{1,0:T(8,128)(2,1)S(1)}, u32[]{:S(2)}, u32[]{:S(2)}) %collective-permute-start.6) | collective-permute-done | bytes 262176 | tf_op jit(solution)/shard_map/ppermute | solution.py:384
  139.3 0.2 collective-permute-done.9.three_ref
  139.5 2.3 %finish.1 = f32[128,2048]{1,0:T(8,128)} custom-call(f32[128,2048]{1,0:T(8,128)S(1)} %rows.3.own_ref, bf16[128,1024]{1,0:T(8,128)(2,1)S(1)} %collective-permute-done.6.one_ref, bf16[128,2048]{1,0:T(8,128)(2,1)S(1)} %collective-permute-done.7.two_ref, bf16[128,2048]{1,0:T(8,128)(2,1)S(1)} %collective-permute-done.9.three_ref, bf16[128,2048]{1,0:T(8,128)(2,1)S(1)} %bitcast.9, ...), custom_call_target="tpu_custom_call" | custom-call | flops 4194304 | bytes 5242880 | tf_op jit(solution)/shard_map/finish/pallas_call | solution.py:471
  (34 shorter events, 0.1 us)
Async XLA Ops:
  39.5 8.6 %copy-start.13 = (bf16[128,1536]{1,0:T(8,128)(2,1)S(1)}, bf16[128,1536]{1,0:T(8,128)(2,1)}, u32[]{:S(2)}) copy-start(bf16[128,1536]{1,0:T(8,128)(2,1)} %get-tuple-element.17) | copy-start | bytes 1179652
  39.5 11.4 %copy-start.12 = (bf16[128,1536]{1,0:T(8,128)(2,1)S(1)}, bf16[128,1536]{1,0:T(8,128)(2,1)}, u32[]{:S(2)}) copy-start(bf16[128,1536]{1,0:T(8,128)(2,1)} %get-tuple-element.18) | copy-start | bytes 1179652
  39.5 15.5 %copy-start.8 = (bf16[128,1536]{1,0:T(8,128)(2,1)S(1)}, bf16[128,1536]{1,0:T(8,128)(2,1)}, u32[]{:S(2)}) copy-start(bf16[128,1536]{1,0:T(8,128)(2,1)} %get-tuple-element.15.own) | copy-start | bytes 1179652
  40.6 35.9 %all-to-all-start.1 = ((bf16[4,2,512,128]{3,2,1,0:T(8,128)(2,1)}), bf16[4,2,512,128]{3,2,1,0:T(8,128)(2,1)S(1)}, u32[]{:S(2)}, u32[]{:S(2)}) async-start(bf16[4,2,512,128]{3,2,1,0:T(8,128)(2,1)} %broadcast_in_dim.11), calls=%async_computation.1 | async-start | bytes 2097152 | tf_op jit(solution)/shard_map/all_to_all | solution.py:416
  45.4 17.1 %collective-permute-start.1 = (bf16[128,1536]{1,0:T(8,128)(2,1)}, bf16[128,1536]{1,0:T(8,128)(2,1)S(1)}, u32[]{:S(2)}, u32[]{:S(2)}) collective-permute-start(bf16[128,1536]{1,0:T(8,128)(2,1)} %get-tuple-element.16), channel_id=1, source_target_pairs={{0,3},{1,0},{2,1},{3,2},{4,7},{5,4},{6,5},{7,6},{8,11},{9,8},{10,9... | collective-permute-start | bytes 1179656 | tf_op jit(solution)/shard_map/ppermute | solution.py:384
  48.0 14.5 %collective-permute-start.2 = (bf16[128,1536]{1,0:T(8,128)(2,1)S(1)}, bf16[128,1536]{1,0:T(8,128)(2,1)S(1)}, u32[]{:S(2)}, u32[]{:S(2)}) collective-permute-start(bf16[128,1536]{1,0:T(8,128)(2,1)S(1)} %copy-done.13), channel_id=1, source_target_pairs={{0,2},{1,3},{2,0},{3,1},{4,6},{5,7},{6,4},{7,5},{8,10},{9,11},{10,... | collective-permute-start | bytes 1179656 | tf_op jit(solution)/shard_map/ppermute | solution.py:384
  50.9 14.0 %collective-permute-start.3 = (bf16[128,1536]{1,0:T(8,128)(2,1)S(1)}, bf16[128,1536]{1,0:T(8,128)(2,1)S(1)}, u32[]{:S(2)}, u32[]{:S(2)}) collective-permute-start(bf16[128,1536]{1,0:T(8,128)(2,1)S(1)} %copy-done.12), channel_id=1, source_target_pairs={{0,1},{1,2},{2,3},{3,0},{4,5},{5,6},{6,7},{7,4},{8,9},{9,10},{10,1... | collective-permute-start | bytes 1179656 | tf_op jit(solution)/shard_map/ppermute | solution.py:384
  62.5 2.4 %copy-start.9 = (bf16[128,1536]{1,0:T(8,128)(2,1)}, bf16[128,1536]{1,0:T(8,128)(2,1)S(1)}, u32[]{:S(2)}) copy-start(bf16[128,1536]{1,0:T(8,128)(2,1)S(1)} %collective-permute-done.1.next_piece) | copy-start | bytes 1179652
  62.6 2.4 %copy-start.10 = (bf16[128,1536]{1,0:T(8,128)(2,1)}, bf16[128,1536]{1,0:T(8,128)(2,1)S(1)}, u32[]{:S(2)}) copy-start(bf16[128,1536]{1,0:T(8,128)(2,1)S(1)} %collective-permute-done.2.far) | copy-start | bytes 1179652
  64.9 0.8 copy-start.11
  66.7 33.4 %copy-start.6 = (s32[3]{0:T(128)S(1)}, s32[3]{0:T(128)}, u32[]{:S(2)}) copy-start(s32[3]{0:T(128)} %pad_add_fusion.place_ref) | copy-start | bytes 40
  66.7 33.4 %copy-start.7 = (s32[1,12]{1,0:T(1,128)S(1)}, s32[1,12]{1,0:T(1,128)}, u32[]{:S(2)}) copy-start(s32[1,12]{1,0:T(1,128)} %lengths_ref.9) | copy-start | bytes 148
  66.7 29.4 %collective-permute-start.4 = (bf16[512,1024]{1,0:T(8,128)(2,1)}, bf16[512,1024]{1,0:T(8,128)(2,1)S(1)}, u32[]{:S(2)}, u32[]{:S(2)}) collective-permute-start(bf16[512,1024]{1,0:T(8,128)(2,1)} %pad_maximum_fusion), channel_id=1, source_target_pairs={{0,4},{4,8},{8,12},{12,16},{16,20},{20,24},{24,28},{28,256},{256,2... | collective-permute-start | bytes 3145736 | tf_op jit(solution)/shard_map/ppermute | solution.py:384
  74.2 25.8 %collective-permute-start.5 = (bf16[512,1024]{1,0:T(8,128)(2,1)}, bf16[512,1024]{1,0:T(8,128)(2,1)S(1)}, u32[]{:S(2)}, u32[]{:S(2)}) collective-permute-start(bf16[512,1024]{1,0:T(8,128)(2,1)} %pad_maximum_fusion), channel_id=1, source_target_pairs={{0,284},{4,0},{8,4},{12,8},{16,12},{20,16},{24,20},{28,24},{256,28... | collective-permute-start | bytes 3145736 | tf_op jit(solution)/shard_map/ppermute | solution.py:384
  76.5 26.3 %collective-permute-start = (bf16[4,2,512,128]{3,2,1,0:T(8,128)(2,1)S(1)}, bf16[4,2,512,128]{3,2,1,0:T(8,128)(2,1)S(1)}, u32[]{:S(2)}, u32[]{:S(2)}) collective-permute-start(bf16[4,2,512,128]{3,2,1,0:T(8,128)(2,1)S(1)} %all-to-all-done.1.own_weights), channel_id=1, source_target_pairs={{0,32},{32,0},{1,33},{33,1},{2,34},{34,2},{3,35},{35,3},{4,36},{36... | collective-permute-start | bytes 3145736 | tf_op jit(solution)/shard_map/ppermute | solution.py:384
  100.1 1.2 copy-start.2
  102.8 4.5 %copy-start.4 = (f32[16,128,128]{2,1,0:T(8,128)S(1)}, f32[16,128,128]{2,1,0:T(8,128)}, u32[]{:S(2)}) copy-start(f32[16,128,128]{2,1,0:T(8,128)} %get-tuple-element.22.prior) | copy-start | bytes 3145732
  103.8 11.6 %collective-permute-start.8 = (bf16[128,1024]{1,0:T(8,128)(2,1)S(1)}, bf16[128,1024]{1,0:T(8,128)(2,1)S(1)}, u32[]{:S(2)}, u32[]{:S(2)}) collective-permute-start(bf16[128,1024]{1,0:T(8,128)(2,1)S(1)} %get-tuple-element.24), channel_id=1, source_target_pairs={{0,3},{1,0},{2,1},{3,2},{4,7},{5,4},{6,5},{7,6},{8,11},{9,8},{10,9... | collective-permute-start | bytes 786440 | tf_op jit(solution)/shard_map/ppermute | solution.py:384
  107.2 8.2 %copy-start.1 = (f32[16,128,128]{2,1,0:T(8,128)S(1)}, f32[16,128,128]{2,1,0:T(8,128)}, u32[]{:S(2)}) copy-start(f32[16,128,128]{2,1,0:T(8,128)} %get-tuple-element.23.prior) | copy-start | bytes 3145732
  109.1 30.2 %collective-permute-start.7 = (bf16[128,2048]{1,0:T(8,128)(2,1)S(1)}, bf16[128,2048]{1,0:T(8,128)(2,1)S(1)}, u32[]{:S(2)}, u32[]{:S(2)}) collective-permute-start(bf16[128,2048]{1,0:T(8,128)(2,1)S(1)} %rows.4), channel_id=1, source_target_pairs={{0,1},{1,2},{2,3},{3,0},{4,5},{5,6},{6,7},{7,4},{8,9},{9,10},{10,1... | collective-permute-start | bytes 1572872 | tf_op jit(solution)/shard_map/ppermute | solution.py:384
  115.4 8.9 %copy-start.3 = (f32[16,128,128]{2,1,0:T(8,128)S(1)}, f32[16,128,128]{2,1,0:T(8,128)}, u32[]{:S(2)}) copy-start(f32[16,128,128]{2,1,0:T(8,128)} %get-tuple-element.19.prior) | copy-start | bytes 3145732
  117.3 22.2 %collective-permute-start.9 = (bf16[128,2048]{1,0:T(8,128)(2,1)S(1)}, bf16[128,2048]{1,0:T(8,128)(2,1)S(1)}, u32[]{:S(2)}, u32[]{:S(2)}) collective-permute-start(bf16[128,2048]{1,0:T(8,128)(2,1)S(1)} %rows.5), channel_id=1, source_target_pairs={{0,3},{1,0},{2,1},{3,2},{4,7},{5,4},{6,5},{7,6},{8,11},{9,8},{10,9... | collective-permute-start | bytes 1572872 | tf_op jit(solution)/shard_map/ppermute | solution.py:384
  119.2 20.0 %collective-permute-start.6 = (bf16[128,1024]{1,0:T(8,128)(2,1)S(1)}, bf16[128,1024]{1,0:T(8,128)(2,1)S(1)}, u32[]{:S(2)}, u32[]{:S(2)}) collective-permute-start(bf16[128,1024]{1,0:T(8,128)(2,1)S(1)} %get-tuple-element.21), channel_id=1, source_target_pairs={{0,2},{1,3},{2,0},{3,1},{4,6},{5,7},{6,4},{7,5},{8,10},{9,11},{10,... | collective-permute-start | bytes 786440 | tf_op jit(solution)/shard_map/ppermute | solution.py:384
  124.3 15.2 %copy-start = (f32[1,128,2048]{2,1,0:T(8,128)S(1)}, f32[1,128,2048]{2,1,0:T(8,128)}, u32[]{:S(2)}) copy-start(f32[1,128,2048]{2,1,0:T(8,128)} %param.8) | copy-start | bytes 3145732
  124.3 15.1 %copy-start.5 = (bf16[1,128,2048]{2,1,0:T(8,128)(2,1)S(1)}, bf16[1,128,2048]{2,1,0:T(8,128)(2,1)}, u32[]{:S(2)}) copy-start(bf16[1,128,2048]{2,1,0:T(8,128)(2,1)} %param.7) | copy-start | bytes 1572868

commit v7 on v5

--- a/solution.py
+++ b/solution.py
@@ -210,8 +210,8 @@
         both = jnp.concatenate([own_weights[place, high], other_weights[place, high]], axis=1)
         found = jnp.dot(mixed, both, preferred_element_type=jnp.float32)
         start = tile * 2 * LANES
-        store(pl.multiple_of(start + core * LANES, LANES), found[:, :LANES])
-        store(pl.multiple_of(start + (1 - core) * LANES, LANES), found[:, LANES:])
+        store(tile, pl.multiple_of(start + core * LANES, LANES), found[:, :LANES])
+        store(tile, pl.multiple_of(start + (1 - core) * LANES, LANES), found[:, LANES:])
 
 
 def attend_rows(offsets, lengths_ref, place_ref, before, after, priors, kv, scores, state, mixed, sems):
@@ -271,40 +271,58 @@
     )
 
 
-def project_kernel(place_ref, own_weights, other_weights, mixed, out_ref):
-    def store(start, value):
+HALF = D // 2
+
+
+def project_kernel(place_ref, own_weights, other_weights, mixed, first_ref, second_ref):
+    def store(tile, start, value):
+        out_ref = first_ref if tile < 4 else second_ref
+        start = pl.multiple_of(start - tile // 4 * HALF, LANES)
         out_ref[:, pl.ds(start, LANES)] = value.astype(out_ref.dtype)
 
     project(mixed[...], place_ref[2], own_weights, other_weights, store)
 
 
 def rows_kernel(
-    offsets, lengths_ref, place_ref, own_weights, other_weights, before, after, *rest
+    offset, lengths_ref, place_ref, own_weights, other_weights, before, after, prior, *rest
 ):
-    count = len(offsets)
-    priors, outs, scratch = rest[:count], rest[count : 2 * count], rest[2 * count :]
-    kv, scores, state, sems, mixed = scratch
+    passed, (out_ref, kv, scores, state, sems, mixed) = rest[:-6], rest[-6:]
     attend_rows(
-        offsets, lengths_ref, place_ref, before, after, priors, kv, scores, state, mixed, sems
-    )
-
-    def store(start, value):
-        for i, out_ref in enumerate(outs):
-            part = value[i * TOKENS : (i + 1) * TOKENS]
-            out_ref[:, pl.ds(start, LANES)] = part.astype(out_ref.dtype)
+        (offset,), lengths_ref, place_ref, before, after, (prior,), kv, scores, state, mixed, sems
+    )
+
+    def store(tile, start, value):
+        if passed and tile >= 4:
+            more = passed[0][:, pl.ds(pl.multiple_of(start - HALF, LANES), LANES)]
+            value = value + more.astype(jnp.float32)
+        out_ref[:, pl.ds(start, LANES)] = value.astype(out_ref.dtype)
 
     project(mixed[...], place_ref[2], own_weights, other_weights, store)
 
 
-def finish_kernel(own_ref, one_ref, two_ref, three_ref, resid_ref, earlier_ref, out_ref):
-    branch = own_ref[...] + one_ref[...].astype(jnp.float32)
-    branch = branch + two_ref[...].astype(jnp.float32)
-    branch = branch + three_ref[...].astype(jnp.float32)
-    summed = resid_ref[...].astype(jnp.float32) + branch * (1.0 / math.sqrt(D))
-    centered = summed - jnp.mean(summed, axis=1, keepdims=True)
-    spread = jnp.mean(centered * centered, axis=1, keepdims=True)
-    normed = centered * lax.rsqrt(spread + norm_epsilon)
-    out_ref[...] = (earlier_ref[...] + normed) * (1.0 / TOP_K)
+def finish_kernel(own_ref, far_ref, up_ref, down_ref, resid_ref, earlier_ref, out_hbm, out, sems):
+    def deliver(step):
+        rows = pl.ds(pl.multiple_of(step * PACKED, PACKED), PACKED)
+        return pltpu.make_async_copy(out.at[rows], out_hbm.at[rows], sems.at[step])
+
+    def finish(step, carry):
+        rows = pl.ds(pl.multiple_of(step * PACKED, PACKED), PACKED)
+        far = far_ref[rows].astype(jnp.float32)
+        branch = own_ref[rows] + jnp.concatenate([far, jnp.zeros_like(far)], axis=1)
+        branch = branch + up_ref[rows].astype(jnp.float32)
+        branch = branch + down_ref[rows].astype(jnp.float32)
+        summed = resid_ref[rows].astype(jnp.float32) + branch * (1.0 / math.sqrt(D))
+        centered = summed - jnp.mean(summed, axis=1, keepdims=True)
+        spread = jnp.mean(centered * centered, axis=1, keepdims=True)
+        normed = centered * lax.rsqrt(spread + norm_epsilon)
+        out[rows] = (earlier_ref[rows] + normed) * (1.0 / TOP_K)
+        deliver(step).start()
+        return carry
+
+    steps = TOKENS // PACKED
+    lax.fori_loop(0, steps, finish, 0)
+    for step in range(steps):
+        deliver(step).wait()
 
 
 vmem = pl.BlockSpec(memory_space=pltpu.VMEM)
@@ -391,21 +409,17 @@
         name="local",
     )(lengths, place, *pieces)
 
-    def rows_of(offsets, dtype):
-        count = len(offsets)
+    def rows_of(offset, dtype, *passed):
         return pl.pallas_call(
-            functools.partial(rows_kernel, offsets),
-            out_shape=(array(TOKENS, D, dtype=dtype),) * count,
-            in_specs=[smem, smem, vmem, vmem, anywhere, anywhere] + [vmem] * count,
-            out_specs=(vmem,) * count,
-            scratch_shapes=rows_scratch + [pltpu.VMEM((count * TOKENS, WIDTH), jnp.bfloat16)],
+            functools.partial(rows_kernel, offset),
+            out_shape=array(TOKENS, D, dtype=dtype),
+            in_specs=[smem, smem, vmem, vmem, anywhere, anywhere, vmem] + [vmem] * len(passed),
+            out_specs=vmem,
+            scratch_shapes=rows_scratch + [pltpu.VMEM((TOKENS, WIDTH), jnp.bfloat16)],
             compiler_params=limit(ROWS_LIMIT),
-            cost_estimate=cost(count << 29, 4 << 20, count << 20),
+            cost_estimate=cost(1 << 29, 4 << 20, 1 << 20),
             name="rows",
-        )(
-            lengths, place, own_weights, other_weights, before, after,
-            *[local[offset] for offset in offsets],
-        )
+        )(lengths, place, own_weights, other_weights, before, after, local[offset], *passed)
 
     mixed = pl.pallas_call(
         functools.partial(attend_kernel, (2,)),
@@ -417,27 +431,31 @@
         cost_estimate=cost(1 << 28, 3 << 20, 1 << 20),
         name="attend",
     )(lengths, place, before, after, local[2])
-    far = pl.pallas_call(
+    far, passed = pl.pallas_call(
         project_kernel,
-        out_shape=array(TOKENS, D),
+        out_shape=(array(TOKENS, HALF),) * 2,
         in_specs=[smem, vmem, vmem, vmem],
-        out_specs=vmem,
+        out_specs=(vmem,) * 2,
         compiler_params=limit(8),
         cost_estimate=cost(2 * TOKENS * WIDTH * D, 3 << 20),
         name="project",
     )(place, own_weights, other_weights, mixed)
+    passed = shift(passed, 1)
     far = shift(far, 2)
-    up, down = rows_of((1, 3), jnp.bfloat16)
+    down = rows_of(3, jnp.bfloat16)
+    down = shift(down, 3)
+    up = rows_of(1, jnp.bfloat16, passed)
     up = shift(up, 1)
-    down = shift(down, 3)
-    (own,) = rows_of((0,), jnp.float32)
-    rows = pl.BlockSpec((32, D), lambda i: (i, 0))
+    own = rows_of(0, jnp.float32)
     targets = pl.pallas_call(
         finish_kernel,
-        grid=(4,),
         out_shape=array(TOKENS, D, dtype=jnp.float32),
-        in_specs=[rows] * 6,
-        out_specs=rows,
+        in_specs=[vmem] * 6,
+        out_specs=anywhere,
+        scratch_shapes=[
+            pltpu.VMEM((TOKENS, D), jnp.float32),
+            pltpu.SemaphoreType.DMA((TOKENS // PACKED,)),
+        ],
         compiler_params=limit(12),
         cost_estimate=cost(1 << 22, 5 << 20),
         name="finish",

time: 141 us -> 141 us (level)
  the two profiles are of different devices: /device:TPU:56 before, /device:TPU:4 now
where the time goes in v7:
time: 141 us
  waiting for transfers between devices  40.2 us (29%)
  starting transfers between devices  38.6 us (27%)
  blocking collectives  33.4 us (24%)
  Pallas kernels  22.5 us (16%)
  local copies, waits for them, and re-layouts  3.26 us (2%)
  other arithmetic  1.85 us (1%)
    ppermute x10, waiting for transfers between devices, shift(): lax.ppermute(value, axis, [(i, (i + amount) % size) for i in range(size)])  40.2 us
    ppermute x10, starting transfers between devices, shift(): lax.ppermute(value, axis, [(i, (i + amount) % size) for i in range(size)])  33.8 us
    all_to_all x1, blocking collectives, block(): lax.all_to_all(jnp.broadcast_to(teacher_new[None], (16,) + teacher_new.sh...  33.4 us
    pallas_call x1, Pallas kernels, block(): pl.pallas_call(local_kernel, out_shape=(array(*handed, dtype=jnp.float32)...  10.4 us
    pallas_call x3, Pallas kernels, rows_of(): pl.pallas_call(functools.partial(rows_kernel, offset), out_shape=array(TO...  5.62 us
    all_to_all x1, starting transfers between devices, block(): lax.all_to_all(jnp.broadcast_to(ring_weights[None], (4,) + ring_weights.s...  4.8 us
  transfers between devices with their start and end apart: 11, of which 8 were waited for; matrix products, arithmetic and copies ran while one was open for 1% of the time, Pallas kernels for 14%

profile of v7, /device:TPU:4, one launch (start us, length us, event | category | flops | bytes accessed | tf_op | source)
XLA Modules:
  0.0 140.7 jit_solution(11385877881506327979)
XLA Ops:
  1.4 33.4 %all_to_all.10 = bf16[16,64,128]{2,1,0:T(8,128)(2,1)S(1)} all-to-all(bf16[16,64,128]{2,1,0:T(8,128)(2,1)S(1)} %broadcast_in_dim.16), channel_id=1, replica_groups=mesh['h'=2,'x'=4,'c'=2,'z'=8,'y'=4] {'h','z'}, dimensions={0} | all-to-all | bytes 524288 | tf_op jit(solution)/shard_map/all_to_all | solution.py:392
  34.8 1.1 broadcast_in_dim.18
  35.9 4.8 %all-to-all-start.1 = ((bf16[4,2,512,128]{3,2,1,0:T(8,128)(2,1)}), bf16[4,2,512,128]{3,2,1,0:T(8,128)(2,1)S(1)}, u32[]{:S(2)}, u32[]{:S(2)}) async-start(bf16[4,2,512,128]{3,2,1,0:T(8,128)(2,1)} %broadcast_in_dim.18), calls=%async_computation.1 | async-start | bytes 2097152 | tf_op jit(solution)/shard_map/all_to_all | solution.py:396
  40.8 2.2 %pack.1 = (bf16[128,1536]{1,0:T(8,128)(2,1)S(1)}, bf16[128,1536]{1,0:T(8,128)(2,1)S(1)}, bf16[128,1536]{1,0:T(8,128)(2,1)S(1)}, bf16[128,1536]{1,0:T(8,128)(2,1)S(1)}) custom-call(s32[3]{0:T(128)S(1)} %pad_add_fusion.place_ref, bf16[128,6144]{1,0:T(8,128)(2,1)S(1)} %bitcast.8), custom_call_target="tpu_custom_call" | custom-call | bytes 3145728 | tf_op jit(solution)/shard_map/pack/pallas_call | solution.py:382
  43.0 4.9 %collective-permute-start.1 = (bf16[128,1536]{1,0:T(8,128)(2,1)S(1)}, bf16[128,1536]{1,0:T(8,128)(2,1)S(1)}, u32[]{:S(2)}, u32[]{:S(2)}) collective-permute-start(bf16[128,1536]{1,0:T(8,128)(2,1)S(1)} %get-tuple-element.13), channel_id=1, source_target_pairs={{0,3},{1,0},{2,1},{3,2},{4,7},{5,4},{6,5},{7,6},{8,11},{9,8},{10,9... | collective-permute-start | bytes 1179656 | tf_op jit(solution)/shard_map/ppermute | solution.py:362
  48.0 2.5 %collective-permute-start.2 = (bf16[128,1536]{1,0:T(8,128)(2,1)S(1)}, bf16[128,1536]{1,0:T(8,128)(2,1)S(1)}, u32[]{:S(2)}, u32[]{:S(2)}) collective-permute-start(bf16[128,1536]{1,0:T(8,128)(2,1)S(1)} %get-tuple-element.14), channel_id=1, source_target_pairs={{0,2},{1,3},{2,0},{3,1},{4,6},{5,7},{6,4},{7,5},{8,10},{9,11},{10,... | collective-permute-start | bytes 1179656 | tf_op jit(solution)/shard_map/ppermute | solution.py:362
  50.5 2.9 %collective-permute-start.3 = (bf16[128,1536]{1,0:T(8,128)(2,1)S(1)}, bf16[128,1536]{1,0:T(8,128)(2,1)S(1)}, u32[]{:S(2)}, u32[]{:S(2)}) collective-permute-start(bf16[128,1536]{1,0:T(8,128)(2,1)S(1)} %get-tuple-element.15), channel_id=1, source_target_pairs={{0,1},{1,2},{2,3},{3,0},{4,5},{5,6},{6,7},{7,4},{8,9},{9,10},{10,1... | collective-permute-start | bytes 1179656 | tf_op jit(solution)/shard_map/ppermute | solution.py:362
  53.4 5.9 %collective-permute-done.1.next_piece = bf16[128,1536]{1,0:T(8,128)(2,1)S(1)} collective-permute-done((bf16[128,1536]{1,0:T(8,128)(2,1)S(1)}, bf16[128,1536]{1,0:T(8,128)(2,1)S(1)}, u32[]{:S(2)}, u32[]{:S(2)}) %collective-permute-start.1) | collective-permute-done | bytes 393248 | tf_op jit(solution)/shard_map/ppermute | solution.py:362
  59.3 1.5 %collective-permute-done.2.far = bf16[128,1536]{1,0:T(8,128)(2,1)S(1)} collective-permute-done((bf16[128,1536]{1,0:T(8,128)(2,1)S(1)}, bf16[128,1536]{1,0:T(8,128)(2,1)S(1)}, u32[]{:S(2)}, u32[]{:S(2)}) %collective-permute-start.2) | collective-permute-done | bytes 393248 | tf_op jit(solution)/shard_map/ppermute | solution.py:362
  60.9 4.0 %collective-permute-done.3.last = bf16[128,1536]{1,0:T(8,128)(2,1)S(1)} collective-permute-done((bf16[128,1536]{1,0:T(8,128)(2,1)S(1)}, bf16[128,1536]{1,0:T(8,128)(2,1)S(1)}, u32[]{:S(2)}, u32[]{:S(2)}) %collective-permute-start.3) | collective-permute-done | bytes 393248 | tf_op jit(solution)/shard_map/ppermute | solution.py:362
  64.9 0.8 copy-done.13
  65.7 1.0 pad_maximum_fusion
  66.7 7.5 %collective-permute-start.4 = (bf16[512,1024]{1,0:T(8,128)(2,1)}, bf16[512,1024]{1,0:T(8,128)(2,1)S(1)}, u32[]{:S(2)}, u32[]{:S(2)}) collective-permute-start(bf16[512,1024]{1,0:T(8,128)(2,1)} %pad_maximum_fusion), channel_id=1, source_target_pairs={{0,4},{4,8},{8,12},{12,16},{16,20},{20,24},{24,28},{28,256},{256,2... | collective-permute-start | bytes 3145736 | tf_op jit(solution)/shard_map/ppermute | solution.py:362
  74.2 2.2 %collective-permute-start.5 = (bf16[512,1024]{1,0:T(8,128)(2,1)}, bf16[512,1024]{1,0:T(8,128)(2,1)S(1)}, u32[]{:S(2)}, u32[]{:S(2)}) collective-permute-start(bf16[512,1024]{1,0:T(8,128)(2,1)} %pad_maximum_fusion), channel_id=1, source_target_pairs={{0,284},{4,0},{8,4},{12,8},{16,12},{20,16},{24,20},{28,24},{256,28... | collective-permute-start | bytes 3145736 | tf_op jit(solution)/shard_map/ppermute | solution.py:362
  76.4 1.9 %collective-permute-start = (bf16[4,2,512,128]{3,2,1,0:T(8,128)(2,1)S(1)}, bf16[4,2,512,128]{3,2,1,0:T(8,128)(2,1)S(1)}, u32[]{:S(2)}, u32[]{:S(2)}) collective-permute-start(bf16[4,2,512,128]{3,2,1,0:T(8,128)(2,1)S(1)} %all-to-all-done.1.own_weights), channel_id=1, source_target_pairs={{0,32},{32,0},{1,33},{33,1},{2,34},{34,2},{3,35},{35,3},{4,36},{36... | collective-permute-start | bytes 3145736 | tf_op jit(solution)/shard_map/ppermute | solution.py:362
  78.3 10.4 %local.1 = (f32[16,128,128]{2,1,0:T(8,128)}, f32[16,128,128]{2,1,0:T(8,128)}, f32[16,128,128]{2,1,0:T(8,128)}, f32[16,128,128]{2,1,0:T(8,128)}) custom-call(s32[1,12]{1,0:T(1,128)} %lengths_ref.9, s32[3]{0:T(128)} %copy-done.8, bf16[128,1536]{1,0:T(8,128)(2,1)} %copy-done.7, bf16[128,1536]{1,0:T(8,128)(2,1)} %copy-done.11, bf16[128,1536]{1,0:T(8,128)(2,1)} %copy-done.12, ...), custom_call_target="tpu_custom_call" | custom-call | flops 1073741824 | bytes 8388608 | tf_op jit(solution)/shard_map/local/pallas_call | solution.py:401
  88.7 8.4 %collective-permute-done.4.before = bf16[512,1024]{1,0:T(8,128)(2,1)S(1)} collective-permute-done((bf16[512,1024]{1,0:T(8,128)(2,1)}, bf16[512,1024]{1,0:T(8,128)(2,1)S(1)}, u32[]{:S(2)}, u32[]{:S(2)}) %collective-permute-start.4) | collective-permute-done | bytes 1048608 | tf_op jit(solution)/shard_map/ppermute | solution.py:362
  97.1 4.0 %collective-permute-done.5.after = bf16[512,1024]{1,0:T(8,128)(2,1)S(1)} collective-permute-done((bf16[512,1024]{1,0:T(8,128)(2,1)}, bf16[512,1024]{1,0:T(8,128)(2,1)S(1)}, u32[]{:S(2)}, u32[]{:S(2)}) %collective-permute-start.5) | collective-permute-done | bytes 1048608 | tf_op jit(solution)/shard_map/ppermute | solution.py:362
  101.1 1.2 copy-done.3
  102.3 1.4 %attend.1.mixed = bf16[128,512]{1,0:T(8,128)(2,1)S(1)} custom-call(s32[1,12]{1,0:T(1,128)S(1)} %copy-done.10, s32[3]{0:T(128)S(1)} %copy-done.9, bf16[512,1024]{1,0:T(8,128)(2,1)S(1)} %collective-permute-done.4.before, bf16[512,1024]{1,0:T(8,128)(2,1)S(1)} %collective-permute-done.5.after, f32[16,128,128]{2,1,0:T(8,128)S(1)} %copy-done.3), custom_call_target="tpu_custom_call" | custom-call | flops 268435456 | bytes 3145728 | tf_op jit(solution)/shard_map/attend/pallas_call | solution.py:424
  103.8 1.0 project.1
  104.8 1.9 %collective-permute-start.7 = (bf16[128,1024]{1,0:T(8,128)(2,1)S(1)}, bf16[128,1024]{1,0:T(8,128)(2,1)S(1)}, u32[]{:S(2)}, u32[]{:S(2)}) collective-permute-start(bf16[128,1024]{1,0:T(8,128)(2,1)S(1)} %get-tuple-element.20), channel_id=1, source_target_pairs={{0,1},{1,2},{2,3},{3,0},{4,5},{5,6},{6,7},{7,4},{8,9},{9,10},{10,1... | collective-permute-start | bytes 786440 | tf_op jit(solution)/shard_map/ppermute | solution.py:362
  106.8 1.9 %rows.5 = bf16[128,2048]{1,0:T(8,128)(2,1)S(1)} custom-call(s32[1,12]{1,0:T(1,128)S(1)} %copy-done.10, s32[3]{0:T(128)S(1)} %copy-done.9, bf16[4,2,512,128]{3,2,1,0:T(8,128)(2,1)S(1)} %all-to-all-done.1.own_weights, bf16[4,2,512,128]{3,2,1,0:T(8,128)(2,1)S(1)} %collective-permute-done.other_weights, bf16[512,1024]{1,0:T(8,128)(2,1)S(1)} %collective-permute-done.4.before, ...), custom_call_target="tpu_custom_call" | custom-call | flops 536870912 | bytes 4194304 | tf_op jit(solution)/shard_map/rows/pallas_call | solution.py:413
  108.7 5.1 %collective-permute-start.9 = (bf16[128,2048]{1,0:T(8,128)(2,1)S(1)}, bf16[128,2048]{1,0:T(8,128)(2,1)S(1)}, u32[]{:S(2)}, u32[]{:S(2)}) collective-permute-start(bf16[128,2048]{1,0:T(8,128)(2,1)S(1)} %rows.5), channel_id=1, source_target_pairs={{0,3},{1,0},{2,1},{3,2},{4,7},{5,4},{6,5},{7,6},{8,11},{9,8},{10,9... | collective-permute-start | bytes 1572872 | tf_op jit(solution)/shard_map/ppermute | solution.py:362
  113.8 1.9 %collective-permute-done.7.rest_0_ = bf16[128,1024]{1,0:T(8,128)(2,1)S(1)} collective-permute-done((bf16[128,1024]{1,0:T(8,128)(2,1)S(1)}, bf16[128,1024]{1,0:T(8,128)(2,1)S(1)}, u32[]{:S(2)}, u32[]{:S(2)}) %collective-permute-start.7) | collective-permute-done | bytes 262176 | tf_op jit(solution)/shard_map/ppermute | solution.py:362
  115.7 1.9 %rows.4 = bf16[128,2048]{1,0:T(8,128)(2,1)S(1)} custom-call(s32[1,12]{1,0:T(1,128)S(1)} %copy-done.10, s32[3]{0:T(128)S(1)} %copy-done.9, bf16[4,2,512,128]{3,2,1,0:T(8,128)(2,1)S(1)} %all-to-all-done.1.own_weights, bf16[4,2,512,128]{3,2,1,0:T(8,128)(2,1)S(1)} %collective-permute-done.other_weights, bf16[512,1024]{1,0:T(8,128)(2,1)S(1)} %collective-permute-done.4.before, ...), custom_call_target="tpu_custom_call" | custom-call | flops 536870912 | bytes 4194304 | tf_op jit(solution)/shard_map/rows/pallas_call | solution.py:413
  117.6 1.9 %collective-permute-start.8 = (bf16[128,2048]{1,0:T(8,128)(2,1)S(1)}, bf16[128,2048]{1,0:T(8,128)(2,1)S(1)}, u32[]{:S(2)}, u32[]{:S(2)}) collective-permute-start(bf16[128,2048]{1,0:T(8,128)(2,1)S(1)} %rows.4), channel_id=1, source_target_pairs={{0,1},{1,2},{2,3},{3,0},{4,5},{5,6},{6,7},{7,4},{8,9},{9,10},{10,1... | collective-permute-start | bytes 1572872 | tf_op jit(solution)/shard_map/ppermute | solution.py:362
  119.5 2.9 %collective-permute-start.6 = (bf16[128,1024]{1,0:T(8,128)(2,1)S(1)}, bf16[128,1024]{1,0:T(8,128)(2,1)S(1)}, u32[]{:S(2)}, u32[]{:S(2)}) collective-permute-start(bf16[128,1024]{1,0:T(8,128)(2,1)S(1)} %get-tuple-element.18), channel_id=1, source_target_pairs={{0,2},{1,3},{2,0},{3,1},{4,6},{5,7},{6,4},{7,5},{8,10},{9,11},{10,... | collective-permute-start | bytes 786440 | tf_op jit(solution)/shard_map/ppermute | solution.py:362
  122.4 1.9 %rows.3.own_ref = f32[128,2048]{1,0:T(8,128)S(1)} custom-call(s32[1,12]{1,0:T(1,128)S(1)} %copy-done.10, s32[3]{0:T(128)S(1)} %copy-done.9, bf16[4,2,512,128]{3,2,1,0:T(8,128)(2,1)S(1)} %all-to-all-done.1.own_weights, bf16[4,2,512,128]{3,2,1,0:T(8,128)(2,1)S(1)} %collective-permute-done.other_weights, bf16[512,1024]{1,0:T(8,128)(2,1)S(1)} %collective-permute-done.4.before, ...), custom_call_target="tpu_custom_call" | custom-call | flops 536870912 | bytes 4194304 | tf_op jit(solution)/shard_map/rows/pallas_call | solution.py:413
  124.3 12.4 %collective-permute-done.6.far_ref = bf16[128,1024]{1,0:T(8,128)(2,1)S(1)} collective-permute-done((bf16[128,1024]{1,0:T(8,128)(2,1)S(1)}, bf16[128,1024]{1,0:T(8,128)(2,1)S(1)}, u32[]{:S(2)}, u32[]{:S(2)}) %collective-permute-start.6) | collective-permute-done | bytes 262176 | tf_op jit(solution)/shard_map/ppermute | solution.py:362
  136.7 2.1 %collective-permute-done.8.up_ref = bf16[128,2048]{1,0:T(8,128)(2,1)S(1)} collective-permute-done((bf16[128,2048]{1,0:T(8,128)(2,1)S(1)}, bf16[128,2048]{1,0:T(8,128)(2,1)S(1)}, u32[]{:S(2)}, u32[]{:S(2)}) %collective-permute-start.8) | collective-permute-done | bytes 524320 | tf_op jit(solution)/shard_map/ppermute | solution.py:362
  138.8 1.9 %finish.1 = f32[128,2048]{1,0:T(8,128)} custom-call(f32[128,2048]{1,0:T(8,128)S(1)} %rows.3.own_ref, bf16[128,1024]{1,0:T(8,128)(2,1)S(1)} %collective-permute-done.6.far_ref, bf16[128,2048]{1,0:T(8,128)(2,1)S(1)} %collective-permute-done.8.up_ref, bf16[128,2048]{1,0:T(8,128)(2,1)S(1)} %collective-permute-done.9.down_ref, bf16[128,2048]{1,0:T(8,128)(2,1)S(1)} %bitcast.10, ...), custom_call_target="tpu_custom_call" | custom-call | flops 4194304 | bytes 5242880 | tf_op jit(solution)/shard_map/finish/pallas_call | solution.py:450
  (38 shorter events, 1.0 us)
Async XLA Ops:
  1.4 33.4 %copy-start.14 = (bf16[64,128]{1,0:T(8,128)(2,1)}, bf16[64,128]{1,0:T(8,128)(2,1)S(1)}, u32[]{:S(2)}) copy-start(bf16[64,128]{1,0:T(8,128)(2,1)S(1)} %add_convert_fusion) | copy-start | bytes 49156
  34.8 6.0 %copy-start = (bf16[1,128,6144]{2,1,0:T(8,128)(2,1)S(1)}, bf16[1,128,6144]{2,1,0:T(8,128)(2,1)}, u32[]{:S(2)}) copy-start(bf16[1,128,6144]{2,1,0:T(8,128)(2,1)} %param.6) | copy-start | bytes 4718596
  35.9 40.5 %all-to-all-start.1 = ((bf16[4,2,512,128]{3,2,1,0:T(8,128)(2,1)}), bf16[4,2,512,128]{3,2,1,0:T(8,128)(2,1)S(1)}, u32[]{:S(2)}, u32[]{:S(2)}) async-start(bf16[4,2,512,128]{3,2,1,0:T(8,128)(2,1)} %broadcast_in_dim.18), calls=%async_computation.1 | async-start | bytes 2097152 | tf_op jit(solution)/shard_map/all_to_all | solution.py:396
  40.8 20.1 %copy-start.8 = (s32[3]{0:T(128)}, s32[3]{0:T(128)S(1)}, u32[]{:S(2)}) copy-start(s32[3]{0:T(128)S(1)} %pad_add_fusion.place_ref) | copy-start | bytes 40
  43.0 23.7 %copy-start.7 = (bf16[128,1536]{1,0:T(8,128)(2,1)}, bf16[128,1536]{1,0:T(8,128)(2,1)S(1)}, u32[]{:S(2)}) copy-start(bf16[128,1536]{1,0:T(8,128)(2,1)S(1)} %get-tuple-element.12.own) | copy-start | bytes 1179652
  43.0 16.3 %collective-permute-start.1 = (bf16[128,1536]{1,0:T(8,128)(2,1)S(1)}, bf16[128,1536]{1,0:T(8,128)(2,1)S(1)}, u32[]{:S(2)}, u32[]{:S(2)}) collective-permute-start(bf16[128,1536]{1,0:T(8,128)(2,1)S(1)} %get-tuple-element.13), channel_id=1, source_target_pairs={{0,3},{1,0},{2,1},{3,2},{4,7},{5,4},{6,5},{7,6},{8,11},{9,8},{10,9... | collective-permute-start | bytes 1179656 | tf_op jit(solution)/shard_map/ppermute | solution.py:362
  48.0 12.9 %collective-permute-start.2 = (bf16[128,1536]{1,0:T(8,128)(2,1)S(1)}, bf16[128,1536]{1,0:T(8,128)(2,1)S(1)}, u32[]{:S(2)}, u32[]{:S(2)}) collective-permute-start(bf16[128,1536]{1,0:T(8,128)(2,1)S(1)} %get-tuple-element.14), channel_id=1, source_target_pairs={{0,2},{1,3},{2,0},{3,1},{4,6},{5,7},{6,4},{7,5},{8,10},{9,11},{10,... | collective-permute-start | bytes 1179656 | tf_op jit(solution)/shard_map/ppermute | solution.py:362
  50.5 14.4 %collective-permute-start.3 = (bf16[128,1536]{1,0:T(8,128)(2,1)S(1)}, bf16[128,1536]{1,0:T(8,128)(2,1)S(1)}, u32[]{:S(2)}, u32[]{:S(2)}) collective-permute-start(bf16[128,1536]{1,0:T(8,128)(2,1)S(1)} %get-tuple-element.15), channel_id=1, source_target_pairs={{0,1},{1,2},{2,3},{3,0},{4,5},{5,6},{6,7},{7,4},{8,9},{9,10},{10,1... | collective-permute-start | bytes 1179656 | tf_op jit(solution)/shard_map/ppermute | solution.py:362
  59.3 7.4 %copy-start.11 = (bf16[128,1536]{1,0:T(8,128)(2,1)}, bf16[128,1536]{1,0:T(8,128)(2,1)S(1)}, u32[]{:S(2)}) copy-start(bf16[128,1536]{1,0:T(8,128)(2,1)S(1)} %collective-permute-done.1.next_piece) | copy-start | bytes 1179652
  60.8 4.1 %copy-start.12 = (bf16[128,1536]{1,0:T(8,128)(2,1)}, bf16[128,1536]{1,0:T(8,128)(2,1)S(1)}, u32[]{:S(2)}) copy-start(bf16[128,1536]{1,0:T(8,128)(2,1)S(1)} %collective-permute-done.2.far) | copy-start | bytes 1179652
  64.9 0.8 copy-start.13
  66.7 34.4 %copy-start.9 = (s32[3]{0:T(128)S(1)}, s32[3]{0:T(128)}, u32[]{:S(2)}) copy-start(s32[3]{0:T(128)} %copy-done.8) | copy-start | bytes 40
  66.7 34.4 %copy-start.10 = (s32[1,12]{1,0:T(1,128)S(1)}, s32[1,12]{1,0:T(1,128)}, u32[]{:S(2)}) copy-start(s32[1,12]{1,0:T(1,128)} %lengths_ref.9) | copy-start | bytes 148
  66.7 30.4 %collective-permute-start.4 = (bf16[512,1024]{1,0:T(8,128)(2,1)}, bf16[512,1024]{1,0:T(8,128)(2,1)S(1)}, u32[]{:S(2)}, u32[]{:S(2)}) collective-permute-start(bf16[512,1024]{1,0:T(8,128)(2,1)} %pad_maximum_fusion), channel_id=1, source_target_pairs={{0,4},{4,8},{8,12},{12,16},{16,20},{20,24},{24,28},{28,256},{256,2... | collective-permute-start | bytes 3145736 | tf_op jit(solution)/shard_map/ppermute | solution.py:362
  74.2 26.9 %collective-permute-start.5 = (bf16[512,1024]{1,0:T(8,128)(2,1)}, bf16[512,1024]{1,0:T(8,128)(2,1)S(1)}, u32[]{:S(2)}, u32[]{:S(2)}) collective-permute-start(bf16[512,1024]{1,0:T(8,128)(2,1)} %pad_maximum_fusion), channel_id=1, source_target_pairs={{0,284},{4,0},{8,4},{12,8},{16,12},{20,16},{24,20},{28,24},{256,28... | collective-permute-start | bytes 3145736 | tf_op jit(solution)/shard_map/ppermute | solution.py:362
  76.4 27.4 %collective-permute-start = (bf16[4,2,512,128]{3,2,1,0:T(8,128)(2,1)S(1)}, bf16[4,2,512,128]{3,2,1,0:T(8,128)(2,1)S(1)}, u32[]{:S(2)}, u32[]{:S(2)}) collective-permute-start(bf16[4,2,512,128]{3,2,1,0:T(8,128)(2,1)S(1)} %all-to-all-done.1.own_weights), channel_id=1, source_target_pairs={{0,32},{32,0},{1,33},{33,1},{2,34},{34,2},{3,35},{35,3},{4,36},{36... | collective-permute-start | bytes 3145736 | tf_op jit(solution)/shard_map/ppermute | solution.py:362
  101.1 1.2 copy-start.3
  103.8 3.0 %copy-start.5 = (f32[16,128,128]{2,1,0:T(8,128)S(1)}, f32[16,128,128]{2,1,0:T(8,128)}, u32[]{:S(2)}) copy-start(f32[16,128,128]{2,1,0:T(8,128)} %get-tuple-element.21.prior) | copy-start | bytes 3145732
  104.8 10.9 %collective-permute-start.7 = (bf16[128,1024]{1,0:T(8,128)(2,1)S(1)}, bf16[128,1024]{1,0:T(8,128)(2,1)S(1)}, u32[]{:S(2)}, u32[]{:S(2)}) collective-permute-start(bf16[128,1024]{1,0:T(8,128)(2,1)S(1)} %get-tuple-element.20), channel_id=1, source_target_pairs={{0,1},{1,2},{2,3},{3,0},{4,5},{5,6},{6,7},{7,4},{8,9},{9,10},{10,1... | collective-permute-start | bytes 786440 | tf_op jit(solution)/shard_map/ppermute | solution.py:362
  106.8 8.9 %copy-start.2 = (f32[16,128,128]{2,1,0:T(8,128)S(1)}, f32[16,128,128]{2,1,0:T(8,128)}, u32[]{:S(2)}) copy-start(f32[16,128,128]{2,1,0:T(8,128)} %get-tuple-element.19.prior) | copy-start | bytes 3145732
  108.7 28.0 %collective-permute-start.9 = (bf16[128,2048]{1,0:T(8,128)(2,1)S(1)}, bf16[128,2048]{1,0:T(8,128)(2,1)S(1)}, u32[]{:S(2)}, u32[]{:S(2)}) collective-permute-start(bf16[128,2048]{1,0:T(8,128)(2,1)S(1)} %rows.5), channel_id=1, source_target_pairs={{0,3},{1,0},{2,1},{3,2},{4,7},{5,4},{6,5},{7,6},{8,11},{9,8},{10,9... | collective-permute-start | bytes 1572872 | tf_op jit(solution)/shard_map/ppermute | solution.py:362
  115.7 6.7 %copy-start.4 = (f32[16,128,128]{2,1,0:T(8,128)S(1)}, f32[16,128,128]{2,1,0:T(8,128)}, u32[]{:S(2)}) copy-start(f32[16,128,128]{2,1,0:T(8,128)} %get-tuple-element.16.prior) | copy-start | bytes 3145732
  117.6 21.2 %collective-permute-start.8 = (bf16[128,2048]{1,0:T(8,128)(2,1)S(1)}, bf16[128,2048]{1,0:T(8,128)(2,1)S(1)}, u32[]{:S(2)}, u32[]{:S(2)}) collective-permute-start(bf16[128,2048]{1,0:T(8,128)(2,1)S(1)} %rows.4), channel_id=1, source_target_pairs={{0,1},{1,2},{2,3},{3,0},{4,5},{5,6},{6,7},{7,4},{8,9},{9,10},{10,1... | collective-permute-start | bytes 1572872 | tf_op jit(solution)/shard_map/ppermute | solution.py:362
  119.5 17.2 %collective-permute-start.6 = (bf16[128,1024]{1,0:T(8,128)(2,1)S(1)}, bf16[128,1024]{1,0:T(8,128)(2,1)S(1)}, u32[]{:S(2)}, u32[]{:S(2)}) collective-permute-start(bf16[128,1024]{1,0:T(8,128)(2,1)S(1)} %get-tuple-element.18), channel_id=1, source_target_pairs={{0,2},{1,3},{2,0},{3,1},{4,6},{5,7},{6,4},{7,5},{8,10},{9,11},{10,... | collective-permute-start | bytes 786440 | tf_op jit(solution)/shard_map/ppermute | solution.py:362
  122.4 16.4 %copy-start.1 = (f32[1,128,2048]{2,1,0:T(8,128)S(1)}, f32[1,128,2048]{2,1,0:T(8,128)}, u32[]{:S(2)}) copy-start(f32[1,128,2048]{2,1,0:T(8,128)} %param.8) | copy-start | bytes 3145732
  122.4 16.4 %copy-start.6 = (bf16[1,128,2048]{2,1,0:T(8,128)(2,1)S(1)}, bf16[1,128,2048]{2,1,0:T(8,128)(2,1)}, u32[]{:S(2)}) copy-start(bf16[1,128,2048]{2,1,0:T(8,128)(2,1)} %param.7) | copy-start | bytes 1572868

commit v8 on v5

--- a/solution.py
+++ b/solution.py
@@ -296,15 +296,28 @@
     project(mixed[...], place_ref[2], own_weights, other_weights, store)
 
 
-def finish_kernel(own_ref, one_ref, two_ref, three_ref, resid_ref, earlier_ref, out_ref):
-    branch = own_ref[...] + one_ref[...].astype(jnp.float32)
-    branch = branch + two_ref[...].astype(jnp.float32)
-    branch = branch + three_ref[...].astype(jnp.float32)
-    summed = resid_ref[...].astype(jnp.float32) + branch * (1.0 / math.sqrt(D))
-    centered = summed - jnp.mean(summed, axis=1, keepdims=True)
-    spread = jnp.mean(centered * centered, axis=1, keepdims=True)
-    normed = centered * lax.rsqrt(spread + norm_epsilon)
-    out_ref[...] = (earlier_ref[...] + normed) * (1.0 / TOP_K)
+def finish_kernel(own_ref, one_ref, two_ref, three_ref, resid_ref, earlier_ref, out_hbm, out, sems):
+    def deliver(step):
+        rows = pl.ds(pl.multiple_of(step * PACKED, PACKED), PACKED)
+        return pltpu.make_async_copy(out.at[rows], out_hbm.at[rows], sems.at[step])
+
+    def finish(step, carry):
+        rows = pl.ds(pl.multiple_of(step * PACKED, PACKED), PACKED)
+        branch = own_ref[rows] + one_ref[rows].astype(jnp.float32)
+        branch = branch + two_ref[rows].astype(jnp.float32)
+        branch = branch + three_ref[rows].astype(jnp.float32)
+        summed = resid_ref[rows].astype(jnp.float32) + branch * (1.0 / math.sqrt(D))
+        centered = summed - jnp.mean(summed, axis=1, keepdims=True)
+        spread = jnp.mean(centered * centered, axis=1, keepdims=True)
+        normed = centered * lax.rsqrt(spread + norm_epsilon)
+        out[rows] = (earlier_ref[rows] + normed) * (1.0 / TOP_K)
+        deliver(step).start()
+        return carry
+
+    steps = TOKENS // PACKED
+    lax.fori_loop(0, steps, finish, 0)
+    for step in range(steps):
+        deliver(step).wait()
 
 
 vmem = pl.BlockSpec(memory_space=pltpu.VMEM)
@@ -431,13 +444,15 @@
     up = shift(up, 1)
     down = shift(down, 3)
     (own,) = rows_of((0,), jnp.float32)
-    rows = pl.BlockSpec((32, D), lambda i: (i, 0))
     targets = pl.pallas_call(
         finish_kernel,
-        grid=(4,),
         out_shape=array(TOKENS, D, dtype=jnp.float32),
-        in_specs=[rows] * 6,
-        out_specs=rows,
+        in_specs=[vmem] * 6,
+        out_specs=anywhere,
+        scratch_shapes=[
+            pltpu.VMEM((TOKENS, D), jnp.float32),
+            pltpu.SemaphoreType.DMA((TOKENS // PACKED,)),
+        ],
         compiler_params=limit(12),
         cost_estimate=cost(1 << 22, 5 << 20),
         name="finish",

time: 141 us -> 141 us (level)
  no operation moved by 1% of the time
where the time goes in v8:
time: 141 us; the launch traced here: 140 us
  waiting for transfers between devices  41.8 us (30%)
  starting transfers between devices  33.4 us (24%)
  blocking collectives  32.9 us (23%)
  Pallas kernels  25.7 us (18%)
  local copies, waits for them, and re-layouts  3.86 us (3%)
  other arithmetic  1.85 us (1%)
    ppermute x9, waiting for transfers between devices, shift(): lax.ppermute(value, axis, [(i, (i + amount) % size) for i in range(size)])  41.8 us
    all_to_all x1, blocking collectives, block(): lax.all_to_all(jnp.broadcast_to(teacher_new[None], (16,) + teacher_new.sh...  32.9 us
    ppermute x9, starting transfers between devices, shift(): lax.ppermute(value, axis, [(i, (i + amount) % size) for i in range(size)])  29.1 us
    pallas_call x1, Pallas kernels, block(): pl.pallas_call(local_kernel, out_shape=(array(*handed, dtype=jnp.float32)...  9.76 us
    pallas_call x2, Pallas kernels, rows_of(): pl.pallas_call(functools.partial(rows_kernel, offsets), out_shape=(array(...  8.67 us
    all_to_all x1, starting transfers between devices, block(): lax.all_to_all(jnp.broadcast_to(ring_weights[None], (4,) + ring_weights.s...  4.29 us
  transfers between devices with their start and end apart: 10, of which 6 were waited for; matrix products, arithmetic and copies ran while one was open for 1% of the time, Pallas kernels for 13%

profile of v8, /device:TPU:56, one launch (start us, length us, event | category | flops | bytes accessed | tf_op | source)
XLA Modules:
  0.0 140.4 jit_solution(4577476028070876077)
XLA Ops:
  0.6 0.7 add_convert_fusion
  1.4 0.0 copy-start.14
  1.4 0.6 copy-done.14
  2.0 32.9 %all_to_all.10 = bf16[16,64,128]{2,1,0:T(8,128)(2,1)S(1)} all-to-all(bf16[16,64,128]{2,1,0:T(8,128)(2,1)S(1)} %broadcast_in_dim.16), channel_id=1, replica_groups=mesh['h'=2,'x'=4,'c'=2,'z'=8,'y'=4] {'h','z'}, dimensions={0} | all-to-all | bytes 524288 | tf_op jit(solution)/shard_map/all_to_all | solution.py:387
  35.0 1.1 broadcast_in_dim.18
  36.1 4.3 %all-to-all-start.1 = ((bf16[4,2,512,128]{3,2,1,0:T(8,128)(2,1)}), bf16[4,2,512,128]{3,2,1,0:T(8,128)(2,1)S(1)}, u32[]{:S(2)}, u32[]{:S(2)}) async-start(bf16[4,2,512,128]{3,2,1,0:T(8,128)(2,1)} %broadcast_in_dim.18), calls=%async_computation.1 | async-start | bytes 2097152 | tf_op jit(solution)/shard_map/all_to_all | solution.py:391
  40.4 0.1 pad_add_fusion.place_ref
  40.4 2.2 %pack.1 = (bf16[128,1536]{1,0:T(8,128)(2,1)S(1)}, bf16[128,1536]{1,0:T(8,128)(2,1)S(1)}, bf16[128,1536]{1,0:T(8,128)(2,1)S(1)}, bf16[128,1536]{1,0:T(8,128)(2,1)S(1)}) custom-call(s32[3]{0:T(128)S(1)} %pad_add_fusion.place_ref, bf16[128,6144]{1,0:T(8,128)(2,1)S(1)} %bitcast.8), custom_call_target="tpu_custom_call" | custom-call | bytes 3145728 | tf_op jit(solution)/shard_map/pack/pallas_call | solution.py:377
  42.7 2.7 %collective-permute-start.1 = (bf16[128,1536]{1,0:T(8,128)(2,1)S(1)}, bf16[128,1536]{1,0:T(8,128)(2,1)S(1)}, u32[]{:S(2)}, u32[]{:S(2)}) collective-permute-start(bf16[128,1536]{1,0:T(8,128)(2,1)S(1)} %get-tuple-element.13), channel_id=1, source_target_pairs={{0,3},{1,0},{2,1},{3,2},{4,7},{5,4},{6,5},{7,6},{8,11},{9,8},{10,9... | collective-permute-start | bytes 1179656 | tf_op jit(solution)/shard_map/ppermute | solution.py:357
  45.3 2.8 %collective-permute-start.2 = (bf16[128,1536]{1,0:T(8,128)(2,1)S(1)}, bf16[128,1536]{1,0:T(8,128)(2,1)S(1)}, u32[]{:S(2)}, u32[]{:S(2)}) collective-permute-start(bf16[128,1536]{1,0:T(8,128)(2,1)S(1)} %get-tuple-element.14), channel_id=1, source_target_pairs={{0,2},{1,3},{2,0},{3,1},{4,6},{5,7},{6,4},{7,5},{8,10},{9,11},{10,... | collective-permute-start | bytes 1179656 | tf_op jit(solution)/shard_map/ppermute | solution.py:357
  48.2 4.1 %collective-permute-start.3 = (bf16[128,1536]{1,0:T(8,128)(2,1)S(1)}, bf16[128,1536]{1,0:T(8,128)(2,1)S(1)}, u32[]{:S(2)}, u32[]{:S(2)}) collective-permute-start(bf16[128,1536]{1,0:T(8,128)(2,1)S(1)} %get-tuple-element.15), channel_id=1, source_target_pairs={{0,1},{1,2},{2,3},{3,0},{4,5},{5,6},{6,7},{7,4},{8,9},{9,10},{10,1... | collective-permute-start | bytes 1179656 | tf_op jit(solution)/shard_map/ppermute | solution.py:357
  52.3 11.7 %collective-permute-done.1.next_piece = bf16[128,1536]{1,0:T(8,128)(2,1)S(1)} collective-permute-done((bf16[128,1536]{1,0:T(8,128)(2,1)S(1)}, bf16[128,1536]{1,0:T(8,128)(2,1)S(1)}, u32[]{:S(2)}, u32[]{:S(2)}) %collective-permute-start.1) | collective-permute-done | bytes 393248 | tf_op jit(solution)/shard_map/ppermute | solution.py:357
  64.0 2.5 %collective-permute-done.3.last = bf16[128,1536]{1,0:T(8,128)(2,1)S(1)} collective-permute-done((bf16[128,1536]{1,0:T(8,128)(2,1)S(1)}, bf16[128,1536]{1,0:T(8,128)(2,1)S(1)}, u32[]{:S(2)}, u32[]{:S(2)}) %collective-permute-start.3) | collective-permute-done | bytes 393248 | tf_op jit(solution)/shard_map/ppermute | solution.py:357
  66.5 0.8 copy-done.13
  67.3 1.0 pad_maximum_fusion
  68.3 1.9 %collective-permute-start.4 = (bf16[512,1024]{1,0:T(8,128)(2,1)}, bf16[512,1024]{1,0:T(8,128)(2,1)S(1)}, u32[]{:S(2)}, u32[]{:S(2)}) collective-permute-start(bf16[512,1024]{1,0:T(8,128)(2,1)} %pad_maximum_fusion), channel_id=1, source_target_pairs={{0,4},{4,8},{8,12},{12,16},{16,20},{20,24},{24,28},{28,256},{256,2... | collective-permute-start | bytes 3145736 | tf_op jit(solution)/shard_map/ppermute | solution.py:357
  70.3 3.9 %collective-permute-start.5 = (bf16[512,1024]{1,0:T(8,128)(2,1)}, bf16[512,1024]{1,0:T(8,128)(2,1)S(1)}, u32[]{:S(2)}, u32[]{:S(2)}) collective-permute-start(bf16[512,1024]{1,0:T(8,128)(2,1)} %pad_maximum_fusion), channel_id=1, source_target_pairs={{0,284},{4,0},{8,4},{12,8},{16,12},{20,16},{24,20},{28,24},{256,28... | collective-permute-start | bytes 3145736 | tf_op jit(solution)/shard_map/ppermute | solution.py:357
  74.2 1.9 %collective-permute-start = (bf16[4,2,512,128]{3,2,1,0:T(8,128)(2,1)S(1)}, bf16[4,2,512,128]{3,2,1,0:T(8,128)(2,1)S(1)}, u32[]{:S(2)}, u32[]{:S(2)}) collective-permute-start(bf16[4,2,512,128]{3,2,1,0:T(8,128)(2,1)S(1)} %all-to-all-done.1.own_weights), channel_id=1, source_target_pairs={{0,32},{32,0},{1,33},{33,1},{2,34},{34,2},{3,35},{35,3},{4,36},{36... | collective-permute-start | bytes 3145736 | tf_op jit(solution)/shard_map/ppermute | solution.py:357
  76.1 9.8 %local.1 = (f32[16,128,128]{2,1,0:T(8,128)}, f32[16,128,128]{2,1,0:T(8,128)}, f32[16,128,128]{2,1,0:T(8,128)}, f32[16,128,128]{2,1,0:T(8,128)}) custom-call(s32[1,12]{1,0:T(1,128)} %lengths_ref.7, s32[3]{0:T(128)} %copy-done.8, bf16[128,1536]{1,0:T(8,128)(2,1)} %copy-done.7, bf16[128,1536]{1,0:T(8,128)(2,1)} %copy-done.11, bf16[128,1536]{1,0:T(8,128)(2,1)} %copy-done.12, ...), custom_call_target="tpu_custom_call" | custom-call | flops 1073741824 | bytes 8388608 | tf_op jit(solution)/shard_map/local/pallas_call | solution.py:396
  85.9 8.6 %collective-permute-done.4.before = bf16[512,1024]{1,0:T(8,128)(2,1)S(1)} collective-permute-done((bf16[512,1024]{1,0:T(8,128)(2,1)}, bf16[512,1024]{1,0:T(8,128)(2,1)S(1)}, u32[]{:S(2)}, u32[]{:S(2)}) %collective-permute-start.4) | collective-permute-done | bytes 1048608 | tf_op jit(solution)/shard_map/ppermute | solution.py:357
  94.5 2.4 %collective-permute-done.5.after = bf16[512,1024]{1,0:T(8,128)(2,1)S(1)} collective-permute-done((bf16[512,1024]{1,0:T(8,128)(2,1)}, bf16[512,1024]{1,0:T(8,128)(2,1)S(1)}, u32[]{:S(2)}, u32[]{:S(2)}) %collective-permute-start.5) | collective-permute-done | bytes 1048608 | tf_op jit(solution)/shard_map/ppermute | solution.py:357
  96.8 1.2 copy-done.2
  98.1 2.1 %attend.1.mixed = bf16[128,512]{1,0:T(8,128)(2,1)S(1)} custom-call(s32[1,12]{1,0:T(1,128)S(1)} %copy-done.10, s32[3]{0:T(128)S(1)} %copy-done.9, bf16[512,1024]{1,0:T(8,128)(2,1)S(1)} %collective-permute-done.4.before, bf16[512,1024]{1,0:T(8,128)(2,1)S(1)} %collective-permute-done.5.after, f32[16,128,128]{2,1,0:T(8,128)S(1)} %copy-done.2), custom_call_target="tpu_custom_call" | custom-call | flops 268435456 | bytes 3145728 | tf_op jit(solution)/shard_map/attend/pallas_call | solution.py:423
  100.2 5.4 %rows.3 = (bf16[128,2048]{1,0:T(8,128)(2,1)S(1)}, bf16[128,2048]{1,0:T(8,128)(2,1)S(1)}) custom-call(s32[1,12]{1,0:T(1,128)S(1)} %copy-done.10, s32[3]{0:T(128)S(1)} %copy-done.9, bf16[4,2,512,128]{3,2,1,0:T(8,128)(2,1)S(1)} %all-to-all-done.1.own_weights, bf16[4,2,512,128]{3,2,1,0:T(8,128)(2,1)S(1)} %collective-permute-done.other_weights, ...), custom_call_target="tpu_custom_call" | custom-call | flops 1073741824 | bytes 4194304 | tf_op jit(solution)/shard_map/rows/pallas_call | solution.py:409
  105.7 6.4 %collective-permute-start.7 = (bf16[128,2048]{1,0:T(8,128)(2,1)S(1)}, bf16[128,2048]{1,0:T(8,128)(2,1)S(1)}, u32[]{:S(2)}, u32[]{:S(2)}) collective-permute-start(bf16[128,2048]{1,0:T(8,128)(2,1)S(1)} %get-tuple-element.20), channel_id=1, source_target_pairs={{0,1},{1,2},{2,3},{3,0},{4,5},{5,6},{6,7},{7,4},{8,9},{9,10},{10,1... | collective-permute-start | bytes 1572872 | tf_op jit(solution)/shard_map/ppermute | solution.py:357
  112.1 1.9 %collective-permute-start.8 = (bf16[128,2048]{1,0:T(8,128)(2,1)S(1)}, bf16[128,2048]{1,0:T(8,128)(2,1)S(1)}, u32[]{:S(2)}, u32[]{:S(2)}) collective-permute-start(bf16[128,2048]{1,0:T(8,128)(2,1)S(1)} %get-tuple-element.21), channel_id=1, source_target_pairs={{0,3},{1,0},{2,1},{3,2},{4,7},{5,4},{6,5},{7,6},{8,11},{9,8},{10,9... | collective-permute-start | bytes 1572872 | tf_op jit(solution)/shard_map/ppermute | solution.py:357
  114.0 1.0 project.1
  115.1 3.4 %collective-permute-start.6 = (bf16[128,2048]{1,0:T(8,128)(2,1)S(1)}, bf16[128,2048]{1,0:T(8,128)(2,1)S(1)}, u32[]{:S(2)}, u32[]{:S(2)}) collective-permute-start(bf16[128,2048]{1,0:T(8,128)(2,1)S(1)} %project.1), channel_id=1, source_target_pairs={{0,2},{1,3},{2,0},{3,1},{4,6},{5,7},{6,4},{7,5},{8,10},{9,11},{10,... | collective-permute-start | bytes 1572872 | tf_op jit(solution)/shard_map/ppermute | solution.py:357
  118.5 3.2 %rows.2.own_ref = f32[128,2048]{1,0:T(8,128)S(1)} custom-call(s32[1,12]{1,0:T(1,128)S(1)} %copy-done.10, s32[3]{0:T(128)S(1)} %copy-done.9, bf16[4,2,512,128]{3,2,1,0:T(8,128)(2,1)S(1)} %all-to-all-done.1.own_weights, bf16[4,2,512,128]{3,2,1,0:T(8,128)(2,1)S(1)} %collective-permute-done.other_weights, bf16[512,1024]{1,0:T(8,128)(2,1)S(1)} %collective-permute-done.4.before, ...), custom_call_target="tpu_custom_call" | custom-call | flops 536870912 | bytes 4194304 | tf_op jit(solution)/shard_map/rows/pallas_call | solution.py:409
  121.7 11.4 %collective-permute-done.7.two_ref = bf16[128,2048]{1,0:T(8,128)(2,1)S(1)} collective-permute-done((bf16[128,2048]{1,0:T(8,128)(2,1)S(1)}, bf16[128,2048]{1,0:T(8,128)(2,1)S(1)}, u32[]{:S(2)}, u32[]{:S(2)}) %collective-permute-start.7) | collective-permute-done | bytes 524320 | tf_op jit(solution)/shard_map/ppermute | solution.py:357
  133.1 5.3 %collective-permute-done.8.three_ref = bf16[128,2048]{1,0:T(8,128)(2,1)S(1)} collective-permute-done((bf16[128,2048]{1,0:T(8,128)(2,1)S(1)}, bf16[128,2048]{1,0:T(8,128)(2,1)S(1)}, u32[]{:S(2)}, u32[]{:S(2)}) %collective-permute-start.8) | collective-permute-done | bytes 524320 | tf_op jit(solution)/shard_map/ppermute | solution.py:357
  138.5 1.9 %finish.1 = f32[128,2048]{1,0:T(8,128)} custom-call(f32[128,2048]{1,0:T(8,128)S(1)} %rows.2.own_ref, bf16[128,2048]{1,0:T(8,128)(2,1)S(1)} %collective-permute-done.6.one_ref, bf16[128,2048]{1,0:T(8,128)(2,1)S(1)} %collective-permute-done.7.two_ref, bf16[128,2048]{1,0:T(8,128)(2,1)S(1)} %collective-permute-done.8.three_ref, bf16[128,2048]{1,0:T(8,128)(2,1)S(1)} %bitcast.10, ...), custom_call_target="tpu_custom_call" | custom-call | flops 4194304 | bytes 5242880 | tf_op jit(solution)/shard_map/finish/pallas_call | solution.py:447
  (35 shorter events, 0.2 us)
Async XLA Ops:
  1.4 0.6 copy-start.14
  35.0 5.5 %copy-start = (bf16[1,128,6144]{2,1,0:T(8,128)(2,1)S(1)}, bf16[1,128,6144]{2,1,0:T(8,128)(2,1)}, u32[]{:S(2)}) copy-start(bf16[1,128,6144]{2,1,0:T(8,128)(2,1)} %param.6) | copy-start | bytes 4718596
  36.1 38.1 %all-to-all-start.1 = ((bf16[4,2,512,128]{3,2,1,0:T(8,128)(2,1)}), bf16[4,2,512,128]{3,2,1,0:T(8,128)(2,1)S(1)}, u32[]{:S(2)}, u32[]{:S(2)}) async-start(bf16[4,2,512,128]{3,2,1,0:T(8,128)(2,1)} %broadcast_in_dim.18), calls=%async_computation.1 | async-start | bytes 2097152 | tf_op jit(solution)/shard_map/all_to_all | solution.py:391
  40.4 23.6 %copy-start.8 = (s32[3]{0:T(128)}, s32[3]{0:T(128)S(1)}, u32[]{:S(2)}) copy-start(s32[3]{0:T(128)S(1)} %pad_add_fusion.place_ref) | copy-start | bytes 40
  42.6 25.7 %copy-start.7 = (bf16[128,1536]{1,0:T(8,128)(2,1)}, bf16[128,1536]{1,0:T(8,128)(2,1)S(1)}, u32[]{:S(2)}) copy-start(bf16[128,1536]{1,0:T(8,128)(2,1)S(1)} %get-tuple-element.12.own) | copy-start | bytes 1179652
  42.7 21.3 %collective-permute-start.1 = (bf16[128,1536]{1,0:T(8,128)(2,1)S(1)}, bf16[128,1536]{1,0:T(8,128)(2,1)S(1)}, u32[]{:S(2)}, u32[]{:S(2)}) collective-permute-start(bf16[128,1536]{1,0:T(8,128)(2,1)S(1)} %get-tuple-element.13), channel_id=1, source_target_pairs={{0,3},{1,0},{2,1},{3,2},{4,7},{5,4},{6,5},{7,6},{8,11},{9,8},{10,9... | collective-permute-start | bytes 1179656 | tf_op jit(solution)/shard_map/ppermute | solution.py:357
  45.3 18.7 %collective-permute-start.2 = (bf16[128,1536]{1,0:T(8,128)(2,1)S(1)}, bf16[128,1536]{1,0:T(8,128)(2,1)S(1)}, u32[]{:S(2)}, u32[]{:S(2)}) collective-permute-start(bf16[128,1536]{1,0:T(8,128)(2,1)S(1)} %get-tuple-element.14), channel_id=1, source_target_pairs={{0,2},{1,3},{2,0},{3,1},{4,6},{5,7},{6,4},{7,5},{8,10},{9,11},{10,... | collective-permute-start | bytes 1179656 | tf_op jit(solution)/shard_map/ppermute | solution.py:357
  48.2 18.3 %collective-permute-start.3 = (bf16[128,1536]{1,0:T(8,128)(2,1)S(1)}, bf16[128,1536]{1,0:T(8,128)(2,1)S(1)}, u32[]{:S(2)}, u32[]{:S(2)}) collective-permute-start(bf16[128,1536]{1,0:T(8,128)(2,1)S(1)} %get-tuple-element.15), channel_id=1, source_target_pairs={{0,1},{1,2},{2,3},{3,0},{4,5},{5,6},{6,7},{7,4},{8,9},{9,10},{10,1... | collective-permute-start | bytes 1179656 | tf_op jit(solution)/shard_map/ppermute | solution.py:357
  64.0 4.4 %copy-start.11 = (bf16[128,1536]{1,0:T(8,128)(2,1)}, bf16[128,1536]{1,0:T(8,128)(2,1)S(1)}, u32[]{:S(2)}) copy-start(bf16[128,1536]{1,0:T(8,128)(2,1)S(1)} %collective-permute-done.1.next_piece) | copy-start | bytes 1179652
  64.0 2.5 %copy-start.12 = (bf16[128,1536]{1,0:T(8,128)(2,1)}, bf16[128,1536]{1,0:T(8,128)(2,1)S(1)}, u32[]{:S(2)}) copy-start(bf16[128,1536]{1,0:T(8,128)(2,1)S(1)} %collective-permute-done.2.far) | copy-start | bytes 1179652
  66.5 0.8 copy-start.13
  68.3 28.5 %copy-start.9 = (s32[3]{0:T(128)S(1)}, s32[3]{0:T(128)}, u32[]{:S(2)}) copy-start(s32[3]{0:T(128)} %copy-done.8) | copy-start | bytes 40
  68.3 28.5 %copy-start.10 = (s32[1,12]{1,0:T(1,128)S(1)}, s32[1,12]{1,0:T(1,128)}, u32[]{:S(2)}) copy-start(s32[1,12]{1,0:T(1,128)} %lengths_ref.7) | copy-start | bytes 148
  68.3 26.1 %collective-permute-start.4 = (bf16[512,1024]{1,0:T(8,128)(2,1)}, bf16[512,1024]{1,0:T(8,128)(2,1)S(1)}, u32[]{:S(2)}, u32[]{:S(2)}) collective-permute-start(bf16[512,1024]{1,0:T(8,128)(2,1)} %pad_maximum_fusion), channel_id=1, source_target_pairs={{0,4},{4,8},{8,12},{12,16},{16,20},{20,24},{24,28},{28,256},{256,2... | collective-permute-start | bytes 3145736 | tf_op jit(solution)/shard_map/ppermute | solution.py:357
  70.3 26.6 %collective-permute-start.5 = (bf16[512,1024]{1,0:T(8,128)(2,1)}, bf16[512,1024]{1,0:T(8,128)(2,1)S(1)}, u32[]{:S(2)}, u32[]{:S(2)}) collective-permute-start(bf16[512,1024]{1,0:T(8,128)(2,1)} %pad_maximum_fusion), channel_id=1, source_target_pairs={{0,284},{4,0},{8,4},{12,8},{16,12},{20,16},{24,20},{28,24},{256,28... | collective-permute-start | bytes 3145736 | tf_op jit(solution)/shard_map/ppermute | solution.py:357
  74.2 26.0 %collective-permute-start = (bf16[4,2,512,128]{3,2,1,0:T(8,128)(2,1)S(1)}, bf16[4,2,512,128]{3,2,1,0:T(8,128)(2,1)S(1)}, u32[]{:S(2)}, u32[]{:S(2)}) collective-permute-start(bf16[4,2,512,128]{3,2,1,0:T(8,128)(2,1)S(1)} %all-to-all-done.1.own_weights), channel_id=1, source_target_pairs={{0,32},{32,0},{1,33},{33,1},{2,34},{34,2},{3,35},{35,3},{4,36},{36... | collective-permute-start | bytes 3145736 | tf_op jit(solution)/shard_map/ppermute | solution.py:357
  96.8 1.2 copy-start.2
  98.1 2.1 %copy-start.4 = (f32[16,128,128]{2,1,0:T(8,128)S(1)}, f32[16,128,128]{2,1,0:T(8,128)}, u32[]{:S(2)}) copy-start(f32[16,128,128]{2,1,0:T(8,128)} %get-tuple-element.18.rest_0_) | copy-start | bytes 3145732
  98.1 2.1 %copy-start.5 = (f32[16,128,128]{2,1,0:T(8,128)S(1)}, f32[16,128,128]{2,1,0:T(8,128)}, u32[]{:S(2)}) copy-start(f32[16,128,128]{2,1,0:T(8,128)} %get-tuple-element.19.rest_1_) | copy-start | bytes 3145732
  105.7 12.8 %copy-start.3 = (f32[16,128,128]{2,1,0:T(8,128)S(1)}, f32[16,128,128]{2,1,0:T(8,128)}, u32[]{:S(2)}) copy-start(f32[16,128,128]{2,1,0:T(8,128)} %get-tuple-element.16.rest_0_) | copy-start | bytes 3145732
  105.7 27.5 %collective-permute-start.7 = (bf16[128,2048]{1,0:T(8,128)(2,1)S(1)}, bf16[128,2048]{1,0:T(8,128)(2,1)S(1)}, u32[]{:S(2)}, u32[]{:S(2)}) collective-permute-start(bf16[128,2048]{1,0:T(8,128)(2,1)S(1)} %get-tuple-element.20), channel_id=1, source_target_pairs={{0,1},{1,2},{2,3},{3,0},{4,5},{5,6},{6,7},{7,4},{8,9},{9,10},{10,1... | collective-permute-start | bytes 1572872 | tf_op jit(solution)/shard_map/ppermute | solution.py:357
  112.1 26.3 %collective-permute-start.8 = (bf16[128,2048]{1,0:T(8,128)(2,1)S(1)}, bf16[128,2048]{1,0:T(8,128)(2,1)S(1)}, u32[]{:S(2)}, u32[]{:S(2)}) collective-permute-start(bf16[128,2048]{1,0:T(8,128)(2,1)S(1)} %get-tuple-element.21), channel_id=1, source_target_pairs={{0,3},{1,0},{2,1},{3,2},{4,7},{5,4},{6,5},{7,6},{8,11},{9,8},{10,9... | collective-permute-start | bytes 1572872 | tf_op jit(solution)/shard_map/ppermute | solution.py:357
  115.1 23.4 %collective-permute-start.6 = (bf16[128,2048]{1,0:T(8,128)(2,1)S(1)}, bf16[128,2048]{1,0:T(8,128)(2,1)S(1)}, u32[]{:S(2)}, u32[]{:S(2)}) collective-permute-start(bf16[128,2048]{1,0:T(8,128)(2,1)S(1)} %project.1), channel_id=1, source_target_pairs={{0,2},{1,3},{2,0},{3,1},{4,6},{5,7},{6,4},{7,5},{8,10},{9,11},{10,... | collective-permute-start | bytes 1572872 | tf_op jit(solution)/shard_map/ppermute | solution.py:357
  118.5 20.0 %copy-start.1 = (f32[1,128,2048]{2,1,0:T(8,128)S(1)}, f32[1,128,2048]{2,1,0:T(8,128)}, u32[]{:S(2)}) copy-start(f32[1,128,2048]{2,1,0:T(8,128)} %param.8) | copy-start | bytes 3145732
  118.5 20.0 %copy-start.6 = (bf16[1,128,2048]{2,1,0:T(8,128)(2,1)S(1)}, bf16[1,128,2048]{2,1,0:T(8,128)(2,1)}, u32[]{:S(2)}) copy-start(bf16[1,128,2048]{2,1,0:T(8,128)(2,1)} %param.7) | copy-start | bytes 1572868
